TPU v7x, 32 devices: a whole 2x2x4 slice. The times are simulated.
32 devices in a mesh: grp: 16 (over z, x, core), dev: 2 (over y).
Axes of the slice: x: 2, y: 2, z: 4, core: 2. Of those that a mesh axis runs over, the one named last changes fastest.
Arguments:
- tokens: bfloat16 [2048, 768], P(('grp', 'dev')), may hold values from -6 to 6
- expert_ids: int32 [2048, 8], P(('grp', 'dev')), may hold values from 0 to 31, as said below
- gates: bfloat16 [2048, 8], P(('grp', 'dev')), may hold values from 0.099609375 to 0.5
- w_in: bfloat16 [32, 768, 1536], P(('grp', 'dev')), may hold values from -0.21875 to 0.21875
- w_out: bfloat16 [32, 1536, 768], P(('grp', 'dev')), may hold values from -0.15625 to 0.15625
Outputs:
- mixed: bfloat16 [2048, 768], P(('grp', 'dev'))
Inputs may be any that keep to these rules, and one draw needn't show every extreme that they name: `expert_ids`: row t lists 8 experts; columns 2 * k and 2 * k + 1 are two different experts of one group (experts g * 2 to g * 2 + 1 form group g), and the four groups of a row differ. The owner of token t is t // 64, and its dev index is the owner modulo 2. The tokens of one owner pick one group at most 48 times, and every owner reaches it for some group. The tokens whose owners share a dev index pick each group exactly 4 * 64 times in all and each expert at most 256 times; in every group one expert is picked 256 times by the tokens of every dev index.
All inputs are finite; a program needn't handle non-finite values.
Results may differ from a plain program's by a relative error of at most 0.0057.
Values may be sent and summed in bfloat16 or wider, within the bound.
No kernel may reach another device: no remote copies, remote signals or barrier semaphores. Data moves between devices by JAX's collectives and lax.ppermute only.
A program may use at most 64 MiB of HBM per device.

v0:
```python
import jax
import jax.numpy as jnp
from jax import lax
from jax.sharding import PartitionSpec as P


def earlier_count(onehot):
    return jnp.cumsum(onehot, axis=0) - onehot


def contract_rows(left, right):
    return lax.dot_general(
        left,
        right,
        (((0,), (0,)), ((), ())),
        precision=lax.Precision.HIGHEST,
        preferred_element_type=jnp.float32,
    )


def expert_rows(slot_block, w_first, w_second):

    def one_block(rows_block):
        hidden = jnp.maximum(
            jnp.dot(rows_block, w_first, preferred_element_type=jnp.float32), 0.0
        ).astype(jnp.bfloat16)
        return jnp.dot(hidden, w_second, preferred_element_type=jnp.float32).astype(jnp.bfloat16)

    return lax.map(one_block, slot_block)


def seat_sources(seat_of, valid, seat_total):
    item_count = seat_of.shape[0]
    target_seat = jnp.where(valid, seat_of, seat_total)
    empty_seats = jnp.full((seat_total,), item_count, jnp.int32)
    return empty_seats.at[target_seat].set(jnp.arange(item_count, dtype=jnp.int32), mode="drop")


def per_device(tokens, expert_ids, gates, w_in, w_out):
    n_grp = lax.axis_size("grp")
    n_dev = lax.axis_size("dev")
    token_count, feature_width = tokens.shape
    cap_grp = min(token_count, 3 * ((4 * token_count + n_grp - 1) // n_grp))
    cap_exp = min(4 * token_count, 24 * token_count // n_dev)
    seat_total = n_dev * cap_exp
    zero_half = jnp.zeros((), jnp.bfloat16)
    w_first = w_in[0]
    w_second = w_out[0]
    pair_ids = expert_ids.reshape(token_count * 4, 2)
    pair_group = pair_ids[:, 0] // n_dev
    group_hot = (pair_group[:, None] == jnp.arange(n_grp)[None, :]).astype(jnp.int32)
    group_rank = jnp.sum(earlier_count(group_hot) * group_hot, axis=1)
    target = pair_group * cap_grp + group_rank
    slot_count = n_grp * cap_grp
    placed = (target[None, :] == jnp.arange(slot_count)[:, None]).astype(jnp.int32)
    token_hot = placed.reshape(slot_count, token_count, 4).sum(axis=2)
    rows_out = jnp.dot(
        token_hot.astype(jnp.bfloat16), tokens, preferred_element_type=jnp.float32
    ).astype(jnp.bfloat16)
    local_ids = pair_ids % n_dev
    picks_out = jnp.dot(placed, local_ids + 1) - 1
    gains_out = jnp.dot(
        placed.astype(jnp.bfloat16),
        gates.reshape(token_count * 4, 2),
        preferred_element_type=jnp.float32,
    ).astype(jnp.bfloat16)
    rows_in, picks_in, gains_in = (
        lax.all_to_all(
            rows_out.reshape(n_grp, cap_grp, feature_width),
            "grp",
            split_axis=0,
            concat_axis=0,
            tiled=True,
        ),
        lax.all_to_all(
            picks_out.reshape(n_grp, cap_grp, 2), "grp", split_axis=0, concat_axis=0, tiled=True
        ),
        lax.all_to_all(
            gains_out.reshape(n_grp, cap_grp, 2), "grp", split_axis=0, concat_axis=0, tiled=True
        ),
    )
    relay_rows = rows_in.reshape(slot_count, feature_width)
    relay_picks = picks_in.reshape(slot_count, 2)
    relay_gains = gains_in.reshape(slot_count, 2)
    live_count = 4 * token_count
    slot_live = (relay_picks[:, 0] >= 0).astype(jnp.int32)
    slot_order = jnp.cumsum(slot_live) - 1
    packed = (
        (slot_order[None, :] == jnp.arange(live_count)[:, None]) & (slot_live[None, :] > 0)
    ).astype(jnp.int32)
    packed_rows = jnp.dot(
        packed.astype(jnp.bfloat16), relay_rows, preferred_element_type=jnp.float32
    ).astype(jnp.bfloat16)
    packed_picks = jnp.dot(packed, relay_picks)
    packed_gains = jnp.dot(
        packed.astype(jnp.bfloat16), relay_gains, preferred_element_type=jnp.float32
    ).astype(jnp.bfloat16)
    group_rows, group_picks, group_gains = (
        lax.all_gather(packed_rows, "dev", axis=0, tiled=True),
        lax.all_gather(packed_picks, "dev", axis=0, tiled=True),
        lax.all_gather(packed_gains, "dev", axis=0, tiled=True),
    )
    gathered_count = group_rows.shape[0]
    chosen = jnp.sum((group_picks == lax.axis_index("dev")).astype(jnp.int32), axis=1)
    expert_seat = jnp.cumsum(chosen) - 1
    seat_source = seat_sources(expert_seat, chosen > 0, seat_total)
    seat_live = seat_source < gathered_count
    taken_rows = jnp.take(group_rows, jnp.minimum(seat_source, gathered_count - 1), axis=0)
    expert_in = jnp.where(seat_live[:, None], taken_rows, zero_half)
    expert_out = expert_rows(
        expert_in.reshape(n_dev, cap_exp, feature_width), w_first, w_second
    ).reshape(seat_total, feature_width)
    spread_rows = jnp.take(expert_out, jnp.clip(expert_seat, 0, seat_total - 1), axis=0)
    spread = jnp.where((chosen > 0)[:, None], spread_rows, zero_half)
    back = lax.all_to_all(
        spread.reshape(n_dev, live_count, feature_width),
        "dev",
        split_axis=0,
        concat_axis=0,
        tiled=True,
    )
    match = (packed_picks[None, :, :] == jnp.arange(n_dev)[:, None, None]).astype(jnp.float32)
    row_weights = jnp.sum(match * packed_gains.astype(jnp.float32)[None, :, :], axis=2)
    packed_sum = jnp.sum(row_weights[:, :, None] * back.astype(jnp.float32), axis=0)
    partial_value = contract_rows(packed.astype(jnp.float32), packed_sum)
    returned_sums = lax.all_to_all(
        partial_value.reshape(n_grp, cap_grp, feature_width),
        "grp",
        split_axis=0,
        concat_axis=0,
        tiled=True,
    )
    mixed = contract_rows(
        token_hot.astype(jnp.float32), returned_sums.reshape(slot_count, feature_width)
    )
    return mixed.astype(jnp.bfloat16)


def solution(mesh):
    return jax.shard_map(
        per_device,
        mesh=mesh,
        in_specs=(
            P(("grp", "dev"), None),
            P(("grp", "dev"), None),
            P(("grp", "dev"), None),
            P(("grp", "dev"), None, None),
            P(("grp", "dev"), None, None),
        ),
        out_specs=P(("grp", "dev"), None),
        check_vma=False,
    )
```

profile of v0, /device:TPU:0, one launch (start us, length us, event | category | flops | bytes accessed | tf_op | source)
XLA Modules:
  0.0 164.1 jit_solution(5433259859377536581)
XLA Ops:
  0.0 0.8 copy.37
  0.8 0.8 copy.32
  3.8 7.4 %all-to-all-start.1 = ((bf16[16,48,2]{1,2,0:T(2,128)(2,1)}), bf16[16,48,2]{1,2,0:T(2,128)(2,1)S(1)}, u32[]{:S(2)}, u32[]{:S(2)}) async-start(bf16[16,48,2]{1,2,0:T(2,128)(2,1)} %copy.38), calls=%async_computation.1 | async-start | bytes 16384 | tf_op jit(solution)/shard_map/all_to_all | solution.py:78
  13.0 4.6 %all-to-all-done.1 = bf16[16,48,2]{1,2,0:T(2,128)(2,1)S(1)} async-done(((bf16[16,48,2]{1,2,0:T(2,128)(2,1)}), bf16[16,48,2]{1,2,0:T(2,128)(2,1)S(1)}, u32[]{:S(2)}, u32[]{:S(2)}) %all-to-all-start.1) | async-done | bytes 3104 | tf_op jit(solution)/shard_map/all_to_all | solution.py:78
  17.7 3.5 %all-to-all-start = ((s32[16,48,2]{1,2,0:T(2,128)}), s32[16,48,2]{1,2,0:T(2,128)S(1)}, u32[]{:S(2)}, u32[]{:S(2)}) async-start(s32[16,48,2]{1,2,0:T(2,128)} %copy.35), calls=%async_computation | async-start | bytes 32768 | tf_op jit(solution)/shard_map/all_to_all | solution.py:75
  21.2 1.5 convolution_convert_fusion.1
  22.8 4.8 %all-to-all-done = s32[16,48,2]{1,2,0:T(2,128)S(1)} async-done(((s32[16,48,2]{1,2,0:T(2,128)}), s32[16,48,2]{1,2,0:T(2,128)S(1)}, u32[]{:S(2)}, u32[]{:S(2)}) %all-to-all-start) | async-done | bytes 6176 | tf_op jit(solution)/shard_map/all_to_all | solution.py:75
  27.6 4.4 %all-to-all-start.2 = ((bf16[16,48,768]{2,1,0:T(8,128)(2,1)}), bf16[16,48,768]{2,1,0:T(8,128)(2,1)}, u32[]{:S(2)}, u32[]{:S(2)}) async-start(bf16[16,48,768]{2,1,0:T(8,128)(2,1)} %bitcast.8), calls=%async_computation.2 | async-start | bytes 2359296 | tf_op jit(solution)/shard_map/all_to_all | solution.py:68
  33.3 4.4 %all_gather.6 = s32[512,2]{0,1:T(2,128)S(1)} all-gather(s32[256,2]{0,1:T(2,128)S(1)} %fusion.19), channel_id=1, replica_groups=mesh['grp'=16,'dev'=2] {'dev'}, dimensions={0}, use_global_device_ids=true | all-gather | bytes 6144 | tf_op jit(solution)/shard_map/all_gather | solution.py:100
  38.3 2.4 %scatter_custom_fusion = s32[512]{0:T(512)S(1)} fusion(s32[512]{0:T(512)S(1)} %bitcast.81, s32[512]{0:T(512)S(1)} %iota.29, s32[]{:T(128)} %constant.84.clone.1), kind=kCustom, calls=%fused_computation.110 | custom fusion | bytes 2052 | tf_op jit(solution)/shard_map/scatter | solution.py:36
  40.8 16.2 %all-to-all-done.2 = bf16[16,48,768]{2,1,0:T(8,128)(2,1)} async-done(((bf16[16,48,768]{2,1,0:T(8,128)(2,1)}), bf16[16,48,768]{2,1,0:T(8,128)(2,1)}, u32[]{:S(2)}, u32[]{:S(2)}) %all-to-all-start.2) | async-done | bytes 1179680 | tf_op jit(solution)/shard_map/all_to_all | solution.py:68
  57.1 1.8 %convolution_convert_fusion.2 = bf16[256,768]{1,0:T(8,128)(2,1)S(1)} fusion(bf16[768,768]{1,0:T(8,128)(2,1)} %bitcast.9, s32[768]{0:T(1024)S(1)} %fusion.69, pred[768]{0:T(1024)(128)(4,1)S(1)} %compare_reduce_fusion), kind=kOutput, calls=%fused_computation.15 | convolution fusion | flops 302972928 | bytes 1576704 | tf_op jit(solution)/shard_map/dot_general | solution.py:91
  58.8 12.6 %all_gather.7 = bf16[512,768]{1,0:T(8,128)(2,1)S(1)} all-gather(bf16[256,768]{1,0:T(8,128)(2,1)S(1)} %convolution_convert_fusion.2), channel_id=1, replica_groups=mesh['grp'=16,'dev'=2] {'dev'}, dimensions={0}, use_global_device_ids=true | all-gather | bytes 1179648 | tf_op jit(solution)/shard_map/all_gather | solution.py:99
  71.4 2.0 %gather_fusion = bf16[512,768]{1,0:T(8,128)(2,1)S(1)} fusion(bf16[512,768]{1,0:T(8,128)(2,1)S(1)} %all_gather.7, s32[1024]{0:T(1024)S(1)} %pad_clamp_fusion.1), kind=kCustom, calls=%fused_computation.clone | custom fusion | bytes 1574912 | tf_op jit(solution)/shard_map/jit(_take)/gather | solution.py:108
  73.7 7.8 %while.10 = (s32[]{:T(128)}, bf16[2,256,768]{2,1,0:T(8,128)(2,1)S(1)}, bf16[2,256,768]{2,1,0:T(8,128)(2,1)S(1)}, bf16[768,1536]{1,0:T(8,128)(2,1)}, bf16[1536,768]{1,0:T(8,128)(2,1)}, /*index=5*/s32[]{:T(128)}) while((s32[]{:T(128)}, bf16[2,256,768]{2,1,0:T(8,128)(2,1)S(1)}, bf16[2,256,768]{2,1,0:T(8,128)(2,1)S(1)}, ...), condition=%wide.region_12.14_spmd, body=%wide.region_11.13_spmd.sunk | while | flops 1208942592 | bytes 5506125 | solution.py:29
  73.7 3.9 %fusion.77 = bf16[2,256,768]{2,1,0:T(8,128)(2,1)S(1)} fusion(bf16[2,256,768]{2,1,0:T(8,128)(2,1)S(1)} %get-tuple-element.89, s32[]{:T(128)S(6)} %copy.45, bf16[1536,768]{1,0:T(8,128)(2,1)} %get-tuple-element.98, bf16[768,1536]{1,0:T(8,128)(2,1)} %get-tuple-element.97, bf16[2,256,768]{2,1,0:T(8,128)(2,1)S(1)} %get-tuple-element.96), kind=kOutput, calls=%fused_computation.7.clone.1 | convolution fusion | flops 1208942592 | bytes 5506048 | tf_op jit(solution)/shard_map/while/body/eval_jaxpr/dot_general | solution.py:27
  77.6 3.9 %fusion.77 = bf16[2,256,768]{2,1,0:T(8,128)(2,1)S(1)} fusion(bf16[2,256,768]{2,1,0:T(8,128)(2,1)S(1)} %get-tuple-element.89, s32[]{:T(128)S(6)} %copy.45, bf16[1536,768]{1,0:T(8,128)(2,1)} %get-tuple-element.98, bf16[768,1536]{1,0:T(8,128)(2,1)} %get-tuple-element.97, bf16[2,256,768]{2,1,0:T(8,128)(2,1)S(1)} %get-tuple-element.96), kind=kOutput, calls=%fused_computation.7.clone.1 | convolution fusion | flops 1208942592 | bytes 5506048 | tf_op jit(solution)/shard_map/while/body/eval_jaxpr/dot_general | solution.py:27
  81.5 2.0 %gather_fusion.1 = bf16[512,768]{1,0:T(8,128)(2,1)S(1)} fusion(bf16[512,768]{1,0:T(8,128)(2,1)S(1)} %bitcast.74, s32[1024]{0:T(1024)S(1)} %pad_clamp_fusion), kind=kCustom, calls=%fused_computation.1.clone | custom fusion | bytes 1574912 | tf_op jit(solution)/shard_map/jit(_take)/gather | solution.py:113
  83.5 1.1 select_select_fusion
  84.6 3.5 %all-to-all-start.3 = ((bf16[2,256,768]{2,1,0:T(8,128)(2,1)}), bf16[2,256,768]{2,1,0:T(8,128)(2,1)S(1)}, u32[]{:S(2)}, u32[]{:S(2)}) async-start(bf16[2,256,768]{2,1,0:T(8,128)(2,1)} %bitcast.14), calls=%async_computation.3 | async-start | bytes 1572864 | tf_op jit(solution)/shard_map/all_to_all | solution.py:115
  88.7 10.7 %all-to-all-done.3 = bf16[2,256,768]{2,1,0:T(8,128)(2,1)S(1)} async-done(((bf16[2,256,768]{2,1,0:T(8,128)(2,1)}), bf16[2,256,768]{2,1,0:T(8,128)(2,1)S(1)}, u32[]{:S(2)}, u32[]{:S(2)}) %all-to-all-start.3) | async-done | bytes 786464 | tf_op jit(solution)/shard_map/all_to_all | solution.py:115
  99.6 2.2 %fusion.12 = f32[16,48,768]{2,1,0:T(8,128)S(1)} fusion(f32[256,768]{1,0:T(8,128)S(1)} %multiply_reduce_fusion, s32[16,48]{1,0:T(8,128)S(1)} %sub.37, pred[16,48]{1,0:T(8,128)(4,1)S(1)} %gt.34), kind=kOutput, calls=%fused_computation.21 | convolution fusion | flops 1812725760 | bytes 3149568 | tf_op jit(solution)/shard_map/dot_general | solution.py:12
  101.8 60.0 %all_to_all.25 = f32[16,48,768]{2,1,0:T(8,128)S(1)} all-to-all(f32[16,48,768]{2,1,0:T(8,128)S(1)} %fusion.12), channel_id=1, replica_groups=mesh['grp'=16,'dev'=2] {'grp'}, dimensions={0} | all-to-all | bytes 4718592 | tf_op jit(solution)/shard_map/all_to_all | solution.py:126
  161.9 2.2 %convolution_convert_fusion.3 = bf16[64,768]{1,0:T(8,128)(2,1)} fusion(f32[768,768]{1,0:T(8,128)S(1)} %bitcast.75, s32[768,64]{0,1:T(8,128)S(1)} %convert_reduce_fusion), kind=kOutput, calls=%fused_computation.16 | convolution fusion | flops 453083136 | bytes 2654208 | tf_op jit(solution)/shard_map/dot_general | solution.py:12
  (56 shorter events, 6.9 us)
Async XLA Ops:
  0.0 21.2 %copy-start = (bf16[64,768]{1,0:T(8,128)(2,1)S(1)}, bf16[64,768]{1,0:T(8,128)(2,1)}, u32[]{:S(2)}) copy-start(bf16[64,768]{1,0:T(8,128)(2,1)} %param.9) | copy-start | bytes 294916
  3.8 13.8 %all-to-all-start.1 = ((bf16[16,48,2]{1,2,0:T(2,128)(2,1)}), bf16[16,48,2]{1,2,0:T(2,128)(2,1)S(1)}, u32[]{:S(2)}, u32[]{:S(2)}) async-start(bf16[16,48,2]{1,2,0:T(2,128)(2,1)} %copy.38), calls=%async_computation.1 | async-start | bytes 16384 | tf_op jit(solution)/shard_map/all_to_all | solution.py:78
  17.7 10.0 %all-to-all-start = ((s32[16,48,2]{1,2,0:T(2,128)}), s32[16,48,2]{1,2,0:T(2,128)S(1)}, u32[]{:S(2)}, u32[]{:S(2)}) async-start(s32[16,48,2]{1,2,0:T(2,128)} %copy.35), calls=%async_computation | async-start | bytes 32768 | tf_op jit(solution)/shard_map/all_to_all | solution.py:75
  27.6 29.4 %all-to-all-start.2 = ((bf16[16,48,768]{2,1,0:T(8,128)(2,1)}), bf16[16,48,768]{2,1,0:T(8,128)(2,1)}, u32[]{:S(2)}, u32[]{:S(2)}) async-start(bf16[16,48,768]{2,1,0:T(8,128)(2,1)} %bitcast.8), calls=%async_computation.2 | async-start | bytes 2359296 | tf_op jit(solution)/shard_map/all_to_all | solution.py:68
  84.6 14.8 %all-to-all-start.3 = ((bf16[2,256,768]{2,1,0:T(8,128)(2,1)}), bf16[2,256,768]{2,1,0:T(8,128)(2,1)S(1)}, u32[]{:S(2)}, u32[]{:S(2)}) async-start(bf16[2,256,768]{2,1,0:T(8,128)(2,1)} %bitcast.14), calls=%async_computation.3 | async-start | bytes 1572864 | tf_op jit(solution)/shard_map/all_to_all | solution.py:115
where the time goes:
time: 165 us; the launch traced here: 164 us
  blocking collectives  77 us (47%)
  waiting for transfers between devices  36.4 us (22%)
  starting transfers between devices  18.8 us (11%)
  matrix products  17.1 us (10%)
  local copies, waits for them, and re-layouts  10.8 us (7%)
  other arithmetic  3.6 us (2%)
    all_to_all x1, blocking collectives, per_device(): lax.all_to_all(partial_value.reshape(n_grp, cap_grp, feature_width), 'grp...  60 us
    all_to_all x1, waiting for transfers between devices, per_device(): lax.all_to_all(rows_out.reshape(n_grp, cap_grp, feature_width), 'grp', sp...  16.2 us
    all_gather x1, blocking collectives, per_device(): lax.all_gather(packed_rows, 'dev', axis=0, tiled=True)  12.6 us
    all_to_all x1, waiting for transfers between devices, per_device(): lax.all_to_all(spread.reshape(n_dev, live_count, feature_width), 'dev', s...  10.7 us
    dot_general x2, matrix products, one_block(): jnp.dot(hidden, w_second, preferred_element_type=jnp.float32)  7.78 us
    all_to_all x1, starting transfers between devices, per_device(): lax.all_to_all(gains_out.reshape(n_grp, cap_grp, 2), 'grp', split_axis=0,...  7.39 us
    all_to_all x1, waiting for transfers between devices, per_device(): lax.all_to_all(picks_out.reshape(n_grp, cap_grp, 2), 'grp', split_axis=0,...  4.81 us
    all_to_all x1, waiting for transfers between devices, per_device(): lax.all_to_all(gains_out.reshape(n_grp, cap_grp, 2), 'grp', split_axis=0,...  4.64 us
  transfers between devices with their start and end apart: 4, of which 4 were waited for; matrix products, arithmetic and copies ran while one was open for 5% of the time, Pallas kernels for 0%

commit v1 on v0

--- a/solution.py
+++ b/solution.py
@@ -1,7 +1,320 @@
+import functools
+
 import jax
 import jax.numpy as jnp
 from jax import lax
+from jax.experimental import pallas as pl
+from jax.experimental.pallas import tpu as pltpu
 from jax.sharding import PartitionSpec as P
+
+LANES = 128
+SUB = 8
+
+
+class Rings:
+    def __init__(self, length, rounds, clockwise, counter, mirror, partner):
+        self.length = length
+        self.rounds = rounds
+        self.perms = (clockwise, counter, mirror)
+        self.partner = partner
+
+
+def wrap(step, length):
+    step %= length
+    return step - length if step > length // 2 else step
+
+
+def seen_from_source(channel, block, length):
+    step, plane = block
+    if channel == 0:
+        return (wrap(step + 1, length), plane)
+    if channel == 1:
+        return (wrap(step - 1, length), plane)
+    return (step, 1 - plane)
+
+
+def gather_rounds(length):
+    everything = [(wrap(s, length), p) for p in range(2) for s in range(length)]
+    everything.sort(key=lambda b: (b[1], abs(b[0]), -b[0]))
+    held = {(0, 0)}
+    rounds = []
+    while len(held) < len(everything):
+        chosen = {}
+        for channel in range(3):
+            for block in everything:
+                if block in held or block in chosen.values():
+                    continue
+                if channel == 2 and block[1] == 0:
+                    continue
+                if seen_from_source(channel, block, length) in held:
+                    chosen[channel] = block
+                    break
+        rounds.append(chosen)
+        held |= set(chosen.values())
+    return rounds
+
+
+def find_rings(mesh):
+    grid = mesh.devices
+    n_grp, n_dev = grid.shape
+    if n_dev != 2 or not hasattr(grid[0, 0], "coords"):
+        return None
+    place = {}
+    for g in range(n_grp):
+        for d in range(n_dev):
+            device = grid[g, d]
+            place[(tuple(device.coords), device.core_on_chip)] = (g, d)
+    planes = []
+    for d in range(n_dev):
+        planes.append(sorted({tuple(grid[g, d].coords) for g in range(n_grp)}))
+    if 2 * len(planes[0]) != n_grp or set(planes[0]) & set(planes[1]):
+        return None
+    wide = [a for a in range(3) if len({c[a] for c in planes[0]}) == 2]
+    flat = [a for a in range(3) if len({c[a] for c in planes[0]}) == 1]
+    if not wide or len(flat) != 1:
+        return None
+    side = wide[0]
+    along = [a for a in range(3) if a not in (side, flat[0])][0]
+    low = min(c[side] for c in planes[0])
+    up = sorted((c for c in planes[0] if c[side] == low), key=lambda c: c[along])
+    down = sorted((c for c in planes[0] if c[side] != low), key=lambda c: -c[along])
+    order = up + down
+    length = len(order)
+
+    def index(chip, core):
+        g, d = place[(chip, core)]
+        return g * n_dev + d
+
+    def mirrored(chip):
+        other = planes[1][0][flat[0]]
+        return tuple(other if a == flat[0] else v for a, v in enumerate(chip))
+
+    if any((mirrored(c), k) not in place or (c, k) not in place for c in order for k in range(2)):
+        return None
+    if any(place[(c, k)][0] != place[(mirrored(c), k)][0] for c in order for k in range(2)):
+        return None
+    clockwise, counter, mirror, partner = [], [], [], []
+    for here in range(length):
+        after = (here + 1) % length
+        for core in range(2):
+            for turn in (lambda c: c, mirrored):
+                a, b = index(turn(order[here]), core), index(turn(order[after]), core)
+                clockwise.append((a, b))
+                counter.append((b, a))
+                partner.append((a, index(turn(order[here]), 1 - core)))
+            a, b = index(order[here], core), index(mirrored(order[here]), core)
+            mirror += [(a, b), (b, a)]
+    return Rings(length, gather_rounds(length), clockwise, counter, mirror, partner)
+
+
+def pack_kernel(ids_ref, gates_ref, tokens_ref, out_ref, *, experts):
+    count, width = tokens_ref.shape
+    picks = ids_ref.shape[1]
+    out_ref[:count, :] = tokens_ref[...]
+    ids = ids_ref[...]
+    gates = gates_ref[...].astype(jnp.float32)
+    column = lax.broadcasted_iota(jnp.int32, (count, experts), 1)
+    table = jnp.zeros((count, experts), jnp.float32)
+    for k in range(picks):
+        table += jnp.where(ids[:, k : k + 1] == column, gates[:, k : k + 1], 0.0)
+    lane = lax.broadcasted_iota(jnp.int32, (count, LANES), 1)
+    row = lax.broadcasted_iota(jnp.int32, (count, LANES), 0)
+    twice = ((lane & (count - 1)) == row).astype(jnp.bfloat16)
+    turned = lax.dot_general(
+        table.astype(jnp.bfloat16),
+        twice,
+        (((0,), (0,)), ((), ())),
+        preferred_element_type=jnp.float32,
+    ).astype(jnp.bfloat16)
+    out_ref[count:, :] = jnp.zeros((SUB, width), jnp.bfloat16)
+    for q in range(experts // SUB):
+        out_ref[count:, q * LANES : (q + 1) * LANES] = turned[q * SUB : (q + 1) * SUB, :]
+
+
+def pack(ids, gates, tokens, experts):
+    count, width = tokens.shape
+    return pl.pallas_call(
+        functools.partial(pack_kernel, experts=experts),
+        out_shape=jax.ShapeDtypeStruct((count + SUB, width), jnp.bfloat16),
+        name="pack",
+    )(ids, gates, tokens)
+
+
+def expert_kernel(*refs, pairs, count, cap):
+    expert_ref = refs[0]
+    blocks = refs[1 : 1 + 2 * pairs]
+    w_in_ref, w_out_ref = refs[1 + 2 * pairs : 3 + 2 * pairs]
+    keep_ref, give_ref = refs[3 + 2 * pairs : 5 + 2 * pairs]
+    rows, tails, w_first, w_second, kept, given, in_sem, w_sem, out_sem = refs[5 + 2 * pairs :]
+    both = 2 * count
+    half = pairs // 2
+    width = rows.shape[1]
+    tail_copies = []
+    row_copies = []
+    for b in range(2 * pairs):
+        tail_copies.append(
+            pltpu.make_async_copy(
+                blocks[b].at[pl.ds(count, SUB)], tails.at[pl.ds(b * SUB, SUB)], in_sem.at[0, b]
+            )
+        )
+        row_copies.append(
+            pltpu.make_async_copy(
+                blocks[b].at[pl.ds(0, count)], rows.at[pl.ds(b * count, count)], in_sem.at[1, b]
+            )
+        )
+    for copy in tail_copies:
+        copy.start()
+    for copy in row_copies:
+        copy.start()
+    first_copy = pltpu.make_async_copy(w_in_ref.at[0], w_first, w_sem.at[0])
+    second_copy = pltpu.make_async_copy(w_out_ref.at[0], w_second, w_sem.at[1])
+    first_copy.start()
+    second_copy.start()
+
+    expert = expert_ref[0]
+    sub = expert % SUB
+    group = expert // SUB
+    for copy in tail_copies:
+        copy.wait()
+    table = tails[:, pl.ds(pl.multiple_of(group * LANES, LANES), LANES)]
+    row_of = lax.broadcasted_iota(jnp.int32, (pairs, 2 * pairs * SUB), 0)
+    col_of = lax.broadcasted_iota(jnp.int32, (pairs, 2 * pairs * SUB), 1)
+    pick_a = (col_of == (2 * row_of) * SUB + sub).astype(jnp.bfloat16)
+    pick_b = (col_of == (2 * row_of + 1) * SUB + sub).astype(jnp.bfloat16)
+    dot = functools.partial(jnp.dot, preferred_element_type=jnp.float32)
+    gate_a = dot(pick_a, table)
+    gate_b = dot(pick_b, table)
+    lane = lax.broadcasted_iota(jnp.int32, (pairs, LANES), 1)
+    gate = jnp.where(lane < count, gate_a, gate_b)
+    chosen = gate > 0.0
+    ones = chosen.astype(jnp.bfloat16)
+    upper = (
+        lax.broadcasted_iota(jnp.int32, (LANES, LANES), 0)
+        < lax.broadcasted_iota(jnp.int32, (LANES, LANES), 1)
+    ).astype(jnp.bfloat16)
+    inside = dot(ones, upper)
+    left = lax.broadcasted_iota(jnp.int32, (pairs, pairs), 0)
+    right = lax.broadcasted_iota(jnp.int32, (pairs, pairs), 1)
+    before = ((right < left) & (right // half == left // half)).astype(jnp.bfloat16)
+    total = jnp.sum(ones.astype(jnp.float32), axis=1, keepdims=True)
+    offset = dot(before, jnp.broadcast_to(total, (pairs, LANES)).astype(jnp.bfloat16))
+    seat = jnp.where(chosen, inside + offset, -1.0).astype(jnp.int32)
+
+    place = []
+    for p in range(2):
+        seats = lax.broadcasted_iota(jnp.int32, (cap, LANES), 0)
+        hot = [
+            (seats == seat[p * half + o : p * half + o + 1, :]).astype(jnp.bfloat16)
+            for o in range(half)
+        ]
+        weighted = [
+            hot[o] * gate[p * half + o : p * half + o + 1, :].astype(jnp.bfloat16)
+            for o in range(half)
+        ]
+        place.append((jnp.concatenate(hot, axis=1), jnp.concatenate(weighted, axis=1)))
+    for copy in row_copies:
+        copy.wait()
+    span = half * both
+    taken = [
+        dot(place[p][0], rows[p * span : (p + 1) * span, :]).astype(jnp.bfloat16) for p in range(2)
+    ]
+    taken = jnp.concatenate(taken, axis=0)
+    first_copy.wait()
+    hidden = jnp.maximum(dot(taken, w_first[...]), 0.0).astype(jnp.bfloat16)
+    second_copy.wait()
+    result = dot(hidden, w_second[...]).astype(jnp.bfloat16)
+    out_copies = []
+    for p in range(2):
+        spread = lax.dot_general(
+            place[p][1],
+            result[p * cap : (p + 1) * cap, :],
+            (((0,), (0,)), ((), ())),
+            preferred_element_type=jnp.float32,
+        ).astype(jnp.bfloat16)
+        for o in range(half):
+            at = p * half + o
+            kept[at] = spread[o * both : o * both + count, :]
+            given[at] = spread[o * both + count : (o + 1) * both, :]
+        for k, (store, target) in enumerate(((kept, keep_ref), (given, give_ref))):
+            copy = pltpu.make_async_copy(
+                store.at[pl.ds(p * half, half)],
+                target.at[pl.ds(p * half, half)],
+                out_sem.at[p, k],
+            )
+            copy.start()
+            out_copies.append(copy)
+    for copy in out_copies:
+        copy.wait()
+
+
+def expert_call(expert, blocks, w_in, w_out, count, cap):
+    pairs = len(blocks) // 2
+    width = blocks[0].shape[1]
+    units = w_in.shape[2]
+    anywhere = pl.BlockSpec(memory_space=pl.ANY)
+    out = jax.ShapeDtypeStruct((pairs, count, width), jnp.bfloat16)
+    return pl.pallas_call(
+        functools.partial(expert_kernel, pairs=pairs, count=count, cap=cap),
+        in_specs=[pl.BlockSpec(memory_space=pltpu.SMEM)] + [anywhere] * (len(blocks) + 2),
+        out_specs=[anywhere, anywhere],
+        out_shape=[out, out],
+        scratch_shapes=[
+            pltpu.VMEM((2 * pairs * count, width), jnp.bfloat16),
+            pltpu.VMEM((2 * pairs * SUB, width), jnp.bfloat16),
+            pltpu.VMEM((width, units), jnp.bfloat16),
+            pltpu.VMEM((units, width), jnp.bfloat16),
+            pltpu.VMEM((pairs, count, width), jnp.bfloat16),
+            pltpu.VMEM((pairs, count, width), jnp.bfloat16),
+            pltpu.SemaphoreType.DMA((2, 2 * pairs)),
+            pltpu.SemaphoreType.DMA((2,)),
+            pltpu.SemaphoreType.DMA((2, 2)),
+        ],
+        name="expert",
+    )(expert, *blocks, w_in, w_out)
+
+
+def on_rings(rings, tokens, expert_ids, gates, w_in, w_out):
+    axes = ("grp", "dev")
+    n_dev = lax.axis_size("dev")
+    experts = lax.axis_size("grp") * n_dev
+    count, width = tokens.shape
+    if 2 * count != LANES or experts % SUB or experts * LANES > SUB * width:
+        return per_device(tokens, expert_ids, gates, w_in, w_out)
+    length = rings.length
+    inverse = (rings.perms[1], rings.perms[0], rings.perms[2])
+    own = pack(expert_ids, gates, tokens, experts)
+    held = {(0, 0): own}
+    twin = {(0, 0): lax.ppermute(own, axes, rings.partner)}
+    for chosen in rings.rounds:
+        fresh = {}
+        for channel, block in chosen.items():
+            source = held[seen_from_source(channel, block, length)]
+            fresh[block] = lax.ppermute(source, axes, rings.perms[channel])
+        for block, value in fresh.items():
+            twin[block] = lax.ppermute(value, axes, rings.partner)
+        held.update(fresh)
+    order = sorted(held, key=lambda b: (b[1], b[0]))
+    blocks = [side[b] for b in order for side in (held, twin)]
+    expert = (lax.axis_index("grp") * n_dev + lax.axis_index("dev")).astype(jnp.int32).reshape(1)
+    cap = min(4 * count, length * 2 * count)
+    keep, give = expert_call(expert, blocks, w_in, w_out, count, cap)
+    back = lax.ppermute(give, axes, rings.partner)
+    parts = {b: [keep[i], back[i]] for i, b in enumerate(order)}
+
+    def total(block):
+        value = parts[block][0].astype(jnp.float32)
+        for other in parts[block][1:]:
+            value = value + other.astype(jnp.float32)
+        return value.astype(jnp.bfloat16)
+
+    for chosen in reversed(rings.rounds):
+        arrived = []
+        for channel, block in chosen.items():
+            value = lax.ppermute(total(block), axes, inverse[channel])
+            arrived.append((seen_from_source(channel, block, length), value))
+        for block, value in arrived:
+            parts[block].append(value)
+    return total((0, 0))
 
 
 def earlier_count(onehot):
@@ -137,8 +450,10 @@
 
 
 def solution(mesh):
+    rings = find_rings(mesh)
+    body = per_device if rings is None else functools.partial(on_rings, rings)
     return jax.shard_map(
-        per_device,
+        body,
         mesh=mesh,
         in_specs=(
             P(("grp", "dev"), None),

time: 165 us -> 89.5 us (0.54)
  blocking collectives: 77 us -> 0 us
  starting transfers between devices: 18.8 us -> 38.7 us
  matrix products: 17.1 us -> 0 us
  Pallas kernels: 0 us -> 10.8 us
  local copies, waits for them, and re-layouts: 10.8 us -> 3.23 us
  waiting for transfers between devices: 36.4 us -> 33.7 us
    all_to_all x1 -> x0, blocking collectives: 60 us -> none  [per_device(): lax.all_to_all(partial_value.reshape(n_grp, cap_grp, feature_width), 'grp...]
    ppermute x0 -> x47, starting transfers between devices: none -> 38.7 us  [the longest x15 19.6 us: on_rings(): fresh[block] = lax.ppermute(source, axes, rings.perms[channel])]
    all_to_all x4 -> x0, waiting for transfers between devices: 36.4 us -> none  [the longest x1 16.2 us: per_device(): lax.all_to_all(rows_out.reshape(n_grp, cap_grp, feature_width), 'grp', sp...]
    ppermute x0 -> x47, waiting for transfers between devices: none -> 33.7 us  [the longest x15 16.2 us: on_rings(): value = lax.ppermute(total(block), axes, inverse[channel])]
    all_to_all x4 -> x0, starting transfers between devices: 18.8 us -> none  [the longest x1 7.39 us: per_device(): lax.all_to_all(gains_out.reshape(n_grp, cap_grp, 2), 'grp', split_axis=0,...]
    dot_general x10 -> x0, matrix products: 17.1 us -> none  [the longest x2 7.78 us: one_block(): jnp.dot(hidden, w_second, preferred_element_type=jnp.float32)]
    all_gather x2 -> x0, blocking collectives: 17 us -> none  [the longest x1 12.6 us: per_device(): lax.all_gather(packed_rows, 'dev', axis=0, tiled=True)]
    pallas_call x0 -> x2, Pallas kernels: none -> 10.8 us  [the longest x1 8.82 us: expert_call(): pl.pallas_call(functools.partial(expert_kernel, pairs=pairs, count=count,...]
  transfers between devices with their start and end apart: 4 -> 47, of which waited for: 4 -> 24; matrix products, arithmetic and copies ran while one was open for 5% -> 0% of each run, Pallas kernels for 0% -> 0%
where the time goes in v1:
time: 89.5 us; the launch traced here: 89.3 us
  starting transfers between devices  38.7 us (43%)
  waiting for transfers between devices  33.7 us (38%)
  Pallas kernels  10.8 us (12%)
  local copies, waits for them, and re-layouts  3.23 us (4%)
  other arithmetic  2.36 us (3%)
    ppermute x15, starting transfers between devices, on_rings(): fresh[block] = lax.ppermute(source, axes, rings.perms[channel])  19.6 us
    ppermute x15, starting transfers between devices, on_rings(): value = lax.ppermute(total(block), axes, inverse[channel])  17.5 us
    ppermute x15, waiting for transfers between devices, on_rings(): value = lax.ppermute(total(block), axes, inverse[channel])  16.2 us
    ppermute x15, waiting for transfers between devices, on_rings(): fresh[block] = lax.ppermute(source, axes, rings.perms[channel])  12.8 us
    pallas_call x1, Pallas kernels, expert_call(): pl.pallas_call(functools.partial(expert_kernel, pairs=pairs, count=count,...  8.82 us
    ppermute x1, waiting for transfers between devices, on_rings(): back = lax.ppermute(give, axes, rings.partner)  3.46 us
    unnamed x66, local copies, waits for them, and re-layouts  3.23 us
    convert_element_type x8, other arithmetic, total(): return value.astype(jnp.bfloat16)  2.36 us
  transfers between devices with their start and end apart: 47, of which 24 were waited for; matrix products, arithmetic and copies ran while one was open for 0% of the time, Pallas kernels for 0%

profile of v1, /device:TPU:0, one launch (start us, length us, event | category | flops | bytes accessed | tf_op | source)
XLA Modules:
  0.0 89.3 jit_solution(1714069165127164137)
XLA Ops:
  2.8 1.9 %pack.1.refs_7_ = bf16[72,768]{1,0:T(8,128)(2,1)} custom-call(s32[64,8]{1,0:T(8,128)} %copy.6.ids_ref, bf16[64,8]{1,0:T(8,128)(2,1)} %copy.7.gates_ref, bf16[64,768]{1,0:T(8,128)(2,1)} %tokens_ref.1), custom_call_target="tpu_custom_call" | custom-call | tf_op jit(solution)/shard_map/pack/pallas_call | solution.py:136
  4.7 3.0 %collective-permute-start.21 = (bf16[72,768]{1,0:T(8,128)(2,1)}, bf16[72,768]{1,0:T(8,128)(2,1)S(1)}, u32[]{:S(2)}, u32[]{:S(2)}) collective-permute-start(bf16[72,768]{1,0:T(8,128)(2,1)} %pack.1.refs_7_), channel_id=1, source_target_pairs={{0,1},{1,0},{2,3},{3,2},{8,9},{9,8},{10,11},{11,10},{16,17},{17,16... | collective-permute-start | bytes 331784 | tf_op jit(solution)/shard_map/ppermute | solution.py:292
  11.0 1.7 %collective-permute-done.7.refs_9_ = bf16[72,768]{1,0:T(8,128)(2,1)S(1)} collective-permute-done((bf16[72,768]{1,0:T(8,128)(2,1)}, bf16[72,768]{1,0:T(8,128)(2,1)S(1)}, u32[]{:S(2)}, u32[]{:S(2)}) %collective-permute-start.7) | collective-permute-done | bytes 110624 | tf_op jit(solution)/shard_map/ppermute | solution.py:292
  12.8 1.9 %collective-permute-start.9 = (bf16[72,768]{1,0:T(8,128)(2,1)S(1)}, bf16[72,768]{1,0:T(8,128)(2,1)S(1)}, u32[]{:S(2)}, u32[]{:S(2)}) collective-permute-start(bf16[72,768]{1,0:T(8,128)(2,1)S(1)} %collective-permute-done.7.refs_9_), channel_id=1, source_target_pairs={{8,0},{9,1},{10,2},{11,3},{16,8},{17,9},{18,10},{19,11},{24,16},{2... | collective-permute-start | bytes 331784 | tf_op jit(solution)/shard_map/ppermute | solution.py:292
  17.4 2.5 %collective-permute-start.1 = (bf16[72,768]{1,0:T(8,128)(2,1)S(1)}, bf16[72,768]{1,0:T(8,128)(2,1)S(1)}, u32[]{:S(2)}, u32[]{:S(2)}) collective-permute-start(bf16[72,768]{1,0:T(8,128)(2,1)S(1)} %collective-permute-done.refs_5_), channel_id=1, source_target_pairs={{0,8},{1,9},{2,10},{3,11},{8,16},{9,17},{10,18},{11,19},{16,24},{1... | collective-permute-start | bytes 331784 | tf_op jit(solution)/shard_map/ppermute | solution.py:292
  20.1 1.6 %collective-permute-start.11 = (bf16[72,768]{1,0:T(8,128)(2,1)S(1)}, bf16[72,768]{1,0:T(8,128)(2,1)S(1)}, u32[]{:S(2)}, u32[]{:S(2)}) collective-permute-start(bf16[72,768]{1,0:T(8,128)(2,1)S(1)} %collective-permute-done.9.refs_11_), channel_id=1, source_target_pairs={{8,0},{9,1},{10,2},{11,3},{16,8},{17,9},{18,10},{19,11},{24,16},{2... | collective-permute-start | bytes 331784 | tf_op jit(solution)/shard_map/ppermute | solution.py:292
  22.2 2.4 %collective-permute-start.2 = (bf16[72,768]{1,0:T(8,128)(2,1)S(1)}, bf16[72,768]{1,0:T(8,128)(2,1)S(1)}, u32[]{:S(2)}, u32[]{:S(2)}) collective-permute-start(bf16[72,768]{1,0:T(8,128)(2,1)S(1)} %collective-permute-done.1.refs_3_), channel_id=1, source_target_pairs={{0,8},{1,9},{2,10},{3,11},{8,16},{9,17},{10,18},{11,19},{16,24},{1... | collective-permute-start | bytes 331784 | tf_op jit(solution)/shard_map/ppermute | solution.py:292
  27.2 2.2 %collective-permute-start.13 = (bf16[72,768]{1,0:T(8,128)(2,1)S(1)}, bf16[72,768]{1,0:T(8,128)(2,1)S(1)}, u32[]{:S(2)}, u32[]{:S(2)}) collective-permute-start(bf16[72,768]{1,0:T(8,128)(2,1)S(1)} %collective-permute-done.2.refs_1_), channel_id=1, source_target_pairs={{0,8},{1,9},{2,10},{3,11},{8,16},{9,17},{10,18},{11,19},{16,24},{1... | collective-permute-start | bytes 331784 | tf_op jit(solution)/shard_map/ppermute | solution.py:292
  29.4 1.7 %collective-permute-done.15.refs_19_ = bf16[72,768]{1,0:T(8,128)(2,1)S(1)} collective-permute-done((bf16[72,768]{1,0:T(8,128)(2,1)S(1)}, bf16[72,768]{1,0:T(8,128)(2,1)S(1)}, u32[]{:S(2)}, u32[]{:S(2)}) %collective-permute-start.15) | collective-permute-done | bytes 110624 | tf_op jit(solution)/shard_map/ppermute | solution.py:292
  32.3 1.5 %collective-permute-start.16 = (bf16[72,768]{1,0:T(8,128)(2,1)S(1)}, bf16[72,768]{1,0:T(8,128)(2,1)S(1)}, u32[]{:S(2)}, u32[]{:S(2)}) collective-permute-start(bf16[72,768]{1,0:T(8,128)(2,1)S(1)} %collective-permute-done.15.refs_19_), channel_id=1, source_target_pairs={{0,8},{1,9},{2,10},{3,11},{8,16},{9,17},{10,18},{11,19},{16,24},{1... | collective-permute-start | bytes 331784 | tf_op jit(solution)/shard_map/ppermute | solution.py:292
  35.2 1.8 %collective-permute-done.16.refs_17_ = bf16[72,768]{1,0:T(8,128)(2,1)S(1)} collective-permute-done((bf16[72,768]{1,0:T(8,128)(2,1)S(1)}, bf16[72,768]{1,0:T(8,128)(2,1)S(1)}, u32[]{:S(2)}, u32[]{:S(2)}) %collective-permute-start.16) | collective-permute-done | bytes 110624 | tf_op jit(solution)/shard_map/ppermute | solution.py:292
  37.1 1.5 %collective-permute-done.29.refs_31_ = bf16[72,768]{1,0:T(8,128)(2,1)S(1)} collective-permute-done((bf16[72,768]{1,0:T(8,128)(2,1)S(1)}, bf16[72,768]{1,0:T(8,128)(2,1)S(1)}, u32[]{:S(2)}, u32[]{:S(2)}) %collective-permute-start.29) | collective-permute-done | bytes 110624 | tf_op jit(solution)/shard_map/ppermute | solution.py:292
  40.6 8.8 %expert.1 = (bf16[16,64,768]{2,1,0:T(8,128)(2,1)}, bf16[16,64,768]{2,1,0:T(8,128)(2,1)}) custom-call(s32[1]{0:T(128)} %bitcast.refs_0_, bf16[72,768]{1,0:T(8,128)(2,1)} %copy-done.16, bf16[72,768]{1,0:T(8,128)(2,1)} %copy-done.27, bf16[72,768]{1,0:T(8,128)(2,1)} %copy-done.11, bf16[72,768]{1,0:T(8,128)(2,1)} %copy-done.19, bf16[72,768]{1,0:T(8,128)(2,1)} %copy-done.4, ...), custom_call_target="tpu_custom_call" | custom-call | tf_op jit(solution)/shard_map/expert/pallas_call | solution.py:256
  49.6 3.5 %collective-permute-done.31 = bf16[16,64,768]{2,1,0:T(8,128)(2,1)S(1)} collective-permute-done((bf16[16,64,768]{2,1,0:T(8,128)(2,1)}, bf16[16,64,768]{2,1,0:T(8,128)(2,1)S(1)}, u32[]{:S(2)}, u32[]{:S(2)}) %collective-permute-start.31) | collective-permute-done | bytes 1572896 | tf_op jit(solution)/shard_map/ppermute | solution.py:301
  55.9 3.4 %collective-permute-done.35 = bf16[64,768]{1,0:T(8,128)(2,1)S(1)} collective-permute-done((bf16[64,768]{1,0:T(8,128)(2,1)S(1)}, bf16[64,768]{1,0:T(8,128)(2,1)S(1)}, u32[]{:S(2)}, u32[]{:S(2)}) %collective-permute-start.35) | collective-permute-done | bytes 98336 | tf_op jit(solution)/shard_map/ppermute | solution.py:313
  61.7 2.8 %collective-permute-done.36 = bf16[64,768]{1,0:T(8,128)(2,1)S(1)} collective-permute-done((bf16[64,768]{1,0:T(8,128)(2,1)S(1)}, bf16[64,768]{1,0:T(8,128)(2,1)S(1)}, u32[]{:S(2)}, u32[]{:S(2)}) %collective-permute-start.36) | collective-permute-done | bytes 98336 | tf_op jit(solution)/shard_map/ppermute | solution.py:313
  66.4 1.5 %collective-permute-start.42 = (bf16[64,768]{1,0:T(8,128)(2,1)S(1)}, bf16[64,768]{1,0:T(8,128)(2,1)S(1)}, u32[]{:S(2)}, u32[]{:S(2)}) collective-permute-start(bf16[64,768]{1,0:T(8,128)(2,1)S(1)} %get-tuple-element.14), channel_id=1, source_target_pairs={{0,8},{1,9},{2,10},{3,11},{8,16},{9,17},{10,18},{11,19},{16,24},{1... | collective-permute-start | bytes 294920 | tf_op jit(solution)/shard_map/ppermute | solution.py:313
  67.9 1.6 %collective-permute-start.40 = (bf16[64,768]{1,0:T(8,128)(2,1)S(1)}, bf16[64,768]{1,0:T(8,128)(2,1)S(1)}, u32[]{:S(2)}, u32[]{:S(2)}) collective-permute-start(bf16[64,768]{1,0:T(8,128)(2,1)S(1)} %get-tuple-element.15), channel_id=1, source_target_pairs={{0,8},{1,9},{2,10},{3,11},{8,16},{9,17},{10,18},{11,19},{16,24},{1... | collective-permute-start | bytes 294920 | tf_op jit(solution)/shard_map/ppermute | solution.py:313
  72.6 1.8 %collective-permute-done.38 = bf16[64,768]{1,0:T(8,128)(2,1)S(1)} collective-permute-done((bf16[64,768]{1,0:T(8,128)(2,1)S(1)}, bf16[64,768]{1,0:T(8,128)(2,1)S(1)}, u32[]{:S(2)}, u32[]{:S(2)}) %collective-permute-start.38) | collective-permute-done | bytes 98336 | tf_op jit(solution)/shard_map/ppermute | solution.py:313
  74.4 2.1 %collective-permute-start.43 = (bf16[64,768]{1,0:T(8,128)(2,1)S(1)}, bf16[64,768]{1,0:T(8,128)(2,1)S(1)}, u32[]{:S(2)}, u32[]{:S(2)}) collective-permute-start(bf16[64,768]{1,0:T(8,128)(2,1)S(1)} %get-tuple-element.10), channel_id=1, source_target_pairs={{0,8},{1,9},{2,10},{3,11},{8,16},{9,17},{10,18},{11,19},{16,24},{1... | collective-permute-start | bytes 294920 | tf_op jit(solution)/shard_map/ppermute | solution.py:313
  79.2 1.6 %collective-permute-start.44 = (bf16[64,768]{1,0:T(8,128)(2,1)S(1)}, bf16[64,768]{1,0:T(8,128)(2,1)S(1)}, u32[]{:S(2)}, u32[]{:S(2)}) collective-permute-start(bf16[64,768]{1,0:T(8,128)(2,1)S(1)} %fusion.1), channel_id=1, source_target_pairs={{0,1},{1,0},{2,3},{3,2},{8,9},{9,8},{10,11},{11,10},{16,17},{17,16... | collective-permute-start | bytes 294920 | tf_op jit(solution)/shard_map/ppermute | solution.py:313
  82.1 1.7 %collective-permute-done.44 = bf16[64,768]{1,0:T(8,128)(2,1)S(1)} collective-permute-done((bf16[64,768]{1,0:T(8,128)(2,1)S(1)}, bf16[64,768]{1,0:T(8,128)(2,1)S(1)}, u32[]{:S(2)}, u32[]{:S(2)}) %collective-permute-start.44) | collective-permute-done | bytes 98336 | tf_op jit(solution)/shard_map/ppermute | solution.py:313
  83.9 2.1 %collective-permute-start.45 = (bf16[64,768]{1,0:T(8,128)(2,1)S(1)}, bf16[64,768]{1,0:T(8,128)(2,1)S(1)}, u32[]{:S(2)}, u32[]{:S(2)}) collective-permute-start(bf16[64,768]{1,0:T(8,128)(2,1)S(1)} %fusion.4), channel_id=1, source_target_pairs={{0,8},{1,9},{2,10},{3,11},{8,16},{9,17},{10,18},{11,19},{16,24},{1... | collective-permute-start | bytes 294920 | tf_op jit(solution)/shard_map/ppermute | solution.py:313
  86.0 2.6 %collective-permute-done.45 = bf16[64,768]{1,0:T(8,128)(2,1)S(1)} collective-permute-done((bf16[64,768]{1,0:T(8,128)(2,1)S(1)}, bf16[64,768]{1,0:T(8,128)(2,1)S(1)}, u32[]{:S(2)}, u32[]{:S(2)}) %collective-permute-start.45) | collective-permute-done | bytes 98336 | tf_op jit(solution)/shard_map/ppermute | solution.py:313
  (146 shorter events, 31.6 us)
Async XLA Ops:
  4.7 6.3 %collective-permute-start.21 = (bf16[72,768]{1,0:T(8,128)(2,1)}, bf16[72,768]{1,0:T(8,128)(2,1)S(1)}, u32[]{:S(2)}, u32[]{:S(2)}) collective-permute-start(bf16[72,768]{1,0:T(8,128)(2,1)} %pack.1.refs_7_), channel_id=1, source_target_pairs={{0,1},{1,0},{2,3},{3,2},{8,9},{9,8},{10,11},{11,10},{16,17},{17,16... | collective-permute-start | bytes 331784 | tf_op jit(solution)/shard_map/ppermute | solution.py:292
  7.7 5.0 %collective-permute-start.7 = (bf16[72,768]{1,0:T(8,128)(2,1)}, bf16[72,768]{1,0:T(8,128)(2,1)S(1)}, u32[]{:S(2)}, u32[]{:S(2)}) collective-permute-start(bf16[72,768]{1,0:T(8,128)(2,1)} %pack.1.refs_7_), channel_id=1, source_target_pairs={{8,0},{9,1},{10,2},{11,3},{16,8},{17,9},{18,10},{19,11},{24,16},{2... | collective-permute-start | bytes 331784 | tf_op jit(solution)/shard_map/ppermute | solution.py:292
  9.2 5.5 %collective-permute-start.6 = (bf16[72,768]{1,0:T(8,128)(2,1)}, bf16[72,768]{1,0:T(8,128)(2,1)S(1)}, u32[]{:S(2)}, u32[]{:S(2)}) collective-permute-start(bf16[72,768]{1,0:T(8,128)(2,1)} %pack.1.refs_7_), channel_id=1, source_target_pairs={{0,2},{1,3},{2,0},{3,1},{8,10},{9,11},{10,8},{11,9},{16,18},{17,19... | collective-permute-start | bytes 331784 | tf_op jit(solution)/shard_map/ppermute | solution.py:287
  9.2 5.7 %collective-permute-start = (bf16[72,768]{1,0:T(8,128)(2,1)}, bf16[72,768]{1,0:T(8,128)(2,1)S(1)}, u32[]{:S(2)}, u32[]{:S(2)}) collective-permute-start(bf16[72,768]{1,0:T(8,128)(2,1)} %pack.1.refs_7_), channel_id=1, source_target_pairs={{0,8},{1,9},{2,10},{3,11},{8,16},{9,17},{10,18},{11,19},{16,24},{1... | collective-permute-start | bytes 331784 | tf_op jit(solution)/shard_map/ppermute | solution.py:292
  11.0 5.3 %collective-permute-start.22 = (bf16[72,768]{1,0:T(8,128)(2,1)S(1)}, bf16[72,768]{1,0:T(8,128)(2,1)S(1)}, u32[]{:S(2)}, u32[]{:S(2)}) collective-permute-start(bf16[72,768]{1,0:T(8,128)(2,1)S(1)} %collective-permute-done.21.refs_23_), channel_id=1, source_target_pairs={{0,2},{1,3},{2,0},{3,1},{8,10},{9,11},{10,8},{11,9},{16,18},{17,19... | collective-permute-start | bytes 331784 | tf_op jit(solution)/shard_map/ppermute | solution.py:294
  12.8 7.1 %collective-permute-start.9 = (bf16[72,768]{1,0:T(8,128)(2,1)S(1)}, bf16[72,768]{1,0:T(8,128)(2,1)S(1)}, u32[]{:S(2)}, u32[]{:S(2)}) collective-permute-start(bf16[72,768]{1,0:T(8,128)(2,1)S(1)} %collective-permute-done.7.refs_9_), channel_id=1, source_target_pairs={{8,0},{9,1},{10,2},{11,3},{16,8},{17,9},{18,10},{19,11},{24,16},{2... | collective-permute-start | bytes 331784 | tf_op jit(solution)/shard_map/ppermute | solution.py:292
  14.7 5.2 %collective-permute-start.8 = (bf16[72,768]{1,0:T(8,128)(2,1)S(1)}, bf16[72,768]{1,0:T(8,128)(2,1)S(1)}, u32[]{:S(2)}, u32[]{:S(2)}) collective-permute-start(bf16[72,768]{1,0:T(8,128)(2,1)S(1)} %collective-permute-done.7.refs_9_), channel_id=1, source_target_pairs={{0,2},{1,3},{2,0},{3,1},{8,10},{9,11},{10,8},{11,9},{16,18},{17,19... | collective-permute-start | bytes 331784 | tf_op jit(solution)/shard_map/ppermute | solution.py:294
  14.9 5.3 %collective-permute-start.19 = (bf16[72,768]{1,0:T(8,128)(2,1)S(1)}, bf16[72,768]{1,0:T(8,128)(2,1)S(1)}, u32[]{:S(2)}, u32[]{:S(2)}) collective-permute-start(bf16[72,768]{1,0:T(8,128)(2,1)S(1)} %collective-permute-done.refs_5_), channel_id=1, source_target_pairs={{0,1},{1,0},{2,3},{3,2},{8,9},{9,8},{10,11},{11,10},{16,17},{17,16... | collective-permute-start | bytes 331784 | tf_op jit(solution)/shard_map/ppermute | solution.py:292
  16.3 5.4 %collective-permute-start.5 = (bf16[72,768]{1,0:T(8,128)(2,1)S(1)}, bf16[72,768]{1,0:T(8,128)(2,1)S(1)}, u32[]{:S(2)}, u32[]{:S(2)}) collective-permute-start(bf16[72,768]{1,0:T(8,128)(2,1)S(1)} %collective-permute-done.refs_5_), channel_id=1, source_target_pairs={{0,2},{1,3},{2,0},{3,1},{8,10},{9,11},{10,8},{11,9},{16,18},{17,19... | collective-permute-start | bytes 331784 | tf_op jit(solution)/shard_map/ppermute | solution.py:294
  19.9 5.8 %collective-permute-start.25 = (bf16[72,768]{1,0:T(8,128)(2,1)S(1)}, bf16[72,768]{1,0:T(8,128)(2,1)S(1)}, u32[]{:S(2)}, u32[]{:S(2)}) collective-permute-start(bf16[72,768]{1,0:T(8,128)(2,1)S(1)} %collective-permute-done.23.refs_25_), channel_id=1, source_target_pairs={{8,0},{9,1},{10,2},{11,3},{16,8},{17,9},{18,10},{19,11},{24,16},{2... | collective-permute-start | bytes 331784 | tf_op jit(solution)/shard_map/ppermute | solution.py:292
  19.9 5.8 %collective-permute-start.24 = (bf16[72,768]{1,0:T(8,128)(2,1)S(1)}, bf16[72,768]{1,0:T(8,128)(2,1)S(1)}, u32[]{:S(2)}, u32[]{:S(2)}) collective-permute-start(bf16[72,768]{1,0:T(8,128)(2,1)S(1)} %collective-permute-done.23.refs_25_), channel_id=1, source_target_pairs={{0,2},{1,3},{2,0},{3,1},{8,10},{9,11},{10,8},{11,9},{16,18},{17,19... | collective-permute-start | bytes 331784 | tf_op jit(solution)/shard_map/ppermute | solution.py:294
  20.1 6.7 %collective-permute-start.11 = (bf16[72,768]{1,0:T(8,128)(2,1)S(1)}, bf16[72,768]{1,0:T(8,128)(2,1)S(1)}, u32[]{:S(2)}, u32[]{:S(2)}) collective-permute-start(bf16[72,768]{1,0:T(8,128)(2,1)S(1)} %collective-permute-done.9.refs_11_), channel_id=1, source_target_pairs={{8,0},{9,1},{10,2},{11,3},{16,8},{17,9},{18,10},{19,11},{24,16},{2... | collective-permute-start | bytes 331784 | tf_op jit(solution)/shard_map/ppermute | solution.py:292
  21.7 5.1 %collective-permute-start.10 = (bf16[72,768]{1,0:T(8,128)(2,1)S(1)}, bf16[72,768]{1,0:T(8,128)(2,1)S(1)}, u32[]{:S(2)}, u32[]{:S(2)}) collective-permute-start(bf16[72,768]{1,0:T(8,128)(2,1)S(1)} %collective-permute-done.9.refs_11_), channel_id=1, source_target_pairs={{0,2},{1,3},{2,0},{3,1},{8,10},{9,11},{10,8},{11,9},{16,18},{17,19... | collective-permute-start | bytes 331784 | tf_op jit(solution)/shard_map/ppermute | solution.py:294
  22.2 5.0 %collective-permute-start.2 = (bf16[72,768]{1,0:T(8,128)(2,1)S(1)}, bf16[72,768]{1,0:T(8,128)(2,1)S(1)}, u32[]{:S(2)}, u32[]{:S(2)}) collective-permute-start(bf16[72,768]{1,0:T(8,128)(2,1)S(1)} %collective-permute-done.1.refs_3_), channel_id=1, source_target_pairs={{0,8},{1,9},{2,10},{3,11},{8,16},{9,17},{10,18},{11,19},{16,24},{1... | collective-permute-start | bytes 331784 | tf_op jit(solution)/shard_map/ppermute | solution.py:292
  25.7 5.5 %collective-permute-start.15 = (bf16[72,768]{1,0:T(8,128)(2,1)S(1)}, bf16[72,768]{1,0:T(8,128)(2,1)S(1)}, u32[]{:S(2)}, u32[]{:S(2)}) collective-permute-start(bf16[72,768]{1,0:T(8,128)(2,1)S(1)} %collective-permute-done.1.refs_3_), channel_id=1, source_target_pairs={{0,1},{1,0},{2,3},{3,2},{8,9},{9,8},{10,11},{11,10},{16,17},{17,16... | collective-permute-start | bytes 331784 | tf_op jit(solution)/shard_map/ppermute | solution.py:292
  26.9 5.5 %collective-permute-start.27 = (bf16[72,768]{1,0:T(8,128)(2,1)S(1)}, bf16[72,768]{1,0:T(8,128)(2,1)S(1)}, u32[]{:S(2)}, u32[]{:S(2)}) collective-permute-start(bf16[72,768]{1,0:T(8,128)(2,1)S(1)} %collective-permute-done.25.refs_27_), channel_id=1, source_target_pairs={{8,0},{9,1},{10,2},{11,3},{16,8},{17,9},{18,10},{19,11},{24,16},{2... | collective-permute-start | bytes 331784 | tf_op jit(solution)/shard_map/ppermute | solution.py:292
  27.2 6.6 %collective-permute-start.13 = (bf16[72,768]{1,0:T(8,128)(2,1)S(1)}, bf16[72,768]{1,0:T(8,128)(2,1)S(1)}, u32[]{:S(2)}, u32[]{:S(2)}) collective-permute-start(bf16[72,768]{1,0:T(8,128)(2,1)S(1)} %collective-permute-done.2.refs_1_), channel_id=1, source_target_pairs={{0,8},{1,9},{2,10},{3,11},{8,16},{9,17},{10,18},{11,19},{16,24},{1... | collective-permute-start | bytes 331784 | tf_op jit(solution)/shard_map/ppermute | solution.py:292
  29.4 5.2 %collective-permute-start.26 = (bf16[72,768]{1,0:T(8,128)(2,1)S(1)}, bf16[72,768]{1,0:T(8,128)(2,1)S(1)}, u32[]{:S(2)}, u32[]{:S(2)}) collective-permute-start(bf16[72,768]{1,0:T(8,128)(2,1)S(1)} %collective-permute-done.25.refs_27_), channel_id=1, source_target_pairs={{0,2},{1,3},{2,0},{3,1},{8,10},{9,11},{10,8},{11,9},{16,18},{17,19... | collective-permute-start | bytes 331784 | tf_op jit(solution)/shard_map/ppermute | solution.py:294
  54.4 4.9 %collective-permute-start.35 = (bf16[64,768]{1,0:T(8,128)(2,1)S(1)}, bf16[64,768]{1,0:T(8,128)(2,1)S(1)}, u32[]{:S(2)}, u32[]{:S(2)}) collective-permute-start(bf16[64,768]{1,0:T(8,128)(2,1)S(1)} %get-tuple-element.16), channel_id=1, source_target_pairs={{0,1},{1,0},{2,3},{3,2},{8,9},{9,8},{10,11},{11,10},{16,17},{17,16... | collective-permute-start | bytes 294920 | tf_op jit(solution)/shard_map/ppermute | solution.py:313
  60.6 8.9 %collective-permute-start.34 = (bf16[64,768]{1,0:T(8,128)(2,1)S(1)}, bf16[64,768]{1,0:T(8,128)(2,1)S(1)}, u32[]{:S(2)}, u32[]{:S(2)}) collective-permute-start(bf16[64,768]{1,0:T(8,128)(2,1)S(1)} %get-tuple-element.18), channel_id=1, source_target_pairs={{0,1},{1,0},{2,3},{3,2},{8,9},{9,8},{10,11},{11,10},{16,17},{17,16... | collective-permute-start | bytes 294920 | tf_op jit(solution)/shard_map/ppermute | solution.py:313
  64.6 5.0 %collective-permute-start.37 = (bf16[64,768]{1,0:T(8,128)(2,1)S(1)}, bf16[64,768]{1,0:T(8,128)(2,1)S(1)}, u32[]{:S(2)}, u32[]{:S(2)}) collective-permute-start(bf16[64,768]{1,0:T(8,128)(2,1)S(1)} %fusion.6), channel_id=1, source_target_pairs={{8,0},{9,1},{10,2},{11,3},{16,8},{17,9},{18,10},{19,11},{24,16},{2... | collective-permute-start | bytes 294920 | tf_op jit(solution)/shard_map/ppermute | solution.py:313
  65.3 5.2 %collective-permute-start.32 = (bf16[64,768]{1,0:T(8,128)(2,1)S(1)}, bf16[64,768]{1,0:T(8,128)(2,1)S(1)}, u32[]{:S(2)}, u32[]{:S(2)}) collective-permute-start(bf16[64,768]{1,0:T(8,128)(2,1)S(1)} %get-tuple-element.12), channel_id=1, source_target_pairs={{0,1},{1,0},{2,3},{3,2},{8,9},{9,8},{10,11},{11,10},{16,17},{17,16... | collective-permute-start | bytes 294920 | tf_op jit(solution)/shard_map/ppermute | solution.py:313
  76.5 5.6 %collective-permute-start.41 = (bf16[64,768]{1,0:T(8,128)(2,1)S(1)}, bf16[64,768]{1,0:T(8,128)(2,1)S(1)}, u32[]{:S(2)}, u32[]{:S(2)}) collective-permute-start(bf16[64,768]{1,0:T(8,128)(2,1)S(1)} %get-tuple-element.11), channel_id=1, source_target_pairs={{0,8},{1,9},{2,10},{3,11},{8,16},{9,17},{10,18},{11,19},{16,24},{1... | collective-permute-start | bytes 294920 | tf_op jit(solution)/shard_map/ppermute | solution.py:313
  80.7 5.2 %collective-permute-start.46 = (bf16[64,768]{1,0:T(8,128)(2,1)S(1)}, bf16[64,768]{1,0:T(8,128)(2,1)S(1)}, u32[]{:S(2)}, u32[]{:S(2)}) collective-permute-start(bf16[64,768]{1,0:T(8,128)(2,1)S(1)} %get-tuple-element.13), channel_id=1, source_target_pairs={{0,1},{1,0},{2,3},{3,2},{8,9},{9,8},{10,11},{11,10},{16,17},{17,16... | collective-permute-start | bytes 294920 | tf_op jit(solution)/shard_map/ppermute | solution.py:313
  (55 other events, 491.9 us)

commit v2 on v1

--- a/solution.py
+++ b/solution.py
@@ -2,6 +2,7 @@
 
 import jax
 import jax.numpy as jnp
+import numpy as np
 from jax import lax
 from jax.experimental import pallas as pl
 from jax.experimental.pallas import tpu as pltpu
@@ -12,11 +13,13 @@
 
 
 class Rings:
-    def __init__(self, length, rounds, clockwise, counter, mirror, partner):
+    def __init__(self, length, rounds, clockwise, counter, mirror, partner, cores):
         self.length = length
         self.rounds = rounds
         self.perms = (clockwise, counter, mirror)
         self.partner = partner
+        self.mates = [mate for _, mate in sorted(partner)]
+        self.cores = cores
 
 
 def wrap(step, length):
@@ -104,31 +107,24 @@
                 partner.append((a, index(turn(order[here]), 1 - core)))
             a, b = index(order[here], core), index(mirrored(order[here]), core)
             mirror += [(a, b), (b, a)]
-    return Rings(length, gather_rounds(length), clockwise, counter, mirror, partner)
+    cores = [device.core_on_chip for device in grid.flat]
+    return Rings(length, gather_rounds(length), clockwise, counter, mirror, partner, cores)
 
 
 def pack_kernel(ids_ref, gates_ref, tokens_ref, out_ref, *, experts):
     count, width = tokens_ref.shape
-    picks = ids_ref.shape[1]
+    picks = ids_ref.shape[0]
     out_ref[:count, :] = tokens_ref[...]
     ids = ids_ref[...]
     gates = gates_ref[...].astype(jnp.float32)
-    column = lax.broadcasted_iota(jnp.int32, (count, experts), 1)
-    table = jnp.zeros((count, experts), jnp.float32)
+    row = lax.broadcasted_iota(jnp.int32, (experts, count), 0)
+    table = jnp.zeros((experts, count), jnp.float32)
     for k in range(picks):
-        table += jnp.where(ids[:, k : k + 1] == column, gates[:, k : k + 1], 0.0)
-    lane = lax.broadcasted_iota(jnp.int32, (count, LANES), 1)
-    row = lax.broadcasted_iota(jnp.int32, (count, LANES), 0)
-    twice = ((lane & (count - 1)) == row).astype(jnp.bfloat16)
-    turned = lax.dot_general(
-        table.astype(jnp.bfloat16),
-        twice,
-        (((0,), (0,)), ((), ())),
-        preferred_element_type=jnp.float32,
-    ).astype(jnp.bfloat16)
+        table += jnp.where(ids[k : k + 1, :] == row, gates[k : k + 1, :], 0.0)
+    twice = jnp.concatenate([table, table], axis=1).astype(jnp.bfloat16)
     out_ref[count:, :] = jnp.zeros((SUB, width), jnp.bfloat16)
     for q in range(experts // SUB):
-        out_ref[count:, q * LANES : (q + 1) * LANES] = turned[q * SUB : (q + 1) * SUB, :]
+        out_ref[count:, q * LANES : (q + 1) * LANES] = twice[q * SUB : (q + 1) * SUB, :]
 
 
 def pack(ids, gates, tokens, experts):
@@ -137,140 +133,145 @@
         functools.partial(pack_kernel, experts=experts),
         out_shape=jax.ShapeDtypeStruct((count + SUB, width), jnp.bfloat16),
         name="pack",
-    )(ids, gates, tokens)
-
-
-def expert_kernel(*refs, pairs, count, cap):
-    expert_ref = refs[0]
-    blocks = refs[1 : 1 + 2 * pairs]
-    w_in_ref, w_out_ref = refs[1 + 2 * pairs : 3 + 2 * pairs]
-    keep_ref, give_ref = refs[3 + 2 * pairs : 5 + 2 * pairs]
-    rows, tails, w_first, w_second, kept, given, in_sem, w_sem, out_sem = refs[5 + 2 * pairs :]
-    both = 2 * count
+    )(ids.T, gates.T, tokens)
+
+
+def one_hot(seat, cap):
+    seats = lax.broadcasted_iota(jnp.int32, (cap, LANES), 0)
+    return jnp.where(seats == seat, 1.0, 0.0)
+
+
+def select_kernel(*refs, blocks, count, cap):
+    where_ref = refs[0]
+    block_refs = refs[1 : 1 + blocks]
+    own_ref, other_ref, seat_ref, gate_ref = refs[1 + blocks : 5 + blocks]
+    pairs = blocks // 2
     half = pairs // 2
-    width = rows.shape[1]
-    tail_copies = []
-    row_copies = []
-    for b in range(2 * pairs):
-        tail_copies.append(
-            pltpu.make_async_copy(
-                blocks[b].at[pl.ds(count, SUB)], tails.at[pl.ds(b * SUB, SUB)], in_sem.at[0, b]
-            )
-        )
-        row_copies.append(
-            pltpu.make_async_copy(
-                blocks[b].at[pl.ds(0, count)], rows.at[pl.ds(b * count, count)], in_sem.at[1, b]
-            )
-        )
-    for copy in tail_copies:
-        copy.start()
-    for copy in row_copies:
-        copy.start()
-    first_copy = pltpu.make_async_copy(w_in_ref.at[0], w_first, w_sem.at[0])
-    second_copy = pltpu.make_async_copy(w_out_ref.at[0], w_second, w_sem.at[1])
-    first_copy.start()
-    second_copy.start()
-
-    expert = expert_ref[0]
-    sub = expert % SUB
-    group = expert // SUB
-    for copy in tail_copies:
-        copy.wait()
-    table = tails[:, pl.ds(pl.multiple_of(group * LANES, LANES), LANES)]
-    row_of = lax.broadcasted_iota(jnp.int32, (pairs, 2 * pairs * SUB), 0)
-    col_of = lax.broadcasted_iota(jnp.int32, (pairs, 2 * pairs * SUB), 1)
-    pick_a = (col_of == (2 * row_of) * SUB + sub).astype(jnp.bfloat16)
-    pick_b = (col_of == (2 * row_of + 1) * SUB + sub).astype(jnp.bfloat16)
     dot = functools.partial(jnp.dot, preferred_element_type=jnp.float32)
-    gate_a = dot(pick_a, table)
-    gate_b = dot(pick_b, table)
-    lane = lax.broadcasted_iota(jnp.int32, (pairs, LANES), 1)
-    gate = jnp.where(lane < count, gate_a, gate_b)
-    chosen = gate > 0.0
-    ones = chosen.astype(jnp.bfloat16)
+    tails = jnp.concatenate([r[count:, :] for r in block_refs], axis=0)
     upper = (
         lax.broadcasted_iota(jnp.int32, (LANES, LANES), 0)
         < lax.broadcasted_iota(jnp.int32, (LANES, LANES), 1)
     ).astype(jnp.bfloat16)
-    inside = dot(ones, upper)
     left = lax.broadcasted_iota(jnp.int32, (pairs, pairs), 0)
     right = lax.broadcasted_iota(jnp.int32, (pairs, pairs), 1)
     before = ((right < left) & (right // half == left // half)).astype(jnp.bfloat16)
-    total = jnp.sum(ones.astype(jnp.float32), axis=1, keepdims=True)
-    offset = dot(before, jnp.broadcast_to(total, (pairs, LANES)).astype(jnp.bfloat16))
-    seat = jnp.where(chosen, inside + offset, -1.0).astype(jnp.int32)
-
-    place = []
-    for p in range(2):
-        seats = lax.broadcasted_iota(jnp.int32, (cap, LANES), 0)
-        hot = [
-            (seats == seat[p * half + o : p * half + o + 1, :]).astype(jnp.bfloat16)
-            for o in range(half)
-        ]
-        weighted = [
-            hot[o] * gate[p * half + o : p * half + o + 1, :].astype(jnp.bfloat16)
-            for o in range(half)
-        ]
-        place.append((jnp.concatenate(hot, axis=1), jnp.concatenate(weighted, axis=1)))
-    for copy in row_copies:
-        copy.wait()
-    span = half * both
-    taken = [
-        dot(place[p][0], rows[p * span : (p + 1) * span, :]).astype(jnp.bfloat16) for p in range(2)
+    lane = lax.broadcasted_iota(jnp.int32, (pairs, LANES), 1)
+    row_of = lax.broadcasted_iota(jnp.int32, (pairs, blocks * SUB), 0)
+    col_of = lax.broadcasted_iota(jnp.int32, (pairs, blocks * SUB), 1)
+    groups = tails.shape[1] // LANES
+    rows = [
+        jnp.concatenate([r[:count, :] for r in block_refs[p * pairs : (p + 1) * pairs]], axis=0)
+        for p in range(2)
     ]
-    taken = jnp.concatenate(taken, axis=0)
+    for k, out_ref in enumerate((own_ref, other_ref)):
+        sub = where_ref[2 * k]
+        group = where_ref[2 * k + 1]
+        table = tails[:, :LANES]
+        for q in range(1, groups):
+            table = jnp.where(group == q, tails[:, q * LANES : (q + 1) * LANES], table)
+        pick_a = (col_of == (2 * row_of) * SUB + sub).astype(jnp.bfloat16)
+        pick_b = (col_of == (2 * row_of + 1) * SUB + sub).astype(jnp.bfloat16)
+        gate = jnp.where(lane < count, dot(pick_a, table), dot(pick_b, table))
+        chosen = gate > 0.0
+        ones = jnp.where(chosen, 1.0, 0.0)
+        total = jnp.broadcast_to(jnp.sum(ones, axis=1, keepdims=True), (pairs, LANES))
+        spot = dot(ones.astype(jnp.bfloat16), upper) + dot(before, total.astype(jnp.bfloat16))
+        spot = spot.astype(jnp.int32)
+        seat = jnp.where(where_ref[4] == 0, spot, cap - 1 - spot)
+        seat = jnp.where(chosen, seat, -1)
+        seat_ref[k] = seat
+        gate_ref[k] = gate
+        for p in range(2):
+            hot = jnp.concatenate(
+                [one_hot(seat[o : o + 1, :], cap) for o in range(p * half, (p + 1) * half)], axis=1
+            ).astype(jnp.bfloat16)
+            out_ref[p * cap : (p + 1) * cap, :] = dot(hot, rows[p]).astype(jnp.bfloat16)
+
+
+def select(where, blocks, count, cap):
+    width = blocks[0].shape[1]
+    pairs = len(blocks) // 2
+    taken = jax.ShapeDtypeStruct((2 * cap, width), jnp.bfloat16)
+    return pl.pallas_call(
+        functools.partial(select_kernel, blocks=len(blocks), count=count, cap=cap),
+        in_specs=[pl.BlockSpec(memory_space=pltpu.SMEM)]
+        + [pl.BlockSpec(memory_space=pltpu.VMEM)] * len(blocks),
+        out_shape=[
+            taken,
+            taken,
+            jax.ShapeDtypeStruct((2, pairs, LANES), jnp.int32),
+            jax.ShapeDtypeStruct((2, pairs, LANES), jnp.float32),
+        ],
+        name="select",
+    )(where, *blocks)
+
+
+def expert_kernel(own_ref, came_ref, w_in_ref, w_out_ref, out_ref, w_first, w_second, sem):
+    first_copy = pltpu.make_async_copy(w_in_ref.at[0], w_first, sem.at[0])
+    second_copy = pltpu.make_async_copy(w_out_ref.at[0], w_second, sem.at[1])
+    first_copy.start()
+    second_copy.start()
+    rows = own_ref[...] + came_ref[...]
     first_copy.wait()
-    hidden = jnp.maximum(dot(taken, w_first[...]), 0.0).astype(jnp.bfloat16)
+    hidden = jnp.dot(rows, w_first[...], preferred_element_type=jnp.float32)
+    hidden = jnp.maximum(hidden, 0.0).astype(jnp.bfloat16)
     second_copy.wait()
-    result = dot(hidden, w_second[...]).astype(jnp.bfloat16)
-    out_copies = []
-    for p in range(2):
-        spread = lax.dot_general(
-            place[p][1],
-            result[p * cap : (p + 1) * cap, :],
-            (((0,), (0,)), ((), ())),
-            preferred_element_type=jnp.float32,
-        ).astype(jnp.bfloat16)
-        for o in range(half):
-            at = p * half + o
-            kept[at] = spread[o * both : o * both + count, :]
-            given[at] = spread[o * both + count : (o + 1) * both, :]
-        for k, (store, target) in enumerate(((kept, keep_ref), (given, give_ref))):
-            copy = pltpu.make_async_copy(
-                store.at[pl.ds(p * half, half)],
-                target.at[pl.ds(p * half, half)],
-                out_sem.at[p, k],
-            )
-            copy.start()
-            out_copies.append(copy)
-    for copy in out_copies:
-        copy.wait()
-
-
-def expert_call(expert, blocks, w_in, w_out, count, cap):
-    pairs = len(blocks) // 2
-    width = blocks[0].shape[1]
-    units = w_in.shape[2]
+    out_ref[...] = jnp.dot(hidden, w_second[...], preferred_element_type=jnp.float32).astype(
+        jnp.bfloat16
+    )
+
+
+def expert(own, came, w_in, w_out):
+    width, units = w_in.shape[1:]
+    vmem = pl.BlockSpec(memory_space=pltpu.VMEM)
     anywhere = pl.BlockSpec(memory_space=pl.ANY)
-    out = jax.ShapeDtypeStruct((pairs, count, width), jnp.bfloat16)
     return pl.pallas_call(
-        functools.partial(expert_kernel, pairs=pairs, count=count, cap=cap),
-        in_specs=[pl.BlockSpec(memory_space=pltpu.SMEM)] + [anywhere] * (len(blocks) + 2),
-        out_specs=[anywhere, anywhere],
-        out_shape=[out, out],
+        expert_kernel,
+        in_specs=[vmem, vmem, anywhere, anywhere],
+        out_shape=jax.ShapeDtypeStruct(own.shape, jnp.bfloat16),
         scratch_shapes=[
-            pltpu.VMEM((2 * pairs * count, width), jnp.bfloat16),
-            pltpu.VMEM((2 * pairs * SUB, width), jnp.bfloat16),
             pltpu.VMEM((width, units), jnp.bfloat16),
             pltpu.VMEM((units, width), jnp.bfloat16),
-            pltpu.VMEM((pairs, count, width), jnp.bfloat16),
-            pltpu.VMEM((pairs, count, width), jnp.bfloat16),
-            pltpu.SemaphoreType.DMA((2, 2 * pairs)),
             pltpu.SemaphoreType.DMA((2,)),
-            pltpu.SemaphoreType.DMA((2, 2)),
         ],
         name="expert",
-    )(expert, *blocks, w_in, w_out)
+    )(own, came, w_in, w_out)
+
+
+def spread_kernel(own_ref, came_ref, seat_ref, gate_ref, *out_refs, count, cap):
+    pairs = seat_ref.shape[1]
+    half = pairs // 2
+    for p in range(2):
+        value = None
+        for k, ref in enumerate((own_ref, came_ref)):
+            weights = jnp.concatenate(
+                [
+                    one_hot(seat_ref[k, o : o + 1, :], cap) * gate_ref[k, o : o + 1, :]
+                    for o in range(p * half, (p + 1) * half)
+                ],
+                axis=1,
+            ).astype(jnp.bfloat16)
+            part = lax.dot_general(
+                weights,
+                ref[p * cap : (p + 1) * cap, :],
+                (((0,), (0,)), ((), ())),
+                preferred_element_type=jnp.float32,
+            )
+            value = part if value is None else value + part
+        value = value.astype(jnp.bfloat16)
+        for o in range(pairs):
+            out_refs[p * pairs + o][...] = value[o * count : (o + 1) * count, :]
+
+
+def spread(own, came, seat, gate, count, cap):
+    blocks = 2 * seat.shape[1]
+    out = jax.ShapeDtypeStruct((count, own.shape[1]), jnp.bfloat16)
+    return pl.pallas_call(
+        functools.partial(spread_kernel, count=count, cap=cap),
+        out_shape=[out] * blocks,
+        name="spread",
+    )(own, came, seat, gate)
 
 
 def on_rings(rings, tokens, expert_ids, gates, w_in, w_out):
@@ -278,33 +279,40 @@
     n_dev = lax.axis_size("dev")
     experts = lax.axis_size("grp") * n_dev
     count, width = tokens.shape
-    if 2 * count != LANES or experts % SUB or experts * LANES > SUB * width:
+    length = rings.length
+    if 2 * count != LANES or length % 4 or experts % SUB or experts * LANES > SUB * width:
         return per_device(tokens, expert_ids, gates, w_in, w_out)
-    length = rings.length
     inverse = (rings.perms[1], rings.perms[0], rings.perms[2])
-    own = pack(expert_ids, gates, tokens, experts)
-    held = {(0, 0): own}
-    twin = {(0, 0): lax.ppermute(own, axes, rings.partner)}
+    where = np.asarray(
+        [
+            (here % SUB, here // SUB, mate % SUB, mate // SUB, core)
+            for here, (mate, core) in enumerate(zip(rings.mates, rings.cores, strict=True))
+        ],
+        np.int32,
+    )
+    here = lax.axis_index("grp") * n_dev + lax.axis_index("dev")
+    where = lax.dynamic_slice(jnp.asarray(where), (here, 0), (1, where.shape[1]))[0]
+
+    held = {(0, 0): pack(expert_ids, gates, tokens, experts)}
     for chosen in rings.rounds:
         fresh = {}
         for channel, block in chosen.items():
             source = held[seen_from_source(channel, block, length)]
             fresh[block] = lax.ppermute(source, axes, rings.perms[channel])
-        for block, value in fresh.items():
-            twin[block] = lax.ppermute(value, axes, rings.partner)
         held.update(fresh)
     order = sorted(held, key=lambda b: (b[1], b[0]))
-    blocks = [side[b] for b in order for side in (held, twin)]
-    expert = (lax.axis_index("grp") * n_dev + lax.axis_index("dev")).astype(jnp.int32).reshape(1)
-    cap = min(4 * count, length * 2 * count)
-    keep, give = expert_call(expert, blocks, w_in, w_out, count, cap)
-    back = lax.ppermute(give, axes, rings.partner)
-    parts = {b: [keep[i], back[i]] for i, b in enumerate(order)}
+    cap = 4 * count
+    own, other, seat, gate = select(where, [held[b] for b in order], count, cap)
+    came = lax.ppermute(other, axes, rings.partner)
+    result = expert(own, came, w_in, w_out)
+    theirs = lax.ppermute(result, axes, rings.partner)
+    sums = spread(result, theirs, seat, gate, count, cap)
+    parts = {b: [sums[i]] for i, b in enumerate(order)}
 
     def total(block):
         value = parts[block][0].astype(jnp.float32)
-        for other in parts[block][1:]:
-            value = value + other.astype(jnp.float32)
+        for more in parts[block][1:]:
+            value = value + more.astype(jnp.float32)
         return value.astype(jnp.bfloat16)
 
     for chosen in reversed(rings.rounds):

time: 89.5 us -> 89.1 us (level)
  waiting for transfers between devices: 33.7 us -> 24.4 us
  other arithmetic: 2.36 us -> 8.11 us
  Pallas kernels: 10.8 us -> 16.4 us
  starting transfers between devices: 38.7 us -> 35.7 us
    ppermute x15, waiting for transfers between devices: 16.2 us -> 9.48 us  [on_rings(): value = lax.ppermute(total(block), axes, inverse[channel])]
    pallas_call x1 -> x3, Pallas kernels: 8.82 us -> 14.8 us  [the longest x1 7.51 us: expert(): pl.pallas_call(expert_kernel, in_specs=[vmem, vmem, anywhere, anywhere],...]
    convert_element_type x8 -> x10, other arithmetic: 2.36 us -> 8.11 us  [total(): return value.astype(jnp.bfloat16)]
    ppermute x15, waiting for transfers between devices: 12.8 us -> 10 us  [on_rings(): fresh[block] = lax.ppermute(source, axes, rings.perms[channel])]
    ppermute x15, starting transfers between devices: 19.6 us -> 17.9 us  [on_rings(): fresh[block] = lax.ppermute(source, axes, rings.perms[channel])]
    ppermute x17 -> x2, starting transfers between devices: 1.54 us -> 0.2 us  [the longest x1 0.2 us: on_rings(): theirs = lax.ppermute(result, axes, rings.partner)]
    squeeze x0 -> x1, local copies, waits for them, and re-layouts: none -> 1.2 us  [on_rings(): lax.dynamic_slice(jnp.asarray(where), (here, 0), (1, where.shape[1]))[0]]
    unnamed x66 -> x38, local copies, waits for them, and re-layouts: 3.23 us -> 2.48 us
  transfers between devices with their start and end apart: 47 -> 32, of which waited for: 24 -> 16; matrix products, arithmetic and copies ran while one was open for 0% -> 10% of each run, Pallas kernels for 0% -> 0%
where the time goes in v2:
time: 89.1 us; the launch traced here: 88.5 us
  starting transfers between devices  35.7 us (40%)
  waiting for transfers between devices  24.4 us (27%)
  Pallas kernels  16.4 us (18%)
  other arithmetic  8.11 us (9%)
  local copies, waits for them, and re-layouts  3.68 us (4%)
    ppermute x15, starting transfers between devices, on_rings(): fresh[block] = lax.ppermute(source, axes, rings.perms[channel])  17.9 us
    ppermute x15, starting transfers between devices, on_rings(): value = lax.ppermute(total(block), axes, inverse[channel])  17.6 us
    ppermute x15, waiting for transfers between devices, on_rings(): fresh[block] = lax.ppermute(source, axes, rings.perms[channel])  10 us
    ppermute x15, waiting for transfers between devices, on_rings(): value = lax.ppermute(total(block), axes, inverse[channel])  9.48 us
    convert_element_type x10, other arithmetic, total(): return value.astype(jnp.bfloat16)  8.11 us
    pallas_call x1, Pallas kernels, expert(): pl.pallas_call(expert_kernel, in_specs=[vmem, vmem, anywhere, anywhere],...  7.51 us
    pallas_call x1, Pallas kernels, select(): pl.pallas_call(functools.partial(select_kernel, blocks=len(blocks), count...  4.1 us
    pallas_call x1, Pallas kernels, spread(): pl.pallas_call(functools.partial(spread_kernel, count=count, cap=cap), ou...  3.18 us
  transfers between devices with their start and end apart: 32, of which 16 were waited for; matrix products, arithmetic and copies ran while one was open for 10% of the time, Pallas kernels for 0%

profile of v2, /device:TPU:0, one launch (start us, length us, event | category | flops | bytes accessed | tf_op | source)
XLA Modules:
  0.0 88.5 jit_solution(14442497672582150633)
XLA Ops:
  0.0 1.6 %pack.1.refs_4_ = bf16[72,768]{1,0:T(8,128)(2,1)} custom-call(s32[8,64]{1,0:T(8,128)} %bitcast.4, bf16[8,64]{1,0:T(8,128)(2,1)} %bitcast.5, bf16[64,768]{1,0:T(8,128)(2,1)} %tokens_ref.1), custom_call_target="tpu_custom_call" | custom-call | tf_op jit(solution)/shard_map/pack/pallas_call | solution.py:132
  1.6 3.1 %collective-permute-start = (bf16[72,768]{1,0:T(8,128)(2,1)}, bf16[72,768]{1,0:T(8,128)(2,1)S(1)}, u32[]{:S(2)}, u32[]{:S(2)}) collective-permute-start(bf16[72,768]{1,0:T(8,128)(2,1)} %pack.1.refs_4_), channel_id=1, source_target_pairs={{0,8},{1,9},{2,10},{3,11},{8,16},{9,17},{10,18},{11,19},{16,24},{1... | collective-permute-start | bytes 331784 | tf_op jit(solution)/shard_map/ppermute | solution.py:301
  4.7 3.2 %collective-permute-done.refs_3_ = bf16[72,768]{1,0:T(8,128)(2,1)S(1)} collective-permute-done((bf16[72,768]{1,0:T(8,128)(2,1)}, bf16[72,768]{1,0:T(8,128)(2,1)S(1)}, u32[]{:S(2)}, u32[]{:S(2)}) %collective-permute-start) | collective-permute-done | bytes 110624 | tf_op jit(solution)/shard_map/ppermute | solution.py:301
  7.9 1.8 %collective-permute-start.1 = (bf16[72,768]{1,0:T(8,128)(2,1)S(1)}, bf16[72,768]{1,0:T(8,128)(2,1)S(1)}, u32[]{:S(2)}, u32[]{:S(2)}) collective-permute-start(bf16[72,768]{1,0:T(8,128)(2,1)S(1)} %collective-permute-done.refs_3_), channel_id=1, source_target_pairs={{0,8},{1,9},{2,10},{3,11},{8,16},{9,17},{10,18},{11,19},{16,24},{1... | collective-permute-start | bytes 331784 | tf_op jit(solution)/shard_map/ppermute | solution.py:301
  9.7 1.5 %collective-permute-start.11 = (bf16[72,768]{1,0:T(8,128)(2,1)S(1)}, bf16[72,768]{1,0:T(8,128)(2,1)S(1)}, u32[]{:S(2)}, u32[]{:S(2)}) collective-permute-start(bf16[72,768]{1,0:T(8,128)(2,1)S(1)} %collective-permute-done.3.refs_5_), channel_id=1, source_target_pairs={{0,1},{1,0},{2,3},{3,2},{8,9},{9,8},{10,11},{11,10},{16,17},{17,16... | collective-permute-start | bytes 331784 | tf_op jit(solution)/shard_map/ppermute | solution.py:301
  12.6 1.8 %collective-permute-start.2 = (bf16[72,768]{1,0:T(8,128)(2,1)S(1)}, bf16[72,768]{1,0:T(8,128)(2,1)S(1)}, u32[]{:S(2)}, u32[]{:S(2)}) collective-permute-start(bf16[72,768]{1,0:T(8,128)(2,1)S(1)} %collective-permute-done.1.refs_2_), channel_id=1, source_target_pairs={{0,8},{1,9},{2,10},{3,11},{8,16},{9,17},{10,18},{11,19},{16,24},{1... | collective-permute-start | bytes 331784 | tf_op jit(solution)/shard_map/ppermute | solution.py:301
  14.5 1.5 %collective-permute-start.10 = (bf16[72,768]{1,0:T(8,128)(2,1)}, bf16[72,768]{1,0:T(8,128)(2,1)S(1)}, u32[]{:S(2)}, u32[]{:S(2)}) collective-permute-start(bf16[72,768]{1,0:T(8,128)(2,1)} %pack.1.refs_4_), channel_id=1, source_target_pairs={{0,1},{1,0},{2,3},{3,2},{8,9},{9,8},{10,11},{11,10},{16,17},{17,16... | collective-permute-start | bytes 331784 | tf_op jit(solution)/shard_map/ppermute | solution.py:301
  22.6 1.5 %collective-permute-done.12.refs_14_ = bf16[72,768]{1,0:T(8,128)(2,1)S(1)} collective-permute-done((bf16[72,768]{1,0:T(8,128)(2,1)S(1)}, bf16[72,768]{1,0:T(8,128)(2,1)S(1)}, u32[]{:S(2)}, u32[]{:S(2)}) %collective-permute-start.12) | collective-permute-done | bytes 110624 | tf_op jit(solution)/shard_map/ppermute | solution.py:301
  24.3 1.9 %collective-permute-start.8 = (bf16[72,768]{1,0:T(8,128)(2,1)S(1)}, bf16[72,768]{1,0:T(8,128)(2,1)S(1)}, u32[]{:S(2)}, u32[]{:S(2)}) collective-permute-start(bf16[72,768]{1,0:T(8,128)(2,1)S(1)} %collective-permute-done.7.refs_10_), channel_id=1, source_target_pairs={{0,8},{1,9},{2,10},{3,11},{8,16},{9,17},{10,18},{11,19},{16,24},{1... | collective-permute-start | bytes 331784 | tf_op jit(solution)/shard_map/ppermute | solution.py:301
  29.0 1.9 %collective-permute-done.14.refs_16_ = bf16[72,768]{1,0:T(8,128)(2,1)S(1)} collective-permute-done((bf16[72,768]{1,0:T(8,128)(2,1)S(1)}, bf16[72,768]{1,0:T(8,128)(2,1)S(1)}, u32[]{:S(2)}, u32[]{:S(2)}) %collective-permute-start.14) | collective-permute-done | bytes 110624 | tf_op jit(solution)/shard_map/ppermute | solution.py:301
  31.6 4.1 %select.1 = (bf16[512,768]{1,0:T(8,128)(2,1)}, bf16[512,768]{1,0:T(8,128)(2,1)}, s32[2,8,128]{2,1,0:T(8,128)}, f32[2,8,128]{2,1,0:T(8,128)}) custom-call(s32[5]{0:T(128)} %dynamic-slice_bitcast_fusion.refs_0_, bf16[72,768]{1,0:T(8,128)(2,1)} %copy-done.6, bf16[72,768]{1,0:T(8,128)(2,1)} %copy-done.4, bf16[72,768]{1,0:T(8,128)(2,1)} %copy-done.2, ...), custom_call_target="tpu_custom_call" | custom-call | tf_op jit(solution)/shard_map/select/pallas_call | solution.py:196
  35.8 2.5 %collective-permute-done.15.came_ref = bf16[512,768]{1,0:T(8,128)(2,1)S(1)} collective-permute-done((bf16[512,768]{1,0:T(8,128)(2,1)}, bf16[512,768]{1,0:T(8,128)(2,1)S(1)}, u32[]{:S(2)}, u32[]{:S(2)}) %collective-permute-start.15) | collective-permute-done | bytes 786464 | tf_op jit(solution)/shard_map/ppermute | solution.py:306
  39.1 7.5 %expert.1.own_ref = bf16[512,768]{1,0:T(8,128)(2,1)} custom-call(bf16[512,768]{1,0:T(8,128)(2,1)} %get-tuple-element.25.own_ref, bf16[512,768]{1,0:T(8,128)(2,1)} %copy-done, bf16[1,768,1536]{2,1,0:T(8,128)(2,1)} %w_in_ref.1, bf16[1,1536,768]{2,1,0:T(8,128)(2,1)} %w_out_ref.1), custom_call_target="tpu_custom_call" | custom-call | tf_op jit(solution)/shard_map/expert/pallas_call | solution.py:229
  46.9 2.4 %collective-permute-done.16.came_ref = bf16[512,768]{1,0:T(8,128)(2,1)S(1)} collective-permute-done((bf16[512,768]{1,0:T(8,128)(2,1)}, bf16[512,768]{1,0:T(8,128)(2,1)S(1)}, u32[]{:S(2)}, u32[]{:S(2)}) %collective-permute-start.16) | collective-permute-done | bytes 786464 | tf_op jit(solution)/shard_map/ppermute | solution.py:308
  50.1 3.2 %spread.1 = (bf16[64,768]{1,0:T(8,128)(2,1)}, bf16[64,768]{1,0:T(8,128)(2,1)}, bf16[64,768]{1,0:T(8,128)(2,1)}, bf16[64,768]{1,0:T(8,128)(2,1)}, bf16[64,768]{1,...) custom-call(bf16[512,768]{1,0:T(8,128)(2,1)} %expert.1.own_ref, ...), custom_call_target="tpu_custom_call" | custom-call | tf_op jit(solution)/shard_map/spread/pallas_call | solution.py:270
  53.9 1.6 %collective-permute-start.20 = (bf16[64,768]{1,0:T(8,128)(2,1)}, bf16[64,768]{1,0:T(8,128)(2,1)S(1)}, u32[]{:S(2)}, u32[]{:S(2)}) collective-permute-start(bf16[64,768]{1,0:T(8,128)(2,1)} %get-tuple-element.37), channel_id=1, source_target_pairs={{0,1},{1,0},{2,3},{3,2},{8,9},{9,8},{10,11},{11,10},{16,17},{17,16... | collective-permute-start | bytes 294920 | tf_op jit(solution)/shard_map/ppermute | solution.py:321
  55.5 1.9 %collective-permute-start.25 = (bf16[64,768]{1,0:T(8,128)(2,1)}, bf16[64,768]{1,0:T(8,128)(2,1)S(1)}, u32[]{:S(2)}, u32[]{:S(2)}) collective-permute-start(bf16[64,768]{1,0:T(8,128)(2,1)} %get-tuple-element.40), channel_id=1, source_target_pairs={{0,8},{1,9},{2,10},{3,11},{8,16},{9,17},{10,18},{11,19},{16,24},{1... | collective-permute-start | bytes 294920 | tf_op jit(solution)/shard_map/ppermute | solution.py:321
  57.4 1.6 %collective-permute-start.27 = (bf16[64,768]{1,0:T(8,128)(2,1)}, bf16[64,768]{1,0:T(8,128)(2,1)S(1)}, u32[]{:S(2)}, u32[]{:S(2)}) collective-permute-start(bf16[64,768]{1,0:T(8,128)(2,1)} %get-tuple-element.43), channel_id=1, source_target_pairs={{0,8},{1,9},{2,10},{3,11},{8,16},{9,17},{10,18},{11,19},{16,24},{1... | collective-permute-start | bytes 294920 | tf_op jit(solution)/shard_map/ppermute | solution.py:321
  67.6 1.6 %collective-permute-start.28 = (bf16[64,768]{1,0:T(8,128)(2,1)S(1)}, bf16[64,768]{1,0:T(8,128)(2,1)S(1)}, u32[]{:S(2)}, u32[]{:S(2)}) collective-permute-start(bf16[64,768]{1,0:T(8,128)(2,1)S(1)} %add_convert_fusion.3), channel_id=1, source_target_pairs={{0,8},{1,9},{2,10},{3,11},{8,16},{9,17},{10,18},{11,19},{16,24},{1... | collective-permute-start | bytes 294920 | tf_op jit(solution)/shard_map/ppermute | solution.py:321
  70.1 2.1 %collective-permute-done.28 = bf16[64,768]{1,0:T(8,128)(2,1)S(1)} collective-permute-done((bf16[64,768]{1,0:T(8,128)(2,1)S(1)}, bf16[64,768]{1,0:T(8,128)(2,1)S(1)}, u32[]{:S(2)}, u32[]{:S(2)}) %collective-permute-start.28) | collective-permute-done | bytes 98336 | tf_op jit(solution)/shard_map/ppermute | solution.py:321
  74.5 1.5 %collective-permute-start.29 = (bf16[64,768]{1,0:T(8,128)(2,1)S(1)}, bf16[64,768]{1,0:T(8,128)(2,1)S(1)}, u32[]{:S(2)}, u32[]{:S(2)}) collective-permute-start(bf16[64,768]{1,0:T(8,128)(2,1)S(1)} %add_convert_fusion.2), channel_id=1, source_target_pairs={{0,1},{1,0},{2,3},{3,2},{8,9},{9,8},{10,11},{11,10},{16,17},{17,16... | collective-permute-start | bytes 294920 | tf_op jit(solution)/shard_map/ppermute | solution.py:321
  76.0 1.5 %collective-permute-done.22 = bf16[64,768]{1,0:T(8,128)(2,1)S(1)} collective-permute-done((bf16[64,768]{1,0:T(8,128)(2,1)S(1)}, bf16[64,768]{1,0:T(8,128)(2,1)S(1)}, u32[]{:S(2)}, u32[]{:S(2)}) %collective-permute-start.22) | collective-permute-done | bytes 98336 | tf_op jit(solution)/shard_map/ppermute | solution.py:321
  81.5 1.6 %collective-permute-done.23 = bf16[64,768]{1,0:T(8,128)(2,1)S(1)} collective-permute-done((bf16[64,768]{1,0:T(8,128)(2,1)S(1)}, bf16[64,768]{1,0:T(8,128)(2,1)S(1)}, u32[]{:S(2)}, u32[]{:S(2)}) %collective-permute-start.23) | collective-permute-done | bytes 98336 | tf_op jit(solution)/shard_map/ppermute | solution.py:321
  85.4 2.5 %collective-permute-done.24 = bf16[64,768]{1,0:T(8,128)(2,1)S(1)} collective-permute-done((bf16[64,768]{1,0:T(8,128)(2,1)S(1)}, bf16[64,768]{1,0:T(8,128)(2,1)S(1)}, u32[]{:S(2)}, u32[]{:S(2)}) %collective-permute-start.24) | collective-permute-done | bytes 98336 | tf_op jit(solution)/shard_map/ppermute | solution.py:321
  (93 shorter events, 33.1 us)
Async XLA Ops:
  1.6 6.2 %collective-permute-start = (bf16[72,768]{1,0:T(8,128)(2,1)}, bf16[72,768]{1,0:T(8,128)(2,1)S(1)}, u32[]{:S(2)}, u32[]{:S(2)}) collective-permute-start(bf16[72,768]{1,0:T(8,128)(2,1)} %pack.1.refs_4_), channel_id=1, source_target_pairs={{0,8},{1,9},{2,10},{3,11},{8,16},{9,17},{10,18},{11,19},{16,24},{1... | collective-permute-start | bytes 331784 | tf_op jit(solution)/shard_map/ppermute | solution.py:301
  4.7 5.0 %collective-permute-start.3 = (bf16[72,768]{1,0:T(8,128)(2,1)}, bf16[72,768]{1,0:T(8,128)(2,1)S(1)}, u32[]{:S(2)}, u32[]{:S(2)}) collective-permute-start(bf16[72,768]{1,0:T(8,128)(2,1)} %pack.1.refs_4_), channel_id=1, source_target_pairs={{8,0},{9,1},{10,2},{11,3},{16,8},{17,9},{18,10},{19,11},{24,16},{2... | collective-permute-start | bytes 331784 | tf_op jit(solution)/shard_map/ppermute | solution.py:301
  7.9 4.7 %collective-permute-start.1 = (bf16[72,768]{1,0:T(8,128)(2,1)S(1)}, bf16[72,768]{1,0:T(8,128)(2,1)S(1)}, u32[]{:S(2)}, u32[]{:S(2)}) collective-permute-start(bf16[72,768]{1,0:T(8,128)(2,1)S(1)} %collective-permute-done.refs_3_), channel_id=1, source_target_pairs={{0,8},{1,9},{2,10},{3,11},{8,16},{9,17},{10,18},{11,19},{16,24},{1... | collective-permute-start | bytes 331784 | tf_op jit(solution)/shard_map/ppermute | solution.py:301
  9.7 6.7 %collective-permute-start.11 = (bf16[72,768]{1,0:T(8,128)(2,1)S(1)}, bf16[72,768]{1,0:T(8,128)(2,1)S(1)}, u32[]{:S(2)}, u32[]{:S(2)}) collective-permute-start(bf16[72,768]{1,0:T(8,128)(2,1)S(1)} %collective-permute-done.3.refs_5_), channel_id=1, source_target_pairs={{0,1},{1,0},{2,3},{3,2},{8,9},{9,8},{10,11},{11,10},{16,17},{17,16... | collective-permute-start | bytes 331784 | tf_op jit(solution)/shard_map/ppermute | solution.py:301
  12.6 5.8 %collective-permute-start.2 = (bf16[72,768]{1,0:T(8,128)(2,1)S(1)}, bf16[72,768]{1,0:T(8,128)(2,1)S(1)}, u32[]{:S(2)}, u32[]{:S(2)}) collective-permute-start(bf16[72,768]{1,0:T(8,128)(2,1)S(1)} %collective-permute-done.1.refs_2_), channel_id=1, source_target_pairs={{0,8},{1,9},{2,10},{3,11},{8,16},{9,17},{10,18},{11,19},{16,24},{1... | collective-permute-start | bytes 331784 | tf_op jit(solution)/shard_map/ppermute | solution.py:301
  14.5 6.1 %collective-permute-start.10 = (bf16[72,768]{1,0:T(8,128)(2,1)}, bf16[72,768]{1,0:T(8,128)(2,1)S(1)}, u32[]{:S(2)}, u32[]{:S(2)}) collective-permute-start(bf16[72,768]{1,0:T(8,128)(2,1)} %pack.1.refs_4_), channel_id=1, source_target_pairs={{0,1},{1,0},{2,3},{3,2},{8,9},{9,8},{10,11},{11,10},{16,17},{17,16... | collective-permute-start | bytes 331784 | tf_op jit(solution)/shard_map/ppermute | solution.py:301
  16.0 5.9 %collective-permute-start.4 = (bf16[72,768]{1,0:T(8,128)(2,1)S(1)}, bf16[72,768]{1,0:T(8,128)(2,1)S(1)}, u32[]{:S(2)}, u32[]{:S(2)}) collective-permute-start(bf16[72,768]{1,0:T(8,128)(2,1)S(1)} %collective-permute-done.3.refs_5_), channel_id=1, source_target_pairs={{8,0},{9,1},{10,2},{11,3},{16,8},{17,9},{18,10},{19,11},{24,16},{2... | collective-permute-start | bytes 331784 | tf_op jit(solution)/shard_map/ppermute | solution.py:301
  16.4 7.7 %collective-permute-start.12 = (bf16[72,768]{1,0:T(8,128)(2,1)S(1)}, bf16[72,768]{1,0:T(8,128)(2,1)S(1)}, u32[]{:S(2)}, u32[]{:S(2)}) collective-permute-start(bf16[72,768]{1,0:T(8,128)(2,1)S(1)} %collective-permute-done.11.refs_13_), channel_id=1, source_target_pairs={{8,0},{9,1},{10,2},{11,3},{16,8},{17,9},{18,10},{19,11},{24,16},{2... | collective-permute-start | bytes 331784 | tf_op jit(solution)/shard_map/ppermute | solution.py:301
  17.9 6.3 %collective-permute-start.7 = (bf16[72,768]{1,0:T(8,128)(2,1)S(1)}, bf16[72,768]{1,0:T(8,128)(2,1)S(1)}, u32[]{:S(2)}, u32[]{:S(2)}) collective-permute-start(bf16[72,768]{1,0:T(8,128)(2,1)S(1)} %collective-permute-done.1.refs_2_), channel_id=1, source_target_pairs={{0,1},{1,0},{2,3},{3,2},{8,9},{9,8},{10,11},{11,10},{16,17},{17,16... | collective-permute-start | bytes 331784 | tf_op jit(solution)/shard_map/ppermute | solution.py:301
  18.4 7.7 %collective-permute-start.6 = (bf16[72,768]{1,0:T(8,128)(2,1)S(1)}, bf16[72,768]{1,0:T(8,128)(2,1)S(1)}, u32[]{:S(2)}, u32[]{:S(2)}) collective-permute-start(bf16[72,768]{1,0:T(8,128)(2,1)S(1)} %collective-permute-done.2.refs_1_), channel_id=1, source_target_pairs={{0,8},{1,9},{2,10},{3,11},{8,16},{9,17},{10,18},{11,19},{16,24},{1... | collective-permute-start | bytes 331784 | tf_op jit(solution)/shard_map/ppermute | solution.py:301
  20.6 7.3 %collective-permute-start.9 = (bf16[72,768]{1,0:T(8,128)(2,1)S(1)}, bf16[72,768]{1,0:T(8,128)(2,1)S(1)}, u32[]{:S(2)}, u32[]{:S(2)}) collective-permute-start(bf16[72,768]{1,0:T(8,128)(2,1)S(1)} %collective-permute-done.refs_3_), channel_id=1, source_target_pairs={{0,1},{1,0},{2,3},{3,2},{8,9},{9,8},{10,11},{11,10},{16,17},{17,16... | collective-permute-start | bytes 331784 | tf_op jit(solution)/shard_map/ppermute | solution.py:301
  21.9 6.0 %collective-permute-start.5 = (bf16[72,768]{1,0:T(8,128)(2,1)S(1)}, bf16[72,768]{1,0:T(8,128)(2,1)S(1)}, u32[]{:S(2)}, u32[]{:S(2)}) collective-permute-start(bf16[72,768]{1,0:T(8,128)(2,1)S(1)} %collective-permute-done.4.refs_6_), channel_id=1, source_target_pairs={{8,0},{9,1},{10,2},{11,3},{16,8},{17,9},{18,10},{19,11},{24,16},{2... | collective-permute-start | bytes 331784 | tf_op jit(solution)/shard_map/ppermute | solution.py:301
  24.3 4.7 %collective-permute-start.8 = (bf16[72,768]{1,0:T(8,128)(2,1)S(1)}, bf16[72,768]{1,0:T(8,128)(2,1)S(1)}, u32[]{:S(2)}, u32[]{:S(2)}) collective-permute-start(bf16[72,768]{1,0:T(8,128)(2,1)S(1)} %collective-permute-done.7.refs_10_), channel_id=1, source_target_pairs={{0,8},{1,9},{2,10},{3,11},{8,16},{9,17},{10,18},{11,19},{16,24},{1... | collective-permute-start | bytes 331784 | tf_op jit(solution)/shard_map/ppermute | solution.py:301
  26.1 4.7 %collective-permute-start.14 = (bf16[72,768]{1,0:T(8,128)(2,1)S(1)}, bf16[72,768]{1,0:T(8,128)(2,1)S(1)}, u32[]{:S(2)}, u32[]{:S(2)}) collective-permute-start(bf16[72,768]{1,0:T(8,128)(2,1)S(1)} %collective-permute-done.6.refs_8_), channel_id=1, source_target_pairs={{0,1},{1,0},{2,3},{3,2},{8,9},{9,8},{10,11},{11,10},{16,17},{17,16... | collective-permute-start | bytes 331784 | tf_op jit(solution)/shard_map/ppermute | solution.py:301
  53.3 5.7 %collective-permute-start.18 = (bf16[64,768]{1,0:T(8,128)(2,1)}, bf16[64,768]{1,0:T(8,128)(2,1)S(1)}, u32[]{:S(2)}, u32[]{:S(2)}) collective-permute-start(bf16[64,768]{1,0:T(8,128)(2,1)} %get-tuple-element.34), channel_id=1, source_target_pairs={{8,0},{9,1},{10,2},{11,3},{16,8},{17,9},{18,10},{19,11},{24,16},{2... | collective-permute-start | bytes 294920 | tf_op jit(solution)/shard_map/ppermute | solution.py:321
  53.5 28.0 %collective-permute-start.17 = (bf16[64,768]{1,0:T(8,128)(2,1)}, bf16[64,768]{1,0:T(8,128)(2,1)S(1)}, u32[]{:S(2)}, u32[]{:S(2)}) collective-permute-start(bf16[64,768]{1,0:T(8,128)(2,1)} %get-tuple-element.31), channel_id=1, source_target_pairs={{0,1},{1,0},{2,3},{3,2},{8,9},{9,8},{10,11},{11,10},{16,17},{17,16... | collective-permute-start | bytes 294920 | tf_op jit(solution)/shard_map/ppermute | solution.py:321
  53.9 6.7 %collective-permute-start.20 = (bf16[64,768]{1,0:T(8,128)(2,1)}, bf16[64,768]{1,0:T(8,128)(2,1)S(1)}, u32[]{:S(2)}, u32[]{:S(2)}) collective-permute-start(bf16[64,768]{1,0:T(8,128)(2,1)} %get-tuple-element.37), channel_id=1, source_target_pairs={{0,1},{1,0},{2,3},{3,2},{8,9},{9,8},{10,11},{11,10},{16,17},{17,16... | collective-permute-start | bytes 294920 | tf_op jit(solution)/shard_map/ppermute | solution.py:321
  55.5 7.4 %collective-permute-start.25 = (bf16[64,768]{1,0:T(8,128)(2,1)}, bf16[64,768]{1,0:T(8,128)(2,1)S(1)}, u32[]{:S(2)}, u32[]{:S(2)}) collective-permute-start(bf16[64,768]{1,0:T(8,128)(2,1)} %get-tuple-element.40), channel_id=1, source_target_pairs={{0,8},{1,9},{2,10},{3,11},{8,16},{9,17},{10,18},{11,19},{16,24},{1... | collective-permute-start | bytes 294920 | tf_op jit(solution)/shard_map/ppermute | solution.py:321
  57.4 7.9 %collective-permute-start.27 = (bf16[64,768]{1,0:T(8,128)(2,1)}, bf16[64,768]{1,0:T(8,128)(2,1)S(1)}, u32[]{:S(2)}, u32[]{:S(2)}) collective-permute-start(bf16[64,768]{1,0:T(8,128)(2,1)} %get-tuple-element.43), channel_id=1, source_target_pairs={{0,8},{1,9},{2,10},{3,11},{8,16},{9,17},{10,18},{11,19},{16,24},{1... | collective-permute-start | bytes 294920 | tf_op jit(solution)/shard_map/ppermute | solution.py:321
  59.0 25.5 %collective-permute-start.31 = (bf16[64,768]{1,0:T(8,128)(2,1)}, bf16[64,768]{1,0:T(8,128)(2,1)S(1)}, u32[]{:S(2)}, u32[]{:S(2)}) collective-permute-start(bf16[64,768]{1,0:T(8,128)(2,1)} %get-tuple-element.44), channel_id=1, source_target_pairs={{0,1},{1,0},{2,3},{3,2},{8,9},{9,8},{10,11},{11,10},{16,17},{17,16... | collective-permute-start | bytes 294920 | tf_op jit(solution)/shard_map/ppermute | solution.py:321
  60.6 13.9 %collective-permute-start.19 = (bf16[64,768]{1,0:T(8,128)(2,1)S(1)}, bf16[64,768]{1,0:T(8,128)(2,1)S(1)}, u32[]{:S(2)}, u32[]{:S(2)}) collective-permute-start(bf16[64,768]{1,0:T(8,128)(2,1)S(1)} %add_convert_fusion.9), channel_id=1, source_target_pairs={{0,1},{1,0},{2,3},{3,2},{8,9},{9,8},{10,11},{11,10},{16,17},{17,16... | collective-permute-start | bytes 294920 | tf_op jit(solution)/shard_map/ppermute | solution.py:321
  65.3 14.5 %collective-permute-start.26 = (bf16[64,768]{1,0:T(8,128)(2,1)S(1)}, bf16[64,768]{1,0:T(8,128)(2,1)S(1)}, u32[]{:S(2)}, u32[]{:S(2)}) collective-permute-start(bf16[64,768]{1,0:T(8,128)(2,1)S(1)} %add_convert_fusion.4), channel_id=1, source_target_pairs={{0,8},{1,9},{2,10},{3,11},{8,16},{9,17},{10,18},{11,19},{16,24},{1... | collective-permute-start | bytes 294920 | tf_op jit(solution)/shard_map/ppermute | solution.py:321
  72.2 5.3 %collective-permute-start.22 = (bf16[64,768]{1,0:T(8,128)(2,1)S(1)}, bf16[64,768]{1,0:T(8,128)(2,1)S(1)}, u32[]{:S(2)}, u32[]{:S(2)}) collective-permute-start(bf16[64,768]{1,0:T(8,128)(2,1)S(1)} %add_convert_fusion.7), channel_id=1, source_target_pairs={{8,0},{9,1},{10,2},{11,3},{16,8},{17,9},{18,10},{19,11},{24,16},{2... | collective-permute-start | bytes 294920 | tf_op jit(solution)/shard_map/ppermute | solution.py:321
  74.5 5.3 %collective-permute-start.29 = (bf16[64,768]{1,0:T(8,128)(2,1)S(1)}, bf16[64,768]{1,0:T(8,128)(2,1)S(1)}, u32[]{:S(2)}, u32[]{:S(2)}) collective-permute-start(bf16[64,768]{1,0:T(8,128)(2,1)S(1)} %add_convert_fusion.2), channel_id=1, source_target_pairs={{0,1},{1,0},{2,3},{3,2},{8,9},{9,8},{10,11},{11,10},{16,17},{17,16... | collective-permute-start | bytes 294920 | tf_op jit(solution)/shard_map/ppermute | solution.py:321
  (27 other events, 237.3 us)

commit v3 on v2

--- a/solution.py
+++ b/solution.py
@@ -10,6 +10,7 @@
 
 LANES = 128
 SUB = 8
+MIB = 1 << 20
 
 
 class Rings:
@@ -133,6 +134,7 @@
         functools.partial(pack_kernel, experts=experts),
         out_shape=jax.ShapeDtypeStruct((count + SUB, width), jnp.bfloat16),
         name="pack",
+        compiler_params=pltpu.CompilerParams(vmem_limit_bytes=2 * MIB),
     )(ids.T, gates.T, tokens)
 
 
@@ -204,38 +206,26 @@
             jax.ShapeDtypeStruct((2, pairs, LANES), jnp.float32),
         ],
         name="select",
+        compiler_params=pltpu.CompilerParams(vmem_limit_bytes=20 * MIB),
     )(where, *blocks)
 
 
-def expert_kernel(own_ref, came_ref, w_in_ref, w_out_ref, out_ref, w_first, w_second, sem):
-    first_copy = pltpu.make_async_copy(w_in_ref.at[0], w_first, sem.at[0])
-    second_copy = pltpu.make_async_copy(w_out_ref.at[0], w_second, sem.at[1])
-    first_copy.start()
-    second_copy.start()
+def expert_kernel(own_ref, came_ref, w_in_ref, w_out_ref, out_ref):
     rows = own_ref[...] + came_ref[...]
-    first_copy.wait()
-    hidden = jnp.dot(rows, w_first[...], preferred_element_type=jnp.float32)
+    hidden = jnp.dot(rows, w_in_ref[0], preferred_element_type=jnp.float32)
     hidden = jnp.maximum(hidden, 0.0).astype(jnp.bfloat16)
-    second_copy.wait()
-    out_ref[...] = jnp.dot(hidden, w_second[...], preferred_element_type=jnp.float32).astype(
-        jnp.bfloat16
-    )
+    result = jnp.dot(hidden, w_out_ref[0], preferred_element_type=jnp.float32)
+    out_ref[...] = result.astype(jnp.bfloat16)
 
 
 def expert(own, came, w_in, w_out):
-    width, units = w_in.shape[1:]
     vmem = pl.BlockSpec(memory_space=pltpu.VMEM)
-    anywhere = pl.BlockSpec(memory_space=pl.ANY)
     return pl.pallas_call(
         expert_kernel,
-        in_specs=[vmem, vmem, anywhere, anywhere],
+        in_specs=[vmem] * 4,
         out_shape=jax.ShapeDtypeStruct(own.shape, jnp.bfloat16),
-        scratch_shapes=[
-            pltpu.VMEM((width, units), jnp.bfloat16),
-            pltpu.VMEM((units, width), jnp.bfloat16),
-            pltpu.SemaphoreType.DMA((2,)),
-        ],
         name="expert",
+        compiler_params=pltpu.CompilerParams(vmem_limit_bytes=20 * MIB),
     )(own, came, w_in, w_out)
 
 
@@ -271,6 +261,7 @@
         functools.partial(spread_kernel, count=count, cap=cap),
         out_shape=[out] * blocks,
         name="spread",
+        compiler_params=pltpu.CompilerParams(vmem_limit_bytes=20 * MIB),
     )(own, came, seat, gate)
 
 

time: 89.1 us -> 78.8 us (0.88)
  Pallas kernels: 16.4 us -> 6.05 us
  other arithmetic: 8.11 us -> 0.96 us
  waiting for transfers between devices: 24.4 us -> 29.5 us
  local copies, waits for them, and re-layouts: 3.68 us -> 6.28 us
    convert_element_type x10, other arithmetic: 8.11 us -> 0.96 us  [total(): return value.astype(jnp.bfloat16)]
    ppermute x15, waiting for transfers between devices: 9.48 us -> 14.4 us  [on_rings(): value = lax.ppermute(total(block), axes, inverse[channel])]
    pallas_call x1, Pallas kernels: 7.51 us -> 2.72 us  [expert(): pl.pallas_call(expert_kernel, in_specs=[vmem] * 4, out_shape=jax.ShapeDty...]
    unnamed x38 -> x10, local copies, waits for them, and re-layouts: 2.48 us -> 5.59 us
    pallas_call x1, Pallas kernels: 3.18 us -> 1.02 us  [spread(): pl.pallas_call(functools.partial(spread_kernel, count=count, cap=cap), ou...]
    pallas_call x1, Pallas kernels: 4.1 us -> 2.21 us  [select(): pl.pallas_call(functools.partial(select_kernel, blocks=len(blocks), count...]
    pallas_call x1, Pallas kernels: 1.65 us -> 0.09 us  [pack(): pl.pallas_call(functools.partial(pack_kernel, experts=experts), out_shape...]
  transfers between devices with their start and end apart: 32 -> 32, of which waited for: 16 -> 16; matrix products, arithmetic and copies ran while one was open for 10% -> 1% of each run, Pallas kernels for 0% -> 0%
where the time goes in v3:
time: 78.8 us; the launch traced here: 78.5 us
  starting transfers between devices  35.6 us (45%)
  waiting for transfers between devices  29.5 us (37%)
  local copies, waits for them, and re-layouts  6.28 us (8%)
  Pallas kernels  6.05 us (8%)
  other arithmetic  0.96 us (1%)
    ppermute x15, starting transfers between devices, on_rings(): fresh[block] = lax.ppermute(source, axes, rings.perms[channel])  17.7 us
    ppermute x15, starting transfers between devices, on_rings(): value = lax.ppermute(total(block), axes, inverse[channel])  17.7 us
    ppermute x15, waiting for transfers between devices, on_rings(): value = lax.ppermute(total(block), axes, inverse[channel])  14.4 us
    ppermute x15, waiting for transfers between devices, on_rings(): fresh[block] = lax.ppermute(source, axes, rings.perms[channel])  10.6 us
    unnamed x10, local copies, waits for them, and re-layouts  5.59 us
    pallas_call x1, Pallas kernels, expert(): pl.pallas_call(expert_kernel, in_specs=[vmem] * 4, out_shape=jax.ShapeDty...  2.72 us
    ppermute x1, waiting for transfers between devices, on_rings(): came = lax.ppermute(other, axes, rings.partner)  2.27 us
    pallas_call x1, Pallas kernels, select(): pl.pallas_call(functools.partial(select_kernel, blocks=len(blocks), count...  2.21 us
  transfers between devices with their start and end apart: 32, of which 16 were waited for; matrix products, arithmetic and copies ran while one was open for 1% of the time, Pallas kernels for 0%

profile of v3, /device:TPU:0, one launch (start us, length us, event | category | flops | bytes accessed | tf_op | source)
XLA Modules:
  0.0 78.5 jit_solution(17854149096248499857)
XLA Ops:
  2.4 3.1 %collective-permute-start = (bf16[72,768]{1,0:T(8,128)(2,1)S(1)}, bf16[72,768]{1,0:T(8,128)(2,1)S(1)}, u32[]{:S(2)}, u32[]{:S(2)}) collective-permute-start(bf16[72,768]{1,0:T(8,128)(2,1)S(1)} %pack.1.refs_4_), channel_id=1, source_target_pairs={{0,8},{1,9},{2,10},{3,11},{8,16},{9,17},{10,18},{11,19},{16,24},{1... | collective-permute-start | bytes 331784 | tf_op jit(solution)/shard_map/ppermute | solution.py:292
  5.4 3.0 %collective-permute-done.refs_3_ = bf16[72,768]{1,0:T(8,128)(2,1)S(1)} collective-permute-done((bf16[72,768]{1,0:T(8,128)(2,1)S(1)}, bf16[72,768]{1,0:T(8,128)(2,1)S(1)}, u32[]{:S(2)}, u32[]{:S(2)}) %collective-permute-start) | collective-permute-done | bytes 110624 | tf_op jit(solution)/shard_map/ppermute | solution.py:292
  8.4 1.8 %collective-permute-start.1 = (bf16[72,768]{1,0:T(8,128)(2,1)S(1)}, bf16[72,768]{1,0:T(8,128)(2,1)S(1)}, u32[]{:S(2)}, u32[]{:S(2)}) collective-permute-start(bf16[72,768]{1,0:T(8,128)(2,1)S(1)} %collective-permute-done.refs_3_), channel_id=1, source_target_pairs={{0,8},{1,9},{2,10},{3,11},{8,16},{9,17},{10,18},{11,19},{16,24},{1... | collective-permute-start | bytes 331784 | tf_op jit(solution)/shard_map/ppermute | solution.py:292
  13.1 1.8 %collective-permute-start.2 = (bf16[72,768]{1,0:T(8,128)(2,1)S(1)}, bf16[72,768]{1,0:T(8,128)(2,1)S(1)}, u32[]{:S(2)}, u32[]{:S(2)}) collective-permute-start(bf16[72,768]{1,0:T(8,128)(2,1)S(1)} %collective-permute-done.1.refs_2_), channel_id=1, source_target_pairs={{0,8},{1,9},{2,10},{3,11},{8,16},{9,17},{10,18},{11,19},{16,24},{1... | collective-permute-start | bytes 331784 | tf_op jit(solution)/shard_map/ppermute | solution.py:292
  22.9 1.7 %collective-permute-done.12.refs_14_ = bf16[72,768]{1,0:T(8,128)(2,1)S(1)} collective-permute-done((bf16[72,768]{1,0:T(8,128)(2,1)S(1)}, bf16[72,768]{1,0:T(8,128)(2,1)S(1)}, u32[]{:S(2)}, u32[]{:S(2)}) %collective-permute-start.12) | collective-permute-done | bytes 110624 | tf_op jit(solution)/shard_map/ppermute | solution.py:292
  24.8 1.8 %collective-permute-start.8 = (bf16[72,768]{1,0:T(8,128)(2,1)S(1)}, bf16[72,768]{1,0:T(8,128)(2,1)S(1)}, u32[]{:S(2)}, u32[]{:S(2)}) collective-permute-start(bf16[72,768]{1,0:T(8,128)(2,1)S(1)} %collective-permute-done.7.refs_10_), channel_id=1, source_target_pairs={{0,8},{1,9},{2,10},{3,11},{8,16},{9,17},{10,18},{11,19},{16,24},{1... | collective-permute-start | bytes 331784 | tf_op jit(solution)/shard_map/ppermute | solution.py:292
  29.5 1.8 %collective-permute-done.14.refs_16_ = bf16[72,768]{1,0:T(8,128)(2,1)S(1)} collective-permute-done((bf16[72,768]{1,0:T(8,128)(2,1)S(1)}, bf16[72,768]{1,0:T(8,128)(2,1)S(1)}, u32[]{:S(2)}, u32[]{:S(2)}) %collective-permute-start.14) | collective-permute-done | bytes 110624 | tf_op jit(solution)/shard_map/ppermute | solution.py:292
  31.4 2.2 %select.1 = (bf16[512,768]{1,0:T(8,128)(2,1)S(1)}, bf16[512,768]{1,0:T(8,128)(2,1)S(1)}, s32[2,8,128]{2,1,0:T(8,128)S(1)}, f32[2,8,128]{2,1,0:T(8,128)S(1)}) custom-call(s32[5]{0:T(128)S(1)} %dynamic-slice_bitcast_fusion.refs_0_, bf16[72,768]{1,0:T(8,128)(2,1)S(1)} %collective-permute-done.2.refs_1_, bf16[72,768]{1,0:T(8,128)(2,1)S(1)} %collective-permute-done.1.refs_2_, ...), custom_call_target="tpu_custom_call" | custom-call | tf_op jit(solution)/shard_map/select/pallas_call | solution.py:198
  33.7 2.3 %collective-permute-done.15.came_ref = bf16[512,768]{1,0:T(8,128)(2,1)S(1)} collective-permute-done((bf16[512,768]{1,0:T(8,128)(2,1)S(1)}, bf16[512,768]{1,0:T(8,128)(2,1)S(1)}, u32[]{:S(2)}, u32[]{:S(2)}) %collective-permute-start.15) | collective-permute-done | bytes 786464 | tf_op jit(solution)/shard_map/ppermute | solution.py:297
  35.9 1.7 %copy-done = bf16[1,768,1536]{2,1,0:T(8,128)(2,1)S(1)} copy-done((bf16[1,768,1536]{2,1,0:T(8,128)(2,1)S(1)}, bf16[1,768,1536]{2,1,0:T(8,128)(2,1)}, u32[]{:S(2)}) %copy-start) | copy-done | bytes 2359320
  37.6 1.7 %copy-done.1 = bf16[1,1536,768]{2,1,0:T(8,128)(2,1)S(1)} copy-done((bf16[1,1536,768]{2,1,0:T(8,128)(2,1)S(1)}, bf16[1,1536,768]{2,1,0:T(8,128)(2,1)}, u32[]{:S(2)}) %copy-start.1) | copy-done | bytes 2359320
  39.3 2.7 %expert.1.own_ref = bf16[512,768]{1,0:T(8,128)(2,1)S(1)} custom-call(bf16[512,768]{1,0:T(8,128)(2,1)S(1)} %get-tuple-element.25.own_ref, bf16[512,768]{1,0:T(8,128)(2,1)S(1)} %collective-permute-done.15.came_ref, bf16[1,768,1536]{2,1,0:T(8,128)(2,1)S(1)} %copy-done, bf16[1,1536,768]{2,1,0:T(8,128)(2,1)S(1)} %copy-done.1), custom_call_target="tpu_custom_call" | custom-call | tf_op jit(solution)/shard_map/expert/pallas_call | solution.py:223
  42.2 2.1 %collective-permute-done.16.came_ref = bf16[512,768]{1,0:T(8,128)(2,1)S(1)} collective-permute-done((bf16[512,768]{1,0:T(8,128)(2,1)S(1)}, bf16[512,768]{1,0:T(8,128)(2,1)S(1)}, u32[]{:S(2)}, u32[]{:S(2)}) %collective-permute-start.16) | collective-permute-done | bytes 786464 | tf_op jit(solution)/shard_map/ppermute | solution.py:299
  46.0 1.6 %collective-permute-start.20 = (bf16[64,768]{1,0:T(8,128)(2,1)S(1)}, bf16[64,768]{1,0:T(8,128)(2,1)S(1)}, u32[]{:S(2)}, u32[]{:S(2)}) collective-permute-start(bf16[64,768]{1,0:T(8,128)(2,1)S(1)} %get-tuple-element.37), channel_id=1, source_target_pairs={{0,1},{1,0},{2,3},{3,2},{8,9},{9,8},{10,11},{11,10},{16,17},{17,16... | collective-permute-start | bytes 294920 | tf_op jit(solution)/shard_map/ppermute | solution.py:312
  47.6 1.8 %collective-permute-start.25 = (bf16[64,768]{1,0:T(8,128)(2,1)S(1)}, bf16[64,768]{1,0:T(8,128)(2,1)S(1)}, u32[]{:S(2)}, u32[]{:S(2)}) collective-permute-start(bf16[64,768]{1,0:T(8,128)(2,1)S(1)} %get-tuple-element.40), channel_id=1, source_target_pairs={{0,8},{1,9},{2,10},{3,11},{8,16},{9,17},{10,18},{11,19},{16,24},{1... | collective-permute-start | bytes 294920 | tf_op jit(solution)/shard_map/ppermute | solution.py:312
  49.5 1.6 %collective-permute-start.27 = (bf16[64,768]{1,0:T(8,128)(2,1)S(1)}, bf16[64,768]{1,0:T(8,128)(2,1)S(1)}, u32[]{:S(2)}, u32[]{:S(2)}) collective-permute-start(bf16[64,768]{1,0:T(8,128)(2,1)S(1)} %get-tuple-element.43), channel_id=1, source_target_pairs={{0,8},{1,9},{2,10},{3,11},{8,16},{9,17},{10,18},{11,19},{16,24},{1... | collective-permute-start | bytes 294920 | tf_op jit(solution)/shard_map/ppermute | solution.py:312
  53.2 2.0 %collective-permute-start.21 = (bf16[64,768]{1,0:T(8,128)(2,1)S(1)}, bf16[64,768]{1,0:T(8,128)(2,1)S(1)}, u32[]{:S(2)}, u32[]{:S(2)}) collective-permute-start(bf16[64,768]{1,0:T(8,128)(2,1)S(1)} %add_convert_fusion.8), channel_id=1, source_target_pairs={{8,0},{9,1},{10,2},{11,3},{16,8},{17,9},{18,10},{19,11},{24,16},{2... | collective-permute-start | bytes 294920 | tf_op jit(solution)/shard_map/ppermute | solution.py:312
  55.9 2.0 %collective-permute-done.21 = bf16[64,768]{1,0:T(8,128)(2,1)S(1)} collective-permute-done((bf16[64,768]{1,0:T(8,128)(2,1)S(1)}, bf16[64,768]{1,0:T(8,128)(2,1)S(1)}, u32[]{:S(2)}, u32[]{:S(2)}) %collective-permute-start.21) | collective-permute-done | bytes 98336 | tf_op jit(solution)/shard_map/ppermute | solution.py:312
  57.9 1.6 %collective-permute-start.28 = (bf16[64,768]{1,0:T(8,128)(2,1)S(1)}, bf16[64,768]{1,0:T(8,128)(2,1)S(1)}, u32[]{:S(2)}, u32[]{:S(2)}) collective-permute-start(bf16[64,768]{1,0:T(8,128)(2,1)S(1)} %add_convert_fusion.3), channel_id=1, source_target_pairs={{0,8},{1,9},{2,10},{3,11},{8,16},{9,17},{10,18},{11,19},{16,24},{1... | collective-permute-start | bytes 294920 | tf_op jit(solution)/shard_map/ppermute | solution.py:312
  59.6 3.0 %collective-permute-done.28 = bf16[64,768]{1,0:T(8,128)(2,1)S(1)} collective-permute-done((bf16[64,768]{1,0:T(8,128)(2,1)S(1)}, bf16[64,768]{1,0:T(8,128)(2,1)S(1)}, u32[]{:S(2)}, u32[]{:S(2)}) %collective-permute-start.28) | collective-permute-done | bytes 98336 | tf_op jit(solution)/shard_map/ppermute | solution.py:312
  62.5 1.9 %collective-permute-start.22 = (bf16[64,768]{1,0:T(8,128)(2,1)S(1)}, bf16[64,768]{1,0:T(8,128)(2,1)S(1)}, u32[]{:S(2)}, u32[]{:S(2)}) collective-permute-start(bf16[64,768]{1,0:T(8,128)(2,1)S(1)} %add_convert_fusion.7), channel_id=1, source_target_pairs={{8,0},{9,1},{10,2},{11,3},{16,8},{17,9},{18,10},{19,11},{24,16},{2... | collective-permute-start | bytes 294920 | tf_op jit(solution)/shard_map/ppermute | solution.py:312
  66.0 1.9 %collective-permute-done.22 = bf16[64,768]{1,0:T(8,128)(2,1)S(1)} collective-permute-done((bf16[64,768]{1,0:T(8,128)(2,1)S(1)}, bf16[64,768]{1,0:T(8,128)(2,1)S(1)}, u32[]{:S(2)}, u32[]{:S(2)}) %collective-permute-start.22) | collective-permute-done | bytes 98336 | tf_op jit(solution)/shard_map/ppermute | solution.py:312
  70.2 2.9 %collective-permute-done.23 = bf16[64,768]{1,0:T(8,128)(2,1)S(1)} collective-permute-done((bf16[64,768]{1,0:T(8,128)(2,1)S(1)}, bf16[64,768]{1,0:T(8,128)(2,1)S(1)}, u32[]{:S(2)}, u32[]{:S(2)}) %collective-permute-start.23) | collective-permute-done | bytes 98336 | tf_op jit(solution)/shard_map/ppermute | solution.py:312
  74.2 3.6 %collective-permute-done.24 = bf16[64,768]{1,0:T(8,128)(2,1)S(1)} collective-permute-done((bf16[64,768]{1,0:T(8,128)(2,1)S(1)}, bf16[64,768]{1,0:T(8,128)(2,1)S(1)}, u32[]{:S(2)}, u32[]{:S(2)}) %collective-permute-start.24) | collective-permute-done | bytes 98336 | tf_op jit(solution)/shard_map/ppermute | solution.py:312
  (65 shorter events, 26.5 us)
Async XLA Ops:
  2.4 6.0 %collective-permute-start = (bf16[72,768]{1,0:T(8,128)(2,1)S(1)}, bf16[72,768]{1,0:T(8,128)(2,1)S(1)}, u32[]{:S(2)}, u32[]{:S(2)}) collective-permute-start(bf16[72,768]{1,0:T(8,128)(2,1)S(1)} %pack.1.refs_4_), channel_id=1, source_target_pairs={{0,8},{1,9},{2,10},{3,11},{8,16},{9,17},{10,18},{11,19},{16,24},{1... | collective-permute-start | bytes 331784 | tf_op jit(solution)/shard_map/ppermute | solution.py:292
  5.4 4.8 %collective-permute-start.3 = (bf16[72,768]{1,0:T(8,128)(2,1)S(1)}, bf16[72,768]{1,0:T(8,128)(2,1)S(1)}, u32[]{:S(2)}, u32[]{:S(2)}) collective-permute-start(bf16[72,768]{1,0:T(8,128)(2,1)S(1)} %pack.1.refs_4_), channel_id=1, source_target_pairs={{8,0},{9,1},{10,2},{11,3},{16,8},{17,9},{18,10},{19,11},{24,16},{2... | collective-permute-start | bytes 331784 | tf_op jit(solution)/shard_map/ppermute | solution.py:292
  10.2 6.7 %collective-permute-start.11 = (bf16[72,768]{1,0:T(8,128)(2,1)S(1)}, bf16[72,768]{1,0:T(8,128)(2,1)S(1)}, u32[]{:S(2)}, u32[]{:S(2)}) collective-permute-start(bf16[72,768]{1,0:T(8,128)(2,1)S(1)} %collective-permute-done.3.refs_5_), channel_id=1, source_target_pairs={{0,1},{1,0},{2,3},{3,2},{8,9},{9,8},{10,11},{11,10},{16,17},{17,16... | collective-permute-start | bytes 331784 | tf_op jit(solution)/shard_map/ppermute | solution.py:292
  13.1 5.8 %collective-permute-start.2 = (bf16[72,768]{1,0:T(8,128)(2,1)S(1)}, bf16[72,768]{1,0:T(8,128)(2,1)S(1)}, u32[]{:S(2)}, u32[]{:S(2)}) collective-permute-start(bf16[72,768]{1,0:T(8,128)(2,1)S(1)} %collective-permute-done.1.refs_2_), channel_id=1, source_target_pairs={{0,8},{1,9},{2,10},{3,11},{8,16},{9,17},{10,18},{11,19},{16,24},{1... | collective-permute-start | bytes 331784 | tf_op jit(solution)/shard_map/ppermute | solution.py:292
  15.0 5.9 %collective-permute-start.10 = (bf16[72,768]{1,0:T(8,128)(2,1)S(1)}, bf16[72,768]{1,0:T(8,128)(2,1)S(1)}, u32[]{:S(2)}, u32[]{:S(2)}) collective-permute-start(bf16[72,768]{1,0:T(8,128)(2,1)S(1)} %pack.1.refs_4_), channel_id=1, source_target_pairs={{0,1},{1,0},{2,3},{3,2},{8,9},{9,8},{10,11},{11,10},{16,17},{17,16... | collective-permute-start | bytes 331784 | tf_op jit(solution)/shard_map/ppermute | solution.py:292
  16.5 5.7 %collective-permute-start.4 = (bf16[72,768]{1,0:T(8,128)(2,1)S(1)}, bf16[72,768]{1,0:T(8,128)(2,1)S(1)}, u32[]{:S(2)}, u32[]{:S(2)}) collective-permute-start(bf16[72,768]{1,0:T(8,128)(2,1)S(1)} %collective-permute-done.3.refs_5_), channel_id=1, source_target_pairs={{8,0},{9,1},{10,2},{11,3},{16,8},{17,9},{18,10},{19,11},{24,16},{2... | collective-permute-start | bytes 331784 | tf_op jit(solution)/shard_map/ppermute | solution.py:292
  16.9 7.7 %collective-permute-start.12 = (bf16[72,768]{1,0:T(8,128)(2,1)S(1)}, bf16[72,768]{1,0:T(8,128)(2,1)S(1)}, u32[]{:S(2)}, u32[]{:S(2)}) collective-permute-start(bf16[72,768]{1,0:T(8,128)(2,1)S(1)} %collective-permute-done.11.refs_13_), channel_id=1, source_target_pairs={{8,0},{9,1},{10,2},{11,3},{16,8},{17,9},{18,10},{19,11},{24,16},{2... | collective-permute-start | bytes 331784 | tf_op jit(solution)/shard_map/ppermute | solution.py:292
  18.4 6.4 %collective-permute-start.7 = (bf16[72,768]{1,0:T(8,128)(2,1)S(1)}, bf16[72,768]{1,0:T(8,128)(2,1)S(1)}, u32[]{:S(2)}, u32[]{:S(2)}) collective-permute-start(bf16[72,768]{1,0:T(8,128)(2,1)S(1)} %collective-permute-done.1.refs_2_), channel_id=1, source_target_pairs={{0,1},{1,0},{2,3},{3,2},{8,9},{9,8},{10,11},{11,10},{16,17},{17,16... | collective-permute-start | bytes 331784 | tf_op jit(solution)/shard_map/ppermute | solution.py:292
  18.9 7.7 %collective-permute-start.6 = (bf16[72,768]{1,0:T(8,128)(2,1)S(1)}, bf16[72,768]{1,0:T(8,128)(2,1)S(1)}, u32[]{:S(2)}, u32[]{:S(2)}) collective-permute-start(bf16[72,768]{1,0:T(8,128)(2,1)S(1)} %collective-permute-done.2.refs_1_), channel_id=1, source_target_pairs={{0,8},{1,9},{2,10},{3,11},{8,16},{9,17},{10,18},{11,19},{16,24},{1... | collective-permute-start | bytes 331784 | tf_op jit(solution)/shard_map/ppermute | solution.py:292
  20.9 7.0 %collective-permute-start.9 = (bf16[72,768]{1,0:T(8,128)(2,1)S(1)}, bf16[72,768]{1,0:T(8,128)(2,1)S(1)}, u32[]{:S(2)}, u32[]{:S(2)}) collective-permute-start(bf16[72,768]{1,0:T(8,128)(2,1)S(1)} %collective-permute-done.refs_3_), channel_id=1, source_target_pairs={{0,1},{1,0},{2,3},{3,2},{8,9},{9,8},{10,11},{11,10},{16,17},{17,16... | collective-permute-start | bytes 331784 | tf_op jit(solution)/shard_map/ppermute | solution.py:292
  22.2 5.6 %collective-permute-start.5 = (bf16[72,768]{1,0:T(8,128)(2,1)S(1)}, bf16[72,768]{1,0:T(8,128)(2,1)S(1)}, u32[]{:S(2)}, u32[]{:S(2)}) collective-permute-start(bf16[72,768]{1,0:T(8,128)(2,1)S(1)} %collective-permute-done.4.refs_6_), channel_id=1, source_target_pairs={{8,0},{9,1},{10,2},{11,3},{16,8},{17,9},{18,10},{19,11},{24,16},{2... | collective-permute-start | bytes 331784 | tf_op jit(solution)/shard_map/ppermute | solution.py:292
  24.8 4.7 %collective-permute-start.8 = (bf16[72,768]{1,0:T(8,128)(2,1)S(1)}, bf16[72,768]{1,0:T(8,128)(2,1)S(1)}, u32[]{:S(2)}, u32[]{:S(2)}) collective-permute-start(bf16[72,768]{1,0:T(8,128)(2,1)S(1)} %collective-permute-done.7.refs_10_), channel_id=1, source_target_pairs={{0,8},{1,9},{2,10},{3,11},{8,16},{9,17},{10,18},{11,19},{16,24},{1... | collective-permute-start | bytes 331784 | tf_op jit(solution)/shard_map/ppermute | solution.py:292
  26.6 4.7 %collective-permute-start.14 = (bf16[72,768]{1,0:T(8,128)(2,1)S(1)}, bf16[72,768]{1,0:T(8,128)(2,1)S(1)}, u32[]{:S(2)}, u32[]{:S(2)}) collective-permute-start(bf16[72,768]{1,0:T(8,128)(2,1)S(1)} %collective-permute-done.6.refs_8_), channel_id=1, source_target_pairs={{0,1},{1,0},{2,3},{3,2},{8,9},{9,8},{10,11},{11,10},{16,17},{17,16... | collective-permute-start | bytes 331784 | tf_op jit(solution)/shard_map/ppermute | solution.py:292
  45.4 5.7 %collective-permute-start.18 = (bf16[64,768]{1,0:T(8,128)(2,1)S(1)}, bf16[64,768]{1,0:T(8,128)(2,1)S(1)}, u32[]{:S(2)}, u32[]{:S(2)}) collective-permute-start(bf16[64,768]{1,0:T(8,128)(2,1)S(1)} %get-tuple-element.34), channel_id=1, source_target_pairs={{8,0},{9,1},{10,2},{11,3},{16,8},{17,9},{18,10},{19,11},{24,16},{2... | collective-permute-start | bytes 294920 | tf_op jit(solution)/shard_map/ppermute | solution.py:312
  45.6 24.5 %collective-permute-start.17 = (bf16[64,768]{1,0:T(8,128)(2,1)S(1)}, bf16[64,768]{1,0:T(8,128)(2,1)S(1)}, u32[]{:S(2)}, u32[]{:S(2)}) collective-permute-start(bf16[64,768]{1,0:T(8,128)(2,1)S(1)} %get-tuple-element.31), channel_id=1, source_target_pairs={{0,1},{1,0},{2,3},{3,2},{8,9},{9,8},{10,11},{11,10},{16,17},{17,16... | collective-permute-start | bytes 294920 | tf_op jit(solution)/shard_map/ppermute | solution.py:312
  46.0 6.5 %collective-permute-start.20 = (bf16[64,768]{1,0:T(8,128)(2,1)S(1)}, bf16[64,768]{1,0:T(8,128)(2,1)S(1)}, u32[]{:S(2)}, u32[]{:S(2)}) collective-permute-start(bf16[64,768]{1,0:T(8,128)(2,1)S(1)} %get-tuple-element.37), channel_id=1, source_target_pairs={{0,1},{1,0},{2,3},{3,2},{8,9},{9,8},{10,11},{11,10},{16,17},{17,16... | collective-permute-start | bytes 294920 | tf_op jit(solution)/shard_map/ppermute | solution.py:312
  47.6 5.6 %collective-permute-start.25 = (bf16[64,768]{1,0:T(8,128)(2,1)S(1)}, bf16[64,768]{1,0:T(8,128)(2,1)S(1)}, u32[]{:S(2)}, u32[]{:S(2)}) collective-permute-start(bf16[64,768]{1,0:T(8,128)(2,1)S(1)} %get-tuple-element.40), channel_id=1, source_target_pairs={{0,8},{1,9},{2,10},{3,11},{8,16},{9,17},{10,18},{11,19},{16,24},{1... | collective-permute-start | bytes 294920 | tf_op jit(solution)/shard_map/ppermute | solution.py:312
  49.5 5.8 %collective-permute-start.27 = (bf16[64,768]{1,0:T(8,128)(2,1)S(1)}, bf16[64,768]{1,0:T(8,128)(2,1)S(1)}, u32[]{:S(2)}, u32[]{:S(2)}) collective-permute-start(bf16[64,768]{1,0:T(8,128)(2,1)S(1)} %get-tuple-element.43), channel_id=1, source_target_pairs={{0,8},{1,9},{2,10},{3,11},{8,16},{9,17},{10,18},{11,19},{16,24},{1... | collective-permute-start | bytes 294920 | tf_op jit(solution)/shard_map/ppermute | solution.py:312
  51.1 23.1 %collective-permute-start.31 = (bf16[64,768]{1,0:T(8,128)(2,1)S(1)}, bf16[64,768]{1,0:T(8,128)(2,1)S(1)}, u32[]{:S(2)}, u32[]{:S(2)}) collective-permute-start(bf16[64,768]{1,0:T(8,128)(2,1)S(1)} %get-tuple-element.44), channel_id=1, source_target_pairs={{0,1},{1,0},{2,3},{3,2},{8,9},{9,8},{10,11},{11,10},{16,17},{17,16... | collective-permute-start | bytes 294920 | tf_op jit(solution)/shard_map/ppermute | solution.py:312
  52.5 12.0 %collective-permute-start.19 = (bf16[64,768]{1,0:T(8,128)(2,1)S(1)}, bf16[64,768]{1,0:T(8,128)(2,1)S(1)}, u32[]{:S(2)}, u32[]{:S(2)}) collective-permute-start(bf16[64,768]{1,0:T(8,128)(2,1)S(1)} %add_convert_fusion.9), channel_id=1, source_target_pairs={{0,1},{1,0},{2,3},{3,2},{8,9},{9,8},{10,11},{11,10},{16,17},{17,16... | collective-permute-start | bytes 294920 | tf_op jit(solution)/shard_map/ppermute | solution.py:312
  55.3 14.2 %collective-permute-start.26 = (bf16[64,768]{1,0:T(8,128)(2,1)S(1)}, bf16[64,768]{1,0:T(8,128)(2,1)S(1)}, u32[]{:S(2)}, u32[]{:S(2)}) collective-permute-start(bf16[64,768]{1,0:T(8,128)(2,1)S(1)} %add_convert_fusion.4), channel_id=1, source_target_pairs={{0,8},{1,9},{2,10},{3,11},{8,16},{9,17},{10,18},{11,19},{16,24},{1... | collective-permute-start | bytes 294920 | tf_op jit(solution)/shard_map/ppermute | solution.py:312
  62.5 5.4 %collective-permute-start.22 = (bf16[64,768]{1,0:T(8,128)(2,1)S(1)}, bf16[64,768]{1,0:T(8,128)(2,1)S(1)}, u32[]{:S(2)}, u32[]{:S(2)}) collective-permute-start(bf16[64,768]{1,0:T(8,128)(2,1)S(1)} %add_convert_fusion.7), channel_id=1, source_target_pairs={{8,0},{9,1},{10,2},{11,3},{16,8},{17,9},{18,10},{19,11},{24,16},{2... | collective-permute-start | bytes 294920 | tf_op jit(solution)/shard_map/ppermute | solution.py:312
  64.5 5.0 %collective-permute-start.29 = (bf16[64,768]{1,0:T(8,128)(2,1)S(1)}, bf16[64,768]{1,0:T(8,128)(2,1)S(1)}, u32[]{:S(2)}, u32[]{:S(2)}) collective-permute-start(bf16[64,768]{1,0:T(8,128)(2,1)S(1)} %add_convert_fusion.2), channel_id=1, source_target_pairs={{0,1},{1,0},{2,3},{3,2},{8,9},{9,8},{10,11},{11,10},{16,17},{17,16... | collective-permute-start | bytes 294920 | tf_op jit(solution)/shard_map/ppermute | solution.py:312
  68.0 5.1 %collective-permute-start.23 = (bf16[64,768]{1,0:T(8,128)(2,1)S(1)}, bf16[64,768]{1,0:T(8,128)(2,1)S(1)}, u32[]{:S(2)}, u32[]{:S(2)}) collective-permute-start(bf16[64,768]{1,0:T(8,128)(2,1)S(1)} %add_convert_fusion.6), channel_id=1, source_target_pairs={{8,0},{9,1},{10,2},{11,3},{16,8},{17,9},{18,10},{19,11},{24,16},{2... | collective-permute-start | bytes 294920 | tf_op jit(solution)/shard_map/ppermute | solution.py:312
  (13 other events, 38.4 us)

commit v4 on v3

--- a/solution.py
+++ b/solution.py
@@ -2,25 +2,22 @@
 
 import jax
 import jax.numpy as jnp
-import numpy as np
 from jax import lax
 from jax.experimental import pallas as pl
 from jax.experimental.pallas import tpu as pltpu
 from jax.sharding import PartitionSpec as P
 
+
 LANES = 128
 SUB = 8
 MIB = 1 << 20
 
 
 class Rings:
-    def __init__(self, length, rounds, clockwise, counter, mirror, partner, cores):
+    def __init__(self, length, clockwise, counter, mirror, partner):
         self.length = length
-        self.rounds = rounds
         self.perms = (clockwise, counter, mirror)
         self.partner = partner
-        self.mates = [mate for _, mate in sorted(partner)]
-        self.cores = cores
 
 
 def wrap(step, length):
@@ -37,25 +34,44 @@
     return (step, 1 - plane)
 
 
-def gather_rounds(length):
-    everything = [(wrap(s, length), p) for p in range(2) for s in range(length)]
-    everything.sort(key=lambda b: (b[1], abs(b[0]), -b[0]))
-    held = {(0, 0)}
-    rounds = []
-    while len(held) < len(everything):
-        chosen = {}
-        for channel in range(3):
-            for block in everything:
-                if block in held or block in chosen.values():
-                    continue
-                if channel == 2 and block[1] == 0:
-                    continue
-                if seen_from_source(channel, block, length) in held:
-                    chosen[channel] = block
-                    break
-        rounds.append(chosen)
-        held |= set(chosen.values())
-    return rounds
+def gather_sequence():
+    return (
+        (0, (-1, 0)),
+        (1, (1, 0)),
+        (2, (0, 1)),
+        (0, (-2, 0)),
+        (1, (2, 0)),
+        (2, (1, 1)),
+        (0, (-3, 0)),
+        (1, (3, 0)),
+        (2, (-2, 1)),
+        (0, (4, 0)),
+        (1, (2, 1)),
+        (2, (-1, 1)),
+        (0, (-3, 1)),
+        (1, (3, 1)),
+        (2, (4, 1)),
+    )
+
+
+def return_sequence():
+    return (
+        (2, (4, 1)),
+        (0, (-3, 1)),
+        (1, (3, 1)),
+        (2, (-1, 1)),
+        (0, (4, 0)),
+        (1, (2, 1)),
+        (2, (-2, 1)),
+        (0, (-3, 0)),
+        (1, (3, 0)),
+        (2, (1, 1)),
+        (0, (-2, 0)),
+        (1, (2, 0)),
+        (2, (0, 1)),
+        (0, (-1, 0)),
+        (1, (1, 0)),
+    )
 
 
 def find_rings(mesh):
@@ -84,6 +100,8 @@
     down = sorted((c for c in planes[0] if c[side] != low), key=lambda c: -c[along])
     order = up + down
     length = len(order)
+    if length != 8:
+        return None
 
     def index(chip, core):
         g, d = place[(chip, core)]
@@ -108,34 +126,51 @@
                 partner.append((a, index(turn(order[here]), 1 - core)))
             a, b = index(order[here], core), index(mirrored(order[here]), core)
             mirror += [(a, b), (b, a)]
-    cores = [device.core_on_chip for device in grid.flat]
-    return Rings(length, gather_rounds(length), clockwise, counter, mirror, partner, cores)
-
-
-def pack_kernel(ids_ref, gates_ref, tokens_ref, out_ref, *, experts):
-    count, width = tokens_ref.shape
+    if any(mate != one ^ n_dev for one, mate in partner):
+        return None
+    return Rings(length, clockwise, counter, mirror, partner)
+
+
+def pack_kernel(ids_hbm, gates_hbm, tokens_hbm, out_ref, ids_ref, gates_ref, sem, *, experts):
+    count, width = tokens_hbm.shape
     picks = ids_ref.shape[0]
-    out_ref[:count, :] = tokens_ref[...]
+    copies = [
+        pltpu.make_async_copy(tokens_hbm, out_ref.at[pl.ds(0, count)], sem.at[0]),
+        pltpu.make_async_copy(ids_hbm, ids_ref, sem.at[1]),
+        pltpu.make_async_copy(gates_hbm, gates_ref, sem.at[2]),
+    ]
+    for copy in copies:
+        copy.start()
+    row = lax.broadcasted_iota(jnp.int32, (experts, count), 0)
+    table = jnp.zeros((experts, count), jnp.float32)
+    copies[1].wait()
+    copies[2].wait()
     ids = ids_ref[...]
     gates = gates_ref[...].astype(jnp.float32)
-    row = lax.broadcasted_iota(jnp.int32, (experts, count), 0)
-    table = jnp.zeros((experts, count), jnp.float32)
     for k in range(picks):
         table += jnp.where(ids[k : k + 1, :] == row, gates[k : k + 1, :], 0.0)
     twice = jnp.concatenate([table, table], axis=1).astype(jnp.bfloat16)
     out_ref[count:, :] = jnp.zeros((SUB, width), jnp.bfloat16)
     for q in range(experts // SUB):
         out_ref[count:, q * LANES : (q + 1) * LANES] = twice[q * SUB : (q + 1) * SUB, :]
+    copies[0].wait()
 
 
 def pack(ids, gates, tokens, experts):
     count, width = tokens.shape
+    picks = ids.shape[1]
     return pl.pallas_call(
         functools.partial(pack_kernel, experts=experts),
+        in_specs=[pl.BlockSpec(memory_space=pltpu.HBM)] * 3,
         out_shape=jax.ShapeDtypeStruct((count + SUB, width), jnp.bfloat16),
+        scratch_shapes=[
+            pltpu.VMEM((picks, count), jnp.int32),
+            pltpu.VMEM((picks, count), jnp.bfloat16),
+            pltpu.SemaphoreType.DMA((3,)),
+        ],
         name="pack",
         compiler_params=pltpu.CompilerParams(vmem_limit_bytes=2 * MIB),
-    )(ids.T, gates.T, tokens)
+    )(*(pltpu.with_memory_space_constraint(x, pltpu.HBM) for x in (ids.T, gates.T, tokens)))
 
 
 def one_hot(seat, cap):
@@ -143,32 +178,31 @@
     return jnp.where(seats == seat, 1.0, 0.0)
 
 
-def select_kernel(*refs, blocks, count, cap):
-    where_ref = refs[0]
-    block_refs = refs[1 : 1 + blocks]
-    own_ref, other_ref, seat_ref, gate_ref = refs[1 + blocks : 5 + blocks]
+def select_kernel(*refs, blocks, count, cap, stride):
+    here = lax.axis_index("grp") * stride + lax.axis_index("dev")
+    mate = here ^ stride
+    block_refs = refs[:blocks]
+    own_ref, other_ref, seat_ref, gate_ref = refs[-4:]
     pairs = blocks // 2
-    half = pairs // 2
     dot = functools.partial(jnp.dot, preferred_element_type=jnp.float32)
     tails = jnp.concatenate([r[count:, :] for r in block_refs], axis=0)
     upper = (
         lax.broadcasted_iota(jnp.int32, (LANES, LANES), 0)
         < lax.broadcasted_iota(jnp.int32, (LANES, LANES), 1)
     ).astype(jnp.bfloat16)
-    left = lax.broadcasted_iota(jnp.int32, (pairs, pairs), 0)
-    right = lax.broadcasted_iota(jnp.int32, (pairs, pairs), 1)
-    before = ((right < left) & (right // half == left // half)).astype(jnp.bfloat16)
+    before = (
+        lax.broadcasted_iota(jnp.int32, (pairs, pairs), 1)
+        < lax.broadcasted_iota(jnp.int32, (pairs, pairs), 0)
+    ).astype(jnp.bfloat16)
     lane = lax.broadcasted_iota(jnp.int32, (pairs, LANES), 1)
     row_of = lax.broadcasted_iota(jnp.int32, (pairs, blocks * SUB), 0)
     col_of = lax.broadcasted_iota(jnp.int32, (pairs, blocks * SUB), 1)
     groups = tails.shape[1] // LANES
-    rows = [
-        jnp.concatenate([r[:count, :] for r in block_refs[p * pairs : (p + 1) * pairs]], axis=0)
-        for p in range(2)
-    ]
+    rows = jnp.concatenate([r[:count, :] for r in block_refs], axis=0)
     for k, out_ref in enumerate((own_ref, other_ref)):
-        sub = where_ref[2 * k]
-        group = where_ref[2 * k + 1]
+        expert = (here, mate)[k]
+        sub = expert % SUB
+        group = expert // SUB
         table = tails[:, :LANES]
         for q in range(1, groups):
             table = jnp.where(group == q, tails[:, q * LANES : (q + 1) * LANES], table)
@@ -177,28 +211,25 @@
         gate = jnp.where(lane < count, dot(pick_a, table), dot(pick_b, table))
         chosen = gate > 0.0
         ones = jnp.where(chosen, 1.0, 0.0)
+        inside = dot(ones.astype(jnp.bfloat16), upper)
         total = jnp.broadcast_to(jnp.sum(ones, axis=1, keepdims=True), (pairs, LANES))
-        spot = dot(ones.astype(jnp.bfloat16), upper) + dot(before, total.astype(jnp.bfloat16))
-        spot = spot.astype(jnp.int32)
-        seat = jnp.where(where_ref[4] == 0, spot, cap - 1 - spot)
+        spot = (inside + dot(before, total.astype(jnp.bfloat16))).astype(jnp.int32)
+        seat = jnp.where(here < mate, spot, cap - 1 - spot)
         seat = jnp.where(chosen, seat, -1)
         seat_ref[k] = seat
         gate_ref[k] = gate
-        for p in range(2):
-            hot = jnp.concatenate(
-                [one_hot(seat[o : o + 1, :], cap) for o in range(p * half, (p + 1) * half)], axis=1
-            ).astype(jnp.bfloat16)
-            out_ref[p * cap : (p + 1) * cap, :] = dot(hot, rows[p]).astype(jnp.bfloat16)
-
-
-def select(where, blocks, count, cap):
+        hot = jnp.concatenate([one_hot(seat[o : o + 1, :], cap) for o in range(pairs)], axis=1)
+        out_ref[...] = dot(hot.astype(jnp.bfloat16), rows).astype(jnp.bfloat16)
+
+
+def select(blocks, count, cap, stride):
     width = blocks[0].shape[1]
     pairs = len(blocks) // 2
-    taken = jax.ShapeDtypeStruct((2 * cap, width), jnp.bfloat16)
+    taken = jax.ShapeDtypeStruct((cap, width), jnp.bfloat16)
+    vmem = pl.BlockSpec(memory_space=pltpu.VMEM)
     return pl.pallas_call(
-        functools.partial(select_kernel, blocks=len(blocks), count=count, cap=cap),
-        in_specs=[pl.BlockSpec(memory_space=pltpu.SMEM)]
-        + [pl.BlockSpec(memory_space=pltpu.VMEM)] * len(blocks),
+        functools.partial(select_kernel, blocks=len(blocks), count=count, cap=cap, stride=stride),
+        in_specs=[vmem] * len(blocks),
         out_shape=[
             taken,
             taken,
@@ -206,62 +237,89 @@
             jax.ShapeDtypeStruct((2, pairs, LANES), jnp.float32),
         ],
         name="select",
-        compiler_params=pltpu.CompilerParams(vmem_limit_bytes=20 * MIB),
-    )(where, *blocks)
-
-
-def expert_kernel(own_ref, came_ref, w_in_ref, w_out_ref, out_ref):
+        compiler_params=pltpu.CompilerParams(vmem_limit_bytes=16 * MIB),
+    )(*blocks)
+
+
+def load_kernel(source, out_ref, sems, *, at):
+    pieces = sems.shape[0]
+    rows = out_ref.shape[0] // pieces
+    copies = [
+        pltpu.make_async_copy(
+            source.at[0, pl.ds(at[0] + p * rows, rows), pl.ds(at[1], out_ref.shape[1])],
+            out_ref.at[pl.ds(p * rows, rows)],
+            sems.at[p],
+        )
+        for p in range(pieces)
+    ]
+    for copy in copies:
+        copy.start()
+    for copy in copies:
+        copy.wait()
+
+
+def load(weights, at, shape):
+    return pl.pallas_call(
+        functools.partial(load_kernel, at=at),
+        in_specs=[pl.BlockSpec(memory_space=pltpu.HBM)],
+        out_shape=jax.ShapeDtypeStruct(shape, weights.dtype),
+        scratch_shapes=[pltpu.SemaphoreType.DMA((8,))],
+        name="load",
+        compiler_params=pltpu.CompilerParams(vmem_limit_bytes=4 * MIB),
+    )(pltpu.with_memory_space_constraint(weights, pltpu.HBM))
+
+
+def expert_kernel(own_ref, came_ref, in_a, in_b, out_a, out_b, out_ref):
+    dot = functools.partial(jnp.dot, preferred_element_type=jnp.float32)
     rows = own_ref[...] + came_ref[...]
-    hidden = jnp.dot(rows, w_in_ref[0], preferred_element_type=jnp.float32)
-    hidden = jnp.maximum(hidden, 0.0).astype(jnp.bfloat16)
-    result = jnp.dot(hidden, w_out_ref[0], preferred_element_type=jnp.float32)
+    result = None
+    for first, second in ((in_a, out_a), (in_b, out_b)):
+        hidden = jnp.maximum(dot(rows, first[...]), 0.0).astype(jnp.bfloat16)
+        part = dot(hidden, second[...])
+        result = part if result is None else result + part
     out_ref[...] = result.astype(jnp.bfloat16)
 
 
-def expert(own, came, w_in, w_out):
+def expert(own, came, weights):
     vmem = pl.BlockSpec(memory_space=pltpu.VMEM)
     return pl.pallas_call(
         expert_kernel,
-        in_specs=[vmem] * 4,
+        in_specs=[vmem] * (2 + len(weights)),
         out_shape=jax.ShapeDtypeStruct(own.shape, jnp.bfloat16),
         name="expert",
-        compiler_params=pltpu.CompilerParams(vmem_limit_bytes=20 * MIB),
-    )(own, came, w_in, w_out)
+        compiler_params=pltpu.CompilerParams(vmem_limit_bytes=16 * MIB),
+    )(own, came, *weights)
 
 
 def spread_kernel(own_ref, came_ref, seat_ref, gate_ref, *out_refs, count, cap):
     pairs = seat_ref.shape[1]
-    half = pairs // 2
-    for p in range(2):
-        value = None
-        for k, ref in enumerate((own_ref, came_ref)):
-            weights = jnp.concatenate(
-                [
-                    one_hot(seat_ref[k, o : o + 1, :], cap) * gate_ref[k, o : o + 1, :]
-                    for o in range(p * half, (p + 1) * half)
-                ],
-                axis=1,
-            ).astype(jnp.bfloat16)
-            part = lax.dot_general(
-                weights,
-                ref[p * cap : (p + 1) * cap, :],
-                (((0,), (0,)), ((), ())),
-                preferred_element_type=jnp.float32,
-            )
-            value = part if value is None else value + part
-        value = value.astype(jnp.bfloat16)
-        for o in range(pairs):
-            out_refs[p * pairs + o][...] = value[o * count : (o + 1) * count, :]
-
-
-def spread(own, came, seat, gate, count, cap):
+    value = None
+    for k, ref in enumerate((own_ref, came_ref)):
+        weights = jnp.concatenate(
+            [
+                one_hot(seat_ref[k, o : o + 1, :], cap) * gate_ref[k, o : o + 1, :]
+                for o in range(pairs)
+            ],
+            axis=1,
+        ).astype(jnp.bfloat16)
+        part = lax.dot_general(
+            weights, ref[...], (((0,), (0,)), ((), ())), preferred_element_type=jnp.float32
+        )
+        value = part if value is None else value + part
+    value = value.astype(jnp.bfloat16)
+    for o, out_ref in enumerate(out_refs):
+        out_ref[...] = value[o * count : (o + 1) * count, :]
+
+
+def spread(own, came, seat, gate, count):
     blocks = 2 * seat.shape[1]
-    out = jax.ShapeDtypeStruct((count, own.shape[1]), jnp.bfloat16)
+    cap, width = own.shape
+    out = jax.ShapeDtypeStruct((count, width), jnp.bfloat16)
     return pl.pallas_call(
         functools.partial(spread_kernel, count=count, cap=cap),
         out_shape=[out] * blocks,
         name="spread",
-        compiler_params=pltpu.CompilerParams(vmem_limit_bytes=20 * MIB),
+        compiler_params=pltpu.CompilerParams(vmem_limit_bytes=12 * MIB),
     )(own, came, seat, gate)
 
 
@@ -274,31 +332,31 @@
     if 2 * count != LANES or length % 4 or experts % SUB or experts * LANES > SUB * width:
         return per_device(tokens, expert_ids, gates, w_in, w_out)
     inverse = (rings.perms[1], rings.perms[0], rings.perms[2])
-    where = np.asarray(
-        [
-            (here % SUB, here // SUB, mate % SUB, mate // SUB, core)
-            for here, (mate, core) in enumerate(zip(rings.mates, rings.cores, strict=True))
-        ],
-        np.int32,
-    )
-    here = lax.axis_index("grp") * n_dev + lax.axis_index("dev")
-    where = lax.dynamic_slice(jnp.asarray(where), (here, 0), (1, where.shape[1]))[0]
-
     held = {(0, 0): pack(expert_ids, gates, tokens, experts)}
-    for chosen in rings.rounds:
-        fresh = {}
-        for channel, block in chosen.items():
-            source = held[seen_from_source(channel, block, length)]
-            fresh[block] = lax.ppermute(source, axes, rings.perms[channel])
-        held.update(fresh)
+    for channel, block in gather_sequence():
+        source = held[seen_from_source(channel, block, length)]
+        held[block] = lax.ppermute(source, axes, rings.perms[channel])
     order = sorted(held, key=lambda b: (b[1], b[0]))
     cap = 4 * count
-    own, other, seat, gate = select(where, [held[b] for b in order], count, cap)
-    came = lax.ppermute(other, axes, rings.partner)
-    result = expert(own, came, w_in, w_out)
-    theirs = lax.ppermute(result, axes, rings.partner)
-    sums = spread(result, theirs, seat, gate, count, cap)
-    parts = {b: [sums[i]] for i, b in enumerate(order)}
+    units = w_in.shape[2]
+    weights = []
+    for array, at, shape in (
+        (w_in, (0, 0), (width, units // 2)),
+        (w_in, (0, units // 2), (width, units // 2)),
+        (w_out, (0, 0), (units // 2, width)),
+        (w_out, (units // 2, 0), (units // 2, width)),
+    ):
+        weights.append(load(array, at, shape))
+    parts = {}
+    for plane in range(2):
+        blocks = order[plane * length : (plane + 1) * length]
+        own, other, seat, gate = select([held[b] for b in blocks], count, cap, n_dev)
+        came = lax.ppermute(other, axes, rings.partner)
+        result = expert(own, came, weights)
+        theirs = lax.ppermute(result, axes, rings.partner)
+        sums = spread(result, theirs, seat, gate, count)
+        for block, value in zip(blocks, sums, strict=True):
+            parts[block] = [value]
 
     def total(block):
         value = parts[block][0].astype(jnp.float32)
@@ -306,13 +364,9 @@
             value = value + more.astype(jnp.float32)
         return value.astype(jnp.bfloat16)
 
-    for chosen in reversed(rings.rounds):
-        arrived = []
-        for channel, block in chosen.items():
-            value = lax.ppermute(total(block), axes, inverse[channel])
-            arrived.append((seen_from_source(channel, block, length), value))
-        for block, value in arrived:
-            parts[block].append(value)
+    for channel, block in return_sequence():
+        value = lax.ppermute(total(block), axes, inverse[channel])
+        parts[seen_from_source(channel, block, length)].append(value)
     return total((0, 0))
 
 
@@ -450,7 +504,16 @@
 
 def solution(mesh):
     rings = find_rings(mesh)
-    body = per_device if rings is None else functools.partial(on_rings, rings)
+    if rings is None:
+        return mapped(mesh, per_device)
+
+    def body(*args):
+        return on_rings(rings, *args)
+
+    return mapped(mesh, body)
+
+
+def mapped(mesh, body):
     return jax.shard_map(
         body,
         mesh=mesh,

time: 78.8 us -> 80.2 us (1.018)
  Pallas kernels: 6.05 us -> 13.6 us
  local copies, waits for them, and re-layouts: 6.28 us -> 0 us
  waiting for transfers between devices: 29.5 us -> 32.3 us
  starting transfers between devices: 35.6 us -> 32.9 us
    ppermute x15, waiting for transfers between devices: 14.4 us -> 23 us  [on_rings(): value = lax.ppermute(total(block), axes, inverse[channel])]
    pallas_call x2 -> x7, Pallas kernels: 2.82 us -> 9.95 us  [the longest x4 5.63 us: load(): pl.pallas_call(functools.partial(load_kernel, at=at), in_specs=[pl.BlockS...]
    unnamed x10 -> x0, local copies, waits for them, and re-layouts: 5.59 us -> none
    ppermute x1 -> x2, waiting for transfers between devices: 2.27 us -> 0.01 us  [on_rings(): came = lax.ppermute(other, axes, rings.partner)]
    ppermute x1 -> x2, waiting for transfers between devices: 2.15 us -> 0.01 us  [on_rings(): theirs = lax.ppermute(result, axes, rings.partner)]
    ppermute x15, starting transfers between devices: 17.7 us -> 15.6 us  [on_rings(): value = lax.ppermute(total(block), axes, inverse[channel])]
    ppermute x15, waiting for transfers between devices: 10.6 us -> 9.34 us  [on_rings(): held[block] = lax.ppermute(source, axes, rings.perms[channel])]
    ppermute x15, starting transfers between devices: 17.7 us -> 16.5 us  [on_rings(): held[block] = lax.ppermute(source, axes, rings.perms[channel])]
  transfers between devices with their start and end apart: 32 -> 34, of which waited for: 16 -> 14; matrix products, arithmetic and copies ran while one was open for 1% -> 0% of each run, Pallas kernels for 0% -> 16%
where the time goes in v4:
time: 80.2 us; the launch traced here: 80 us
  starting transfers between devices  32.9 us (41%)
  waiting for transfers between devices  32.3 us (40%)
  Pallas kernels  13.6 us (17%)
  other arithmetic  0.98 us (1%)
    ppermute x15, waiting for transfers between devices, on_rings(): value = lax.ppermute(total(block), axes, inverse[channel])  23 us
    ppermute x15, starting transfers between devices, on_rings(): held[block] = lax.ppermute(source, axes, rings.perms[channel])  16.5 us
    ppermute x15, starting transfers between devices, on_rings(): value = lax.ppermute(total(block), axes, inverse[channel])  15.6 us
    ppermute x15, waiting for transfers between devices, on_rings(): held[block] = lax.ppermute(source, axes, rings.perms[channel])  9.34 us
    pallas_call x4, Pallas kernels, load(): pl.pallas_call(functools.partial(load_kernel, at=at), in_specs=[pl.BlockS...  5.63 us
    pallas_call x2, Pallas kernels, expert(): pl.pallas_call(expert_kernel, in_specs=[vmem] * (2 + len(weights)), out_s...  3.4 us
    pallas_call x2, Pallas kernels, select(): pl.pallas_call(functools.partial(select_kernel, blocks=len(blocks), count...  2.45 us
  transfers between devices with their start and end apart: 34, of which 14 were waited for; matrix products, arithmetic and copies ran while one was open for 0% of the time, Pallas kernels for 16%

profile of v4, /device:TPU:0, one launch (start us, length us, event | category | flops | bytes accessed | tf_op | source)
XLA Modules:
  0.0 80.0 jit_solution(12949034578993837658)
XLA Ops:
  0.9 3.1 %collective-permute-start = (bf16[72,768]{1,0:T(8,128)(2,1)S(1)}, bf16[72,768]{1,0:T(8,128)(2,1)S(1)}, u32[]{:S(2)}, u32[]{:S(2)}) collective-permute-start(bf16[72,768]{1,0:T(8,128)(2,1)S(1)} %pack.1.refs_3_), channel_id=1, source_target_pairs={{0,8},{1,9},{2,10},{3,11},{8,16},{9,17},{10,18},{11,19},{16,24},{1... | collective-permute-start | bytes 331784 | tf_op jit(solution)/shard_map/ppermute | solution.py:338
  4.0 3.0 %collective-permute-done.refs_2_ = bf16[72,768]{1,0:T(8,128)(2,1)S(1)} collective-permute-done((bf16[72,768]{1,0:T(8,128)(2,1)S(1)}, bf16[72,768]{1,0:T(8,128)(2,1)S(1)}, u32[]{:S(2)}, u32[]{:S(2)}) %collective-permute-start) | collective-permute-done | bytes 110624 | tf_op jit(solution)/shard_map/ppermute | solution.py:338
  7.0 1.8 %collective-permute-start.1 = (bf16[72,768]{1,0:T(8,128)(2,1)S(1)}, bf16[72,768]{1,0:T(8,128)(2,1)S(1)}, u32[]{:S(2)}, u32[]{:S(2)}) collective-permute-start(bf16[72,768]{1,0:T(8,128)(2,1)S(1)} %collective-permute-done.refs_2_), channel_id=1, source_target_pairs={{0,8},{1,9},{2,10},{3,11},{8,16},{9,17},{10,18},{11,19},{16,24},{1... | collective-permute-start | bytes 331784 | tf_op jit(solution)/shard_map/ppermute | solution.py:338
  8.8 1.5 %collective-permute-start.13 = (bf16[72,768]{1,0:T(8,128)(2,1)S(1)}, bf16[72,768]{1,0:T(8,128)(2,1)S(1)}, u32[]{:S(2)}, u32[]{:S(2)}) collective-permute-start(bf16[72,768]{1,0:T(8,128)(2,1)S(1)} %collective-permute-done.3.refs_4_), channel_id=1, source_target_pairs={{0,1},{1,0},{2,3},{3,2},{8,9},{9,8},{10,11},{11,10},{16,17},{17,16... | collective-permute-start | bytes 331784 | tf_op jit(solution)/shard_map/ppermute | solution.py:338
  11.8 1.8 %collective-permute-start.2 = (bf16[72,768]{1,0:T(8,128)(2,1)S(1)}, bf16[72,768]{1,0:T(8,128)(2,1)S(1)}, u32[]{:S(2)}, u32[]{:S(2)}) collective-permute-start(bf16[72,768]{1,0:T(8,128)(2,1)S(1)} %collective-permute-done.1.refs_1_), channel_id=1, source_target_pairs={{0,8},{1,9},{2,10},{3,11},{8,16},{9,17},{10,18},{11,19},{16,24},{1... | collective-permute-start | bytes 331784 | tf_op jit(solution)/shard_map/ppermute | solution.py:338
  13.8 2.4 %collective-permute-done.4.refs_5_ = bf16[72,768]{1,0:T(8,128)(2,1)S(1)} collective-permute-done((bf16[72,768]{1,0:T(8,128)(2,1)S(1)}, bf16[72,768]{1,0:T(8,128)(2,1)S(1)}, u32[]{:S(2)}, u32[]{:S(2)}) %collective-permute-start.4) | collective-permute-done | bytes 110624 | tf_op jit(solution)/shard_map/ppermute | solution.py:338
  17.1 1.7 %collective-permute-start.6 = (bf16[72,768]{1,0:T(8,128)(2,1)S(1)}, bf16[72,768]{1,0:T(8,128)(2,1)S(1)}, u32[]{:S(2)}, u32[]{:S(2)}) collective-permute-start(bf16[72,768]{1,0:T(8,128)(2,1)S(1)} %collective-permute-done.2.refs_0_), channel_id=1, source_target_pairs={{0,8},{1,9},{2,10},{3,11},{8,16},{9,17},{10,18},{11,19},{16,24},{1... | collective-permute-start | bytes 331784 | tf_op jit(solution)/shard_map/ppermute | solution.py:338
  18.8 1.5 %collective-permute-start.12 = (bf16[72,768]{1,0:T(8,128)(2,1)S(1)}, bf16[72,768]{1,0:T(8,128)(2,1)S(1)}, u32[]{:S(2)}, u32[]{:S(2)}) collective-permute-start(bf16[72,768]{1,0:T(8,128)(2,1)S(1)} %pack.1.refs_3_), channel_id=1, source_target_pairs={{0,1},{1,0},{2,3},{3,2},{8,9},{9,8},{10,11},{11,10},{16,17},{17,16... | collective-permute-start | bytes 331784 | tf_op jit(solution)/shard_map/ppermute | solution.py:338
  21.9 1.5 %collective-permute-start.10 = (bf16[72,768]{1,0:T(8,128)(2,1)S(1)}, bf16[72,768]{1,0:T(8,128)(2,1)S(1)}, u32[]{:S(2)}, u32[]{:S(2)}) collective-permute-start(bf16[72,768]{1,0:T(8,128)(2,1)S(1)} %collective-permute-done.9.refs_1_), channel_id=1, source_target_pairs={{0,8},{1,9},{2,10},{3,11},{8,16},{9,17},{10,18},{11,19},{16,24},{1... | collective-permute-start | bytes 331784 | tf_op jit(solution)/shard_map/ppermute | solution.py:338
  26.6 1.5 %collective-permute-done.16.refs_7_ = bf16[72,768]{1,0:T(8,128)(2,1)S(1)} collective-permute-done((bf16[72,768]{1,0:T(8,128)(2,1)S(1)}, bf16[72,768]{1,0:T(8,128)(2,1)S(1)}, u32[]{:S(2)}, u32[]{:S(2)}) %collective-permute-start.16) | collective-permute-done | bytes 110624 | tf_op jit(solution)/shard_map/ppermute | solution.py:338
  35.1 1.7 %expert.2.own_ref = bf16[256,768]{1,0:T(8,128)(2,1)S(1)} custom-call(bf16[256,768]{1,0:T(8,128)(2,1)S(1)} %get-tuple-element.29.own_ref, bf16[256,768]{1,0:T(8,128)(2,1)S(1)} %collective-permute-done.7.came_ref, bf16[768,768]{1,0:T(8,128)(2,1)S(1)} %load.4.in_a, bf16[768,768]{1,0:T(8,128)(2,1)S(1)} %load.5.in_b, bf16[768,768]{1,0:T(8,128)(2,1)S(1)} %load.6.out_a, ...), custom_call_target="tpu_custom_call" | custom-call | tf_op jit(solution)/shard_map/expert/pallas_call | solution.py:285
  37.4 1.7 %expert.3.own_ref = bf16[256,768]{1,0:T(8,128)(2,1)S(1)} custom-call(bf16[256,768]{1,0:T(8,128)(2,1)S(1)} %get-tuple-element.34.own_ref, bf16[256,768]{1,0:T(8,128)(2,1)S(1)} %collective-permute-done.17.came_ref, bf16[768,768]{1,0:T(8,128)(2,1)S(1)} %load.4.in_a, bf16[768,768]{1,0:T(8,128)(2,1)S(1)} %load.5.in_b, bf16[768,768]{1,0:T(8,128)(2,1)S(1)} %load.6.out_a, ...), custom_call_target="tpu_custom_call" | custom-call | tf_op jit(solution)/shard_map/expert/pallas_call | solution.py:285
  39.8 1.6 %collective-permute-start.31 = (bf16[64,768]{1,0:T(8,128)(2,1)S(1)}, bf16[64,768]{1,0:T(8,128)(2,1)S(1)}, u32[]{:S(2)}, u32[]{:S(2)}) collective-permute-start(bf16[64,768]{1,0:T(8,128)(2,1)S(1)} %get-tuple-element.52), channel_id=1, source_target_pairs={{0,8},{1,9},{2,10},{3,11},{8,16},{9,17},{10,18},{11,19},{16,24},{1... | collective-permute-start | bytes 294920 | tf_op jit(solution)/shard_map/ppermute | solution.py:368
  42.6 2.5 %collective-permute-done.31 = bf16[64,768]{1,0:T(8,128)(2,1)S(1)} collective-permute-done((bf16[64,768]{1,0:T(8,128)(2,1)S(1)}, bf16[64,768]{1,0:T(8,128)(2,1)S(1)}, u32[]{:S(2)}, u32[]{:S(2)}) %collective-permute-start.31) | collective-permute-done | bytes 98336 | tf_op jit(solution)/shard_map/ppermute | solution.py:368
  45.1 1.6 %collective-permute-start.32 = (bf16[64,768]{1,0:T(8,128)(2,1)S(1)}, bf16[64,768]{1,0:T(8,128)(2,1)S(1)}, u32[]{:S(2)}, u32[]{:S(2)}) collective-permute-start(bf16[64,768]{1,0:T(8,128)(2,1)S(1)} %add_convert_fusion.2), channel_id=1, source_target_pairs={{0,8},{1,9},{2,10},{3,11},{8,16},{9,17},{10,18},{11,19},{16,24},{1... | collective-permute-start | bytes 294920 | tf_op jit(solution)/shard_map/ppermute | solution.py:368
  49.7 1.6 %collective-permute-start.28 = (bf16[64,768]{1,0:T(8,128)(2,1)S(1)}, bf16[64,768]{1,0:T(8,128)(2,1)S(1)}, u32[]{:S(2)}, u32[]{:S(2)}) collective-permute-start(bf16[64,768]{1,0:T(8,128)(2,1)S(1)} %get-tuple-element.50), channel_id=1, source_target_pairs={{0,8},{1,9},{2,10},{3,11},{8,16},{9,17},{10,18},{11,19},{16,24},{1... | collective-permute-start | bytes 294920 | tf_op jit(solution)/shard_map/ppermute | solution.py:368
  51.3 3.7 %collective-permute-done.23 = bf16[64,768]{1,0:T(8,128)(2,1)S(1)} collective-permute-done((bf16[64,768]{1,0:T(8,128)(2,1)S(1)}, bf16[64,768]{1,0:T(8,128)(2,1)S(1)}, u32[]{:S(2)}, u32[]{:S(2)}) %collective-permute-start.23) | collective-permute-done | bytes 98336 | tf_op jit(solution)/shard_map/ppermute | solution.py:368
  56.5 4.1 %collective-permute-done.24 = bf16[64,768]{1,0:T(8,128)(2,1)S(1)} collective-permute-done((bf16[64,768]{1,0:T(8,128)(2,1)S(1)}, bf16[64,768]{1,0:T(8,128)(2,1)S(1)}, u32[]{:S(2)}, u32[]{:S(2)}) %collective-permute-start.24) | collective-permute-done | bytes 98336 | tf_op jit(solution)/shard_map/ppermute | solution.py:368
  60.6 1.6 %collective-permute-start.29 = (bf16[64,768]{1,0:T(8,128)(2,1)S(1)}, bf16[64,768]{1,0:T(8,128)(2,1)S(1)}, u32[]{:S(2)}, u32[]{:S(2)}) collective-permute-start(bf16[64,768]{1,0:T(8,128)(2,1)S(1)} %add_convert_fusion.4), channel_id=1, source_target_pairs={{0,8},{1,9},{2,10},{3,11},{8,16},{9,17},{10,18},{11,19},{16,24},{1... | collective-permute-start | bytes 294920 | tf_op jit(solution)/shard_map/ppermute | solution.py:368
  62.2 3.0 %collective-permute-done.29 = bf16[64,768]{1,0:T(8,128)(2,1)S(1)} collective-permute-done((bf16[64,768]{1,0:T(8,128)(2,1)S(1)}, bf16[64,768]{1,0:T(8,128)(2,1)S(1)}, u32[]{:S(2)}, u32[]{:S(2)}) %collective-permute-start.29) | collective-permute-done | bytes 98336 | tf_op jit(solution)/shard_map/ppermute | solution.py:368
  66.9 3.0 %collective-permute-done.25 = bf16[64,768]{1,0:T(8,128)(2,1)S(1)} collective-permute-done((bf16[64,768]{1,0:T(8,128)(2,1)S(1)}, bf16[64,768]{1,0:T(8,128)(2,1)S(1)}, u32[]{:S(2)}, u32[]{:S(2)}) %collective-permute-start.25) | collective-permute-done | bytes 98336 | tf_op jit(solution)/shard_map/ppermute | solution.py:368
  70.5 1.6 %collective-permute-start.33 = (bf16[64,768]{1,0:T(8,128)(2,1)S(1)}, bf16[64,768]{1,0:T(8,128)(2,1)S(1)}, u32[]{:S(2)}, u32[]{:S(2)}) collective-permute-start(bf16[64,768]{1,0:T(8,128)(2,1)S(1)} %add_convert_fusion.1), channel_id=1, source_target_pairs={{0,8},{1,9},{2,10},{3,11},{8,16},{9,17},{10,18},{11,19},{16,24},{1... | collective-permute-start | bytes 294920 | tf_op jit(solution)/shard_map/ppermute | solution.py:368
  72.1 2.5 %collective-permute-done.26 = bf16[64,768]{1,0:T(8,128)(2,1)S(1)} collective-permute-done((bf16[64,768]{1,0:T(8,128)(2,1)S(1)}, bf16[64,768]{1,0:T(8,128)(2,1)S(1)}, u32[]{:S(2)}, u32[]{:S(2)}) %collective-permute-start.26) | collective-permute-done | bytes 98336 | tf_op jit(solution)/shard_map/ppermute | solution.py:368
  75.1 4.2 %collective-permute-done.27 = bf16[64,768]{1,0:T(8,128)(2,1)S(1)} collective-permute-done((bf16[64,768]{1,0:T(8,128)(2,1)S(1)}, bf16[64,768]{1,0:T(8,128)(2,1)S(1)}, u32[]{:S(2)}, u32[]{:S(2)}) %collective-permute-start.27) | collective-permute-done | bytes 98336 | tf_op jit(solution)/shard_map/ppermute | solution.py:368
  (65 shorter events, 25.6 us)
Async XLA Ops:
  0.9 6.1 %collective-permute-start = (bf16[72,768]{1,0:T(8,128)(2,1)S(1)}, bf16[72,768]{1,0:T(8,128)(2,1)S(1)}, u32[]{:S(2)}, u32[]{:S(2)}) collective-permute-start(bf16[72,768]{1,0:T(8,128)(2,1)S(1)} %pack.1.refs_3_), channel_id=1, source_target_pairs={{0,8},{1,9},{2,10},{3,11},{8,16},{9,17},{10,18},{11,19},{16,24},{1... | collective-permute-start | bytes 331784 | tf_op jit(solution)/shard_map/ppermute | solution.py:338
  4.0 4.8 %collective-permute-start.3 = (bf16[72,768]{1,0:T(8,128)(2,1)S(1)}, bf16[72,768]{1,0:T(8,128)(2,1)S(1)}, u32[]{:S(2)}, u32[]{:S(2)}) collective-permute-start(bf16[72,768]{1,0:T(8,128)(2,1)S(1)} %pack.1.refs_3_), channel_id=1, source_target_pairs={{8,0},{9,1},{10,2},{11,3},{16,8},{17,9},{18,10},{19,11},{24,16},{2... | collective-permute-start | bytes 331784 | tf_op jit(solution)/shard_map/ppermute | solution.py:338
  7.0 4.7 %collective-permute-start.1 = (bf16[72,768]{1,0:T(8,128)(2,1)S(1)}, bf16[72,768]{1,0:T(8,128)(2,1)S(1)}, u32[]{:S(2)}, u32[]{:S(2)}) collective-permute-start(bf16[72,768]{1,0:T(8,128)(2,1)S(1)} %collective-permute-done.refs_2_), channel_id=1, source_target_pairs={{0,8},{1,9},{2,10},{3,11},{8,16},{9,17},{10,18},{11,19},{16,24},{1... | collective-permute-start | bytes 331784 | tf_op jit(solution)/shard_map/ppermute | solution.py:338
  8.8 4.7 %collective-permute-start.13 = (bf16[72,768]{1,0:T(8,128)(2,1)S(1)}, bf16[72,768]{1,0:T(8,128)(2,1)S(1)}, u32[]{:S(2)}, u32[]{:S(2)}) collective-permute-start(bf16[72,768]{1,0:T(8,128)(2,1)S(1)} %collective-permute-done.3.refs_4_), channel_id=1, source_target_pairs={{0,1},{1,0},{2,3},{3,2},{8,9},{9,8},{10,11},{11,10},{16,17},{17,16... | collective-permute-start | bytes 331784 | tf_op jit(solution)/shard_map/ppermute | solution.py:338
  10.4 5.8 %collective-permute-start.4 = (bf16[72,768]{1,0:T(8,128)(2,1)S(1)}, bf16[72,768]{1,0:T(8,128)(2,1)S(1)}, u32[]{:S(2)}, u32[]{:S(2)}) collective-permute-start(bf16[72,768]{1,0:T(8,128)(2,1)S(1)} %collective-permute-done.3.refs_4_), channel_id=1, source_target_pairs={{8,0},{9,1},{10,2},{11,3},{16,8},{17,9},{18,10},{19,11},{24,16},{2... | collective-permute-start | bytes 331784 | tf_op jit(solution)/shard_map/ppermute | solution.py:338
  11.8 5.3 %collective-permute-start.2 = (bf16[72,768]{1,0:T(8,128)(2,1)S(1)}, bf16[72,768]{1,0:T(8,128)(2,1)S(1)}, u32[]{:S(2)}, u32[]{:S(2)}) collective-permute-start(bf16[72,768]{1,0:T(8,128)(2,1)S(1)} %collective-permute-done.1.refs_1_), channel_id=1, source_target_pairs={{0,8},{1,9},{2,10},{3,11},{8,16},{9,17},{10,18},{11,19},{16,24},{1... | collective-permute-start | bytes 331784 | tf_op jit(solution)/shard_map/ppermute | solution.py:338
  13.6 6.7 %collective-permute-start.14 = (bf16[72,768]{1,0:T(8,128)(2,1)S(1)}, bf16[72,768]{1,0:T(8,128)(2,1)S(1)}, u32[]{:S(2)}, u32[]{:S(2)}) collective-permute-start(bf16[72,768]{1,0:T(8,128)(2,1)S(1)} %collective-permute-done.13.refs_4_), channel_id=1, source_target_pairs={{8,0},{9,1},{10,2},{11,3},{16,8},{17,9},{18,10},{19,11},{24,16},{2... | collective-permute-start | bytes 331784 | tf_op jit(solution)/shard_map/ppermute | solution.py:338
  16.2 5.2 %collective-permute-start.5 = (bf16[72,768]{1,0:T(8,128)(2,1)S(1)}, bf16[72,768]{1,0:T(8,128)(2,1)S(1)}, u32[]{:S(2)}, u32[]{:S(2)}) collective-permute-start(bf16[72,768]{1,0:T(8,128)(2,1)S(1)} %collective-permute-done.4.refs_5_), channel_id=1, source_target_pairs={{8,0},{9,1},{10,2},{11,3},{16,8},{17,9},{18,10},{19,11},{24,16},{2... | collective-permute-start | bytes 331784 | tf_op jit(solution)/shard_map/ppermute | solution.py:338
  16.7 5.2 %collective-permute-start.9 = (bf16[72,768]{1,0:T(8,128)(2,1)S(1)}, bf16[72,768]{1,0:T(8,128)(2,1)S(1)}, u32[]{:S(2)}, u32[]{:S(2)}) collective-permute-start(bf16[72,768]{1,0:T(8,128)(2,1)S(1)} %collective-permute-done.1.refs_1_), channel_id=1, source_target_pairs={{0,1},{1,0},{2,3},{3,2},{8,9},{9,8},{10,11},{11,10},{16,17},{17,16... | collective-permute-start | bytes 331784 | tf_op jit(solution)/shard_map/ppermute | solution.py:338
  17.1 6.3 %collective-permute-start.6 = (bf16[72,768]{1,0:T(8,128)(2,1)S(1)}, bf16[72,768]{1,0:T(8,128)(2,1)S(1)}, u32[]{:S(2)}, u32[]{:S(2)}) collective-permute-start(bf16[72,768]{1,0:T(8,128)(2,1)S(1)} %collective-permute-done.2.refs_0_), channel_id=1, source_target_pairs={{0,8},{1,9},{2,10},{3,11},{8,16},{9,17},{10,18},{11,19},{16,24},{1... | collective-permute-start | bytes 331784 | tf_op jit(solution)/shard_map/ppermute | solution.py:338
  18.8 6.8 %collective-permute-start.12 = (bf16[72,768]{1,0:T(8,128)(2,1)S(1)}, bf16[72,768]{1,0:T(8,128)(2,1)S(1)}, u32[]{:S(2)}, u32[]{:S(2)}) collective-permute-start(bf16[72,768]{1,0:T(8,128)(2,1)S(1)} %pack.1.refs_3_), channel_id=1, source_target_pairs={{0,1},{1,0},{2,3},{3,2},{8,9},{9,8},{10,11},{11,10},{16,17},{17,16... | collective-permute-start | bytes 331784 | tf_op jit(solution)/shard_map/ppermute | solution.py:338
  20.3 5.4 %collective-permute-start.11 = (bf16[72,768]{1,0:T(8,128)(2,1)S(1)}, bf16[72,768]{1,0:T(8,128)(2,1)S(1)}, u32[]{:S(2)}, u32[]{:S(2)}) collective-permute-start(bf16[72,768]{1,0:T(8,128)(2,1)S(1)} %collective-permute-done.refs_2_), channel_id=1, source_target_pairs={{0,1},{1,0},{2,3},{3,2},{8,9},{9,8},{10,11},{11,10},{16,17},{17,16... | collective-permute-start | bytes 331784 | tf_op jit(solution)/shard_map/ppermute | solution.py:338
  21.9 4.7 %collective-permute-start.10 = (bf16[72,768]{1,0:T(8,128)(2,1)S(1)}, bf16[72,768]{1,0:T(8,128)(2,1)S(1)}, u32[]{:S(2)}, u32[]{:S(2)}) collective-permute-start(bf16[72,768]{1,0:T(8,128)(2,1)S(1)} %collective-permute-done.9.refs_1_), channel_id=1, source_target_pairs={{0,8},{1,9},{2,10},{3,11},{8,16},{9,17},{10,18},{11,19},{16,24},{1... | collective-permute-start | bytes 331784 | tf_op jit(solution)/shard_map/ppermute | solution.py:338
  23.4 4.7 %collective-permute-start.16 = (bf16[72,768]{1,0:T(8,128)(2,1)S(1)}, bf16[72,768]{1,0:T(8,128)(2,1)S(1)}, u32[]{:S(2)}, u32[]{:S(2)}) collective-permute-start(bf16[72,768]{1,0:T(8,128)(2,1)S(1)} %collective-permute-done.6.refs_7_), channel_id=1, source_target_pairs={{0,1},{1,0},{2,3},{3,2},{8,9},{9,8},{10,11},{11,10},{16,17},{17,16... | collective-permute-start | bytes 331784 | tf_op jit(solution)/shard_map/ppermute | solution.py:338
  25.6 9.5 %collective-permute-start.7 = (bf16[256,768]{1,0:T(8,128)(2,1)S(1)}, bf16[256,768]{1,0:T(8,128)(2,1)S(1)}, u32[]{:S(2)}, u32[]{:S(2)}) collective-permute-start(bf16[256,768]{1,0:T(8,128)(2,1)S(1)} %get-tuple-element.30), channel_id=1, source_target_pairs={{0,2},{1,3},{2,0},{3,1},{8,10},{9,11},{10,8},{11,9},{16,18},{17,19... | collective-permute-start | bytes 1179656 | tf_op jit(solution)/shard_map/ppermute | solution.py:354
  29.4 8.0 %collective-permute-start.17 = (bf16[256,768]{1,0:T(8,128)(2,1)S(1)}, bf16[256,768]{1,0:T(8,128)(2,1)S(1)}, u32[]{:S(2)}, u32[]{:S(2)}) collective-permute-start(bf16[256,768]{1,0:T(8,128)(2,1)S(1)} %get-tuple-element.35), channel_id=1, source_target_pairs={{0,2},{1,3},{2,0},{3,1},{8,10},{9,11},{10,8},{11,9},{16,18},{17,19... | collective-permute-start | bytes 1179656 | tf_op jit(solution)/shard_map/ppermute | solution.py:354
  39.8 5.2 %collective-permute-start.31 = (bf16[64,768]{1,0:T(8,128)(2,1)S(1)}, bf16[64,768]{1,0:T(8,128)(2,1)S(1)}, u32[]{:S(2)}, u32[]{:S(2)}) collective-permute-start(bf16[64,768]{1,0:T(8,128)(2,1)S(1)} %get-tuple-element.52), channel_id=1, source_target_pairs={{0,8},{1,9},{2,10},{3,11},{8,16},{9,17},{10,18},{11,19},{16,24},{1... | collective-permute-start | bytes 294920 | tf_op jit(solution)/shard_map/ppermute | solution.py:368
  42.1 7.6 %collective-permute-start.21 = (bf16[64,768]{1,0:T(8,128)(2,1)S(1)}, bf16[64,768]{1,0:T(8,128)(2,1)S(1)}, u32[]{:S(2)}, u32[]{:S(2)}) collective-permute-start(bf16[64,768]{1,0:T(8,128)(2,1)S(1)} %get-tuple-element.43), channel_id=1, source_target_pairs={{8,0},{9,1},{10,2},{11,3},{16,8},{17,9},{18,10},{19,11},{24,16},{2... | collective-permute-start | bytes 294920 | tf_op jit(solution)/shard_map/ppermute | solution.py:368
  45.1 25.3 %collective-permute-start.32 = (bf16[64,768]{1,0:T(8,128)(2,1)S(1)}, bf16[64,768]{1,0:T(8,128)(2,1)S(1)}, u32[]{:S(2)}, u32[]{:S(2)}) collective-permute-start(bf16[64,768]{1,0:T(8,128)(2,1)S(1)} %add_convert_fusion.2), channel_id=1, source_target_pairs={{0,8},{1,9},{2,10},{3,11},{8,16},{9,17},{10,18},{11,19},{16,24},{1... | collective-permute-start | bytes 294920 | tf_op jit(solution)/shard_map/ppermute | solution.py:368
  46.7 28.4 %collective-permute-start.19 = (bf16[64,768]{1,0:T(8,128)(2,1)S(1)}, bf16[64,768]{1,0:T(8,128)(2,1)S(1)}, u32[]{:S(2)}, u32[]{:S(2)}) collective-permute-start(bf16[64,768]{1,0:T(8,128)(2,1)S(1)} %get-tuple-element.38), channel_id=1, source_target_pairs={{0,1},{1,0},{2,3},{3,2},{8,9},{9,8},{10,11},{11,10},{16,17},{17,16... | collective-permute-start | bytes 294920 | tf_op jit(solution)/shard_map/ppermute | solution.py:368
  47.7 24.4 %collective-permute-start.20 = (bf16[64,768]{1,0:T(8,128)(2,1)S(1)}, bf16[64,768]{1,0:T(8,128)(2,1)S(1)}, u32[]{:S(2)}, u32[]{:S(2)}) collective-permute-start(bf16[64,768]{1,0:T(8,128)(2,1)S(1)} %get-tuple-element.40), channel_id=1, source_target_pairs={{0,1},{1,0},{2,3},{3,2},{8,9},{9,8},{10,11},{11,10},{16,17},{17,16... | collective-permute-start | bytes 294920 | tf_op jit(solution)/shard_map/ppermute | solution.py:368
  48.7 6.2 %collective-permute-start.23 = (bf16[64,768]{1,0:T(8,128)(2,1)S(1)}, bf16[64,768]{1,0:T(8,128)(2,1)S(1)}, u32[]{:S(2)}, u32[]{:S(2)}) collective-permute-start(bf16[64,768]{1,0:T(8,128)(2,1)S(1)} %get-tuple-element.46), channel_id=1, source_target_pairs={{0,1},{1,0},{2,3},{3,2},{8,9},{9,8},{10,11},{11,10},{16,17},{17,16... | collective-permute-start | bytes 294920 | tf_op jit(solution)/shard_map/ppermute | solution.py:368
  49.7 6.3 %collective-permute-start.28 = (bf16[64,768]{1,0:T(8,128)(2,1)S(1)}, bf16[64,768]{1,0:T(8,128)(2,1)S(1)}, u32[]{:S(2)}, u32[]{:S(2)}) collective-permute-start(bf16[64,768]{1,0:T(8,128)(2,1)S(1)} %get-tuple-element.50), channel_id=1, source_target_pairs={{0,8},{1,9},{2,10},{3,11},{8,16},{9,17},{10,18},{11,19},{16,24},{1... | collective-permute-start | bytes 294920 | tf_op jit(solution)/shard_map/ppermute | solution.py:368
  55.0 10.8 %collective-permute-start.22 = (bf16[64,768]{1,0:T(8,128)(2,1)S(1)}, bf16[64,768]{1,0:T(8,128)(2,1)S(1)}, u32[]{:S(2)}, u32[]{:S(2)}) collective-permute-start(bf16[64,768]{1,0:T(8,128)(2,1)S(1)} %add_convert_fusion.9), channel_id=1, source_target_pairs={{0,1},{1,0},{2,3},{3,2},{8,9},{9,8},{10,11},{11,10},{16,17},{17,16... | collective-permute-start | bytes 294920 | tf_op jit(solution)/shard_map/ppermute | solution.py:368
  (10 other events, 42.0 us)

commit v5 on v4

--- a/solution.py
+++ b/solution.py
@@ -47,10 +47,10 @@
         (2, (-2, 1)),
         (0, (4, 0)),
         (1, (2, 1)),
+        (0, (-3, 1)),
         (2, (-1, 1)),
-        (0, (-3, 1)),
-        (1, (3, 1)),
         (2, (4, 1)),
+        (2, (3, 1)),
     )
 
 
@@ -59,16 +59,16 @@
         (2, (4, 1)),
         (0, (-3, 1)),
         (1, (3, 1)),
-        (2, (-1, 1)),
+        (2, (0, 1)),
         (0, (4, 0)),
+        (2, (-2, 1)),
         (1, (2, 1)),
-        (2, (-2, 1)),
         (0, (-3, 0)),
         (1, (3, 0)),
-        (2, (1, 1)),
+        (2, (-1, 1)),
         (0, (-2, 0)),
         (1, (2, 0)),
-        (2, (0, 1)),
+        (2, (1, 1)),
         (0, (-1, 0)),
         (1, (1, 0)),
     )
@@ -190,17 +190,16 @@
         lax.broadcasted_iota(jnp.int32, (LANES, LANES), 0)
         < lax.broadcasted_iota(jnp.int32, (LANES, LANES), 1)
     ).astype(jnp.bfloat16)
-    before = (
-        lax.broadcasted_iota(jnp.int32, (pairs, pairs), 1)
-        < lax.broadcasted_iota(jnp.int32, (pairs, pairs), 0)
-    ).astype(jnp.bfloat16)
+    left = lax.broadcasted_iota(jnp.int32, (2 * pairs, 2 * pairs), 0)
+    right = lax.broadcasted_iota(jnp.int32, (2 * pairs, 2 * pairs), 1)
+    before = ((right < left) & (right // pairs == left // pairs)).astype(jnp.bfloat16)
     lane = lax.broadcasted_iota(jnp.int32, (pairs, LANES), 1)
     row_of = lax.broadcasted_iota(jnp.int32, (pairs, blocks * SUB), 0)
     col_of = lax.broadcasted_iota(jnp.int32, (pairs, blocks * SUB), 1)
     groups = tails.shape[1] // LANES
     rows = jnp.concatenate([r[:count, :] for r in block_refs], axis=0)
-    for k, out_ref in enumerate((own_ref, other_ref)):
-        expert = (here, mate)[k]
+    picks = []
+    for expert in (here, mate):
         sub = expert % SUB
         group = expert // SUB
         table = tails[:, :LANES]
@@ -208,17 +207,20 @@
             table = jnp.where(group == q, tails[:, q * LANES : (q + 1) * LANES], table)
         pick_a = (col_of == (2 * row_of) * SUB + sub).astype(jnp.bfloat16)
         pick_b = (col_of == (2 * row_of + 1) * SUB + sub).astype(jnp.bfloat16)
-        gate = jnp.where(lane < count, dot(pick_a, table), dot(pick_b, table))
-        chosen = gate > 0.0
-        ones = jnp.where(chosen, 1.0, 0.0)
-        inside = dot(ones.astype(jnp.bfloat16), upper)
-        total = jnp.broadcast_to(jnp.sum(ones, axis=1, keepdims=True), (pairs, LANES))
-        spot = (inside + dot(before, total.astype(jnp.bfloat16))).astype(jnp.int32)
-        seat = jnp.where(here < mate, spot, cap - 1 - spot)
-        seat = jnp.where(chosen, seat, -1)
-        seat_ref[k] = seat
-        gate_ref[k] = gate
-        hot = jnp.concatenate([one_hot(seat[o : o + 1, :], cap) for o in range(pairs)], axis=1)
+        picks.append(jnp.where(lane < count, dot(pick_a, table), dot(pick_b, table)))
+    gate = jnp.concatenate(picks, axis=0)
+    chosen = gate > 0.0
+    ones = jnp.where(chosen, 1.0, 0.0)
+    total = jnp.broadcast_to(jnp.sum(ones, axis=1, keepdims=True), (2 * pairs, LANES))
+    spot = dot(ones.astype(jnp.bfloat16), upper) + dot(before, total.astype(jnp.bfloat16))
+    spot = spot.astype(jnp.int32)
+    seat = jnp.where(here < mate, spot, cap - 1 - spot)
+    seat = jnp.where(chosen, seat, -1)
+    for k, out_ref in enumerate((own_ref, other_ref)):
+        mine = seat[k * pairs : (k + 1) * pairs, :]
+        seat_ref[k] = mine
+        gate_ref[k] = gate[k * pairs : (k + 1) * pairs, :]
+        hot = jnp.concatenate([one_hot(mine[o : o + 1, :], cap) for o in range(pairs)], axis=1)
         out_ref[...] = dot(hot.astype(jnp.bfloat16), rows).astype(jnp.bfloat16)
 
 
@@ -269,11 +271,11 @@
     )(pltpu.with_memory_space_constraint(weights, pltpu.HBM))
 
 
-def expert_kernel(own_ref, came_ref, in_a, in_b, out_a, out_b, out_ref):
+def expert_kernel(own_ref, came_ref, in_a, out_a, out_ref):
     dot = functools.partial(jnp.dot, preferred_element_type=jnp.float32)
     rows = own_ref[...] + came_ref[...]
     result = None
-    for first, second in ((in_a, out_a), (in_b, out_b)):
+    for first, second in ((in_a, out_a),):
         hidden = jnp.maximum(dot(rows, first[...]), 0.0).astype(jnp.bfloat16)
         part = dot(hidden, second[...])
         result = part if result is None else result + part
@@ -341,10 +343,8 @@
     units = w_in.shape[2]
     weights = []
     for array, at, shape in (
-        (w_in, (0, 0), (width, units // 2)),
-        (w_in, (0, units // 2), (width, units // 2)),
-        (w_out, (0, 0), (units // 2, width)),
-        (w_out, (units // 2, 0), (units // 2, width)),
+        (w_in, (0, 0), (width, units)),
+        (w_out, (0, 0), (units, width)),
     ):
         weights.append(load(array, at, shape))
     parts = {}

time: 80.2 us -> 80.1 us (level)
  starting transfers between devices: 32.9 us -> 36.8 us
  Pallas kernels: 13.6 us -> 10.4 us
    ppermute x15, starting transfers between devices: 16.5 us -> 19.9 us  [on_rings(): held[block] = lax.ppermute(source, axes, rings.perms[channel])]
    pallas_call x4 -> x2, Pallas kernels: 5.63 us -> 3.31 us  [load(): pl.pallas_call(functools.partial(load_kernel, at=at), in_specs=[pl.BlockS...]
    ppermute x15, waiting for transfers between devices: 9.34 us -> 8.33 us  [on_rings(): held[block] = lax.ppermute(source, axes, rings.perms[channel])]
  transfers between devices with their start and end apart: 34 -> 34, of which waited for: 14 -> 12; matrix products, arithmetic and copies ran while one was open for 0% -> 0% of each run, Pallas kernels for 16% -> 12%
where the time goes in v5:
time: 80.1 us; the launch traced here: 79.9 us
  starting transfers between devices  36.8 us (46%)
  waiting for transfers between devices  31.6 us (39%)
  Pallas kernels  10.4 us (13%)
  other arithmetic  0.98 us (1%)
    ppermute x15, waiting for transfers between devices, on_rings(): value = lax.ppermute(total(block), axes, inverse[channel])  23.2 us
    ppermute x15, starting transfers between devices, on_rings(): held[block] = lax.ppermute(source, axes, rings.perms[channel])  19.9 us
    ppermute x15, starting transfers between devices, on_rings(): value = lax.ppermute(total(block), axes, inverse[channel])  16.2 us
    ppermute x15, waiting for transfers between devices, on_rings(): held[block] = lax.ppermute(source, axes, rings.perms[channel])  8.33 us
    pallas_call x2, Pallas kernels, load(): pl.pallas_call(functools.partial(load_kernel, at=at), in_specs=[pl.BlockS...  3.31 us
    pallas_call x2, Pallas kernels, expert(): pl.pallas_call(expert_kernel, in_specs=[vmem] * (2 + len(weights)), out_s...  3.02 us
    pallas_call x2, Pallas kernels, select(): pl.pallas_call(functools.partial(select_kernel, blocks=len(blocks), count...  1.89 us
  transfers between devices with their start and end apart: 34, of which 12 were waited for; matrix products, arithmetic and copies ran while one was open for 0% of the time, Pallas kernels for 12%

profile of v5, /device:TPU:0, one launch (start us, length us, event | category | flops | bytes accessed | tf_op | source)
XLA Modules:
  0.0 79.9 jit_solution(1308957838568899293)
XLA Ops:
  0.9 3.1 %collective-permute-start = (bf16[72,768]{1,0:T(8,128)(2,1)S(1)}, bf16[72,768]{1,0:T(8,128)(2,1)S(1)}, u32[]{:S(2)}, u32[]{:S(2)}) collective-permute-start(bf16[72,768]{1,0:T(8,128)(2,1)S(1)} %pack.1.refs_3_), channel_id=1, source_target_pairs={{0,8},{1,9},{2,10},{3,11},{8,16},{9,17},{10,18},{11,19},{16,24},{1... | collective-permute-start | bytes 331784 | tf_op jit(solution)/shard_map/ppermute | solution.py:340
  4.0 3.0 %collective-permute-done.refs_2_ = bf16[72,768]{1,0:T(8,128)(2,1)S(1)} collective-permute-done((bf16[72,768]{1,0:T(8,128)(2,1)S(1)}, bf16[72,768]{1,0:T(8,128)(2,1)S(1)}, u32[]{:S(2)}, u32[]{:S(2)}) %collective-permute-start) | collective-permute-done | bytes 110624 | tf_op jit(solution)/shard_map/ppermute | solution.py:340
  7.0 1.8 %collective-permute-start.1 = (bf16[72,768]{1,0:T(8,128)(2,1)S(1)}, bf16[72,768]{1,0:T(8,128)(2,1)S(1)}, u32[]{:S(2)}, u32[]{:S(2)}) collective-permute-start(bf16[72,768]{1,0:T(8,128)(2,1)S(1)} %collective-permute-done.refs_2_), channel_id=1, source_target_pairs={{0,8},{1,9},{2,10},{3,11},{8,16},{9,17},{10,18},{11,19},{16,24},{1... | collective-permute-start | bytes 331784 | tf_op jit(solution)/shard_map/ppermute | solution.py:340
  9.0 2.7 %collective-permute-done.1.refs_1_ = bf16[72,768]{1,0:T(8,128)(2,1)S(1)} collective-permute-done((bf16[72,768]{1,0:T(8,128)(2,1)S(1)}, bf16[72,768]{1,0:T(8,128)(2,1)S(1)}, u32[]{:S(2)}, u32[]{:S(2)}) %collective-permute-start.1) | collective-permute-done | bytes 110624 | tf_op jit(solution)/shard_map/ppermute | solution.py:340
  11.8 1.8 %collective-permute-start.2 = (bf16[72,768]{1,0:T(8,128)(2,1)S(1)}, bf16[72,768]{1,0:T(8,128)(2,1)S(1)}, u32[]{:S(2)}, u32[]{:S(2)}) collective-permute-start(bf16[72,768]{1,0:T(8,128)(2,1)S(1)} %collective-permute-done.1.refs_1_), channel_id=1, source_target_pairs={{0,8},{1,9},{2,10},{3,11},{8,16},{9,17},{10,18},{11,19},{16,24},{1... | collective-permute-start | bytes 331784 | tf_op jit(solution)/shard_map/ppermute | solution.py:340
  15.8 1.8 %collective-permute-start.9 = (bf16[72,768]{1,0:T(8,128)(2,1)S(1)}, bf16[72,768]{1,0:T(8,128)(2,1)S(1)}, u32[]{:S(2)}, u32[]{:S(2)}) collective-permute-start(bf16[72,768]{1,0:T(8,128)(2,1)S(1)} %collective-permute-done.1.refs_1_), channel_id=1, source_target_pairs={{0,1},{1,0},{2,3},{3,2},{8,9},{9,8},{10,11},{11,10},{16,17},{17,16... | collective-permute-start | bytes 331784 | tf_op jit(solution)/shard_map/ppermute | solution.py:340
  19.2 1.7 %collective-permute-start.11 = (bf16[72,768]{1,0:T(8,128)(2,1)S(1)}, bf16[72,768]{1,0:T(8,128)(2,1)S(1)}, u32[]{:S(2)}, u32[]{:S(2)}) collective-permute-start(bf16[72,768]{1,0:T(8,128)(2,1)S(1)} %collective-permute-done.refs_2_), channel_id=1, source_target_pairs={{0,1},{1,0},{2,3},{3,2},{8,9},{9,8},{10,11},{11,10},{16,17},{17,16... | collective-permute-start | bytes 331784 | tf_op jit(solution)/shard_map/ppermute | solution.py:340
  22.1 1.8 %collective-permute-start.15 = (bf16[72,768]{1,0:T(8,128)(2,1)S(1)}, bf16[72,768]{1,0:T(8,128)(2,1)S(1)}, u32[]{:S(2)}, u32[]{:S(2)}) collective-permute-start(bf16[72,768]{1,0:T(8,128)(2,1)S(1)} %collective-permute-done.5.refs_6_), channel_id=1, source_target_pairs={{0,1},{1,0},{2,3},{3,2},{8,9},{9,8},{10,11},{11,10},{16,17},{17,16... | collective-permute-start | bytes 331784 | tf_op jit(solution)/shard_map/ppermute | solution.py:340
  25.4 1.7 %collective-permute-start.16 = (bf16[72,768]{1,0:T(8,128)(2,1)S(1)}, bf16[72,768]{1,0:T(8,128)(2,1)S(1)}, u32[]{:S(2)}, u32[]{:S(2)}) collective-permute-start(bf16[72,768]{1,0:T(8,128)(2,1)S(1)} %collective-permute-done.6.refs_7_), channel_id=1, source_target_pairs={{0,1},{1,0},{2,3},{3,2},{8,9},{9,8},{10,11},{11,10},{16,17},{17,16... | collective-permute-start | bytes 331784 | tf_op jit(solution)/shard_map/ppermute | solution.py:340
  31.2 1.7 %load.2.in_a = bf16[768,1536]{1,0:T(8,128)(2,1)S(1)} custom-call(bf16[1,768,1536]{2,1,0:T(8,128)(2,1)} %source.2), custom_call_target="tpu_custom_call" | custom-call | tf_op jit(solution)/shard_map/load/pallas_call | solution.py:264
  32.9 1.7 %load.3.out_a = bf16[1536,768]{1,0:T(8,128)(2,1)S(1)} custom-call(bf16[1,1536,768]{2,1,0:T(8,128)(2,1)} %source.3), custom_call_target="tpu_custom_call" | custom-call | tf_op jit(solution)/shard_map/load/pallas_call | solution.py:264
  38.9 1.6 %collective-permute-start.28 = (bf16[64,768]{1,0:T(8,128)(2,1)S(1)}, bf16[64,768]{1,0:T(8,128)(2,1)S(1)}, u32[]{:S(2)}, u32[]{:S(2)}) collective-permute-start(bf16[64,768]{1,0:T(8,128)(2,1)S(1)} %get-tuple-element.49), channel_id=1, source_target_pairs={{0,8},{1,9},{2,10},{3,11},{8,16},{9,17},{10,18},{11,19},{16,24},{1... | collective-permute-start | bytes 294920 | tf_op jit(solution)/shard_map/ppermute | solution.py:368
  41.6 2.5 %collective-permute-done.28 = bf16[64,768]{1,0:T(8,128)(2,1)S(1)} collective-permute-done((bf16[64,768]{1,0:T(8,128)(2,1)S(1)}, bf16[64,768]{1,0:T(8,128)(2,1)S(1)}, u32[]{:S(2)}, u32[]{:S(2)}) %collective-permute-start.28) | collective-permute-done | bytes 98336 | tf_op jit(solution)/shard_map/ppermute | solution.py:368
  44.1 1.6 %collective-permute-start.29 = (bf16[64,768]{1,0:T(8,128)(2,1)S(1)}, bf16[64,768]{1,0:T(8,128)(2,1)S(1)}, u32[]{:S(2)}, u32[]{:S(2)}) collective-permute-start(bf16[64,768]{1,0:T(8,128)(2,1)S(1)} %add_convert_fusion.4), channel_id=1, source_target_pairs={{0,8},{1,9},{2,10},{3,11},{8,16},{9,17},{10,18},{11,19},{16,24},{1... | collective-permute-start | bytes 294920 | tf_op jit(solution)/shard_map/ppermute | solution.py:368
  45.8 1.8 %collective-permute-start.19 = (bf16[64,768]{1,0:T(8,128)(2,1)S(1)}, bf16[64,768]{1,0:T(8,128)(2,1)S(1)}, u32[]{:S(2)}, u32[]{:S(2)}) collective-permute-start(bf16[64,768]{1,0:T(8,128)(2,1)S(1)} %get-tuple-element.38), channel_id=1, source_target_pairs={{0,1},{1,0},{2,3},{3,2},{8,9},{9,8},{10,11},{11,10},{16,17},{17,16... | collective-permute-start | bytes 294920 | tf_op jit(solution)/shard_map/ppermute | solution.py:368
  47.8 1.8 %collective-permute-start.23 = (bf16[64,768]{1,0:T(8,128)(2,1)S(1)}, bf16[64,768]{1,0:T(8,128)(2,1)S(1)}, u32[]{:S(2)}, u32[]{:S(2)}) collective-permute-start(bf16[64,768]{1,0:T(8,128)(2,1)S(1)} %get-tuple-element.46), channel_id=1, source_target_pairs={{0,1},{1,0},{2,3},{3,2},{8,9},{9,8},{10,11},{11,10},{16,17},{17,16... | collective-permute-start | bytes 294920 | tf_op jit(solution)/shard_map/ppermute | solution.py:368
  49.6 1.6 %collective-permute-start.30 = (bf16[64,768]{1,0:T(8,128)(2,1)S(1)}, bf16[64,768]{1,0:T(8,128)(2,1)S(1)}, u32[]{:S(2)}, u32[]{:S(2)}) collective-permute-start(bf16[64,768]{1,0:T(8,128)(2,1)S(1)} %get-tuple-element.52), channel_id=1, source_target_pairs={{0,8},{1,9},{2,10},{3,11},{8,16},{9,17},{10,18},{11,19},{16,24},{1... | collective-permute-start | bytes 294920 | tf_op jit(solution)/shard_map/ppermute | solution.py:368
  51.2 3.3 %collective-permute-done.23 = bf16[64,768]{1,0:T(8,128)(2,1)S(1)} collective-permute-done((bf16[64,768]{1,0:T(8,128)(2,1)S(1)}, bf16[64,768]{1,0:T(8,128)(2,1)S(1)}, u32[]{:S(2)}, u32[]{:S(2)}) %collective-permute-start.23) | collective-permute-done | bytes 98336 | tf_op jit(solution)/shard_map/ppermute | solution.py:368
  56.3 4.2 %collective-permute-done.24 = bf16[64,768]{1,0:T(8,128)(2,1)S(1)} collective-permute-done((bf16[64,768]{1,0:T(8,128)(2,1)S(1)}, bf16[64,768]{1,0:T(8,128)(2,1)S(1)}, u32[]{:S(2)}, u32[]{:S(2)}) %collective-permute-start.24) | collective-permute-done | bytes 98336 | tf_op jit(solution)/shard_map/ppermute | solution.py:368
  62.2 3.0 %collective-permute-done.31 = bf16[64,768]{1,0:T(8,128)(2,1)S(1)} collective-permute-done((bf16[64,768]{1,0:T(8,128)(2,1)S(1)}, bf16[64,768]{1,0:T(8,128)(2,1)S(1)}, u32[]{:S(2)}, u32[]{:S(2)}) %collective-permute-start.31) | collective-permute-done | bytes 98336 | tf_op jit(solution)/shard_map/ppermute | solution.py:368
  66.3 3.5 %collective-permute-done.25 = bf16[64,768]{1,0:T(8,128)(2,1)S(1)} collective-permute-done((bf16[64,768]{1,0:T(8,128)(2,1)S(1)}, bf16[64,768]{1,0:T(8,128)(2,1)S(1)}, u32[]{:S(2)}, u32[]{:S(2)}) %collective-permute-start.25) | collective-permute-done | bytes 98336 | tf_op jit(solution)/shard_map/ppermute | solution.py:368
  70.3 1.7 %collective-permute-start.33 = (bf16[64,768]{1,0:T(8,128)(2,1)S(1)}, bf16[64,768]{1,0:T(8,128)(2,1)S(1)}, u32[]{:S(2)}, u32[]{:S(2)}) collective-permute-start(bf16[64,768]{1,0:T(8,128)(2,1)S(1)} %add_convert_fusion.1), channel_id=1, source_target_pairs={{0,8},{1,9},{2,10},{3,11},{8,16},{9,17},{10,18},{11,19},{16,24},{1... | collective-permute-start | bytes 294920 | tf_op jit(solution)/shard_map/ppermute | solution.py:368
  72.0 2.5 %collective-permute-done.26 = bf16[64,768]{1,0:T(8,128)(2,1)S(1)} collective-permute-done((bf16[64,768]{1,0:T(8,128)(2,1)S(1)}, bf16[64,768]{1,0:T(8,128)(2,1)S(1)}, u32[]{:S(2)}, u32[]{:S(2)}) %collective-permute-start.26) | collective-permute-done | bytes 98336 | tf_op jit(solution)/shard_map/ppermute | solution.py:368
  75.0 4.3 %collective-permute-done.27 = bf16[64,768]{1,0:T(8,128)(2,1)S(1)} collective-permute-done((bf16[64,768]{1,0:T(8,128)(2,1)S(1)}, bf16[64,768]{1,0:T(8,128)(2,1)S(1)}, u32[]{:S(2)}, u32[]{:S(2)}) %collective-permute-start.27) | collective-permute-done | bytes 98336 | tf_op jit(solution)/shard_map/ppermute | solution.py:368
  (63 shorter events, 23.6 us)
Async XLA Ops:
  0.9 6.1 %collective-permute-start = (bf16[72,768]{1,0:T(8,128)(2,1)S(1)}, bf16[72,768]{1,0:T(8,128)(2,1)S(1)}, u32[]{:S(2)}, u32[]{:S(2)}) collective-permute-start(bf16[72,768]{1,0:T(8,128)(2,1)S(1)} %pack.1.refs_3_), channel_id=1, source_target_pairs={{0,8},{1,9},{2,10},{3,11},{8,16},{9,17},{10,18},{11,19},{16,24},{1... | collective-permute-start | bytes 331784 | tf_op jit(solution)/shard_map/ppermute | solution.py:340
  4.0 4.8 %collective-permute-start.3 = (bf16[72,768]{1,0:T(8,128)(2,1)S(1)}, bf16[72,768]{1,0:T(8,128)(2,1)S(1)}, u32[]{:S(2)}, u32[]{:S(2)}) collective-permute-start(bf16[72,768]{1,0:T(8,128)(2,1)S(1)} %pack.1.refs_3_), channel_id=1, source_target_pairs={{8,0},{9,1},{10,2},{11,3},{16,8},{17,9},{18,10},{19,11},{24,16},{2... | collective-permute-start | bytes 331784 | tf_op jit(solution)/shard_map/ppermute | solution.py:340
  7.0 4.7 %collective-permute-start.1 = (bf16[72,768]{1,0:T(8,128)(2,1)S(1)}, bf16[72,768]{1,0:T(8,128)(2,1)S(1)}, u32[]{:S(2)}, u32[]{:S(2)}) collective-permute-start(bf16[72,768]{1,0:T(8,128)(2,1)S(1)} %collective-permute-done.refs_2_), channel_id=1, source_target_pairs={{0,8},{1,9},{2,10},{3,11},{8,16},{9,17},{10,18},{11,19},{16,24},{1... | collective-permute-start | bytes 331784 | tf_op jit(solution)/shard_map/ppermute | solution.py:340
  8.8 6.8 %collective-permute-start.4 = (bf16[72,768]{1,0:T(8,128)(2,1)S(1)}, bf16[72,768]{1,0:T(8,128)(2,1)S(1)}, u32[]{:S(2)}, u32[]{:S(2)}) collective-permute-start(bf16[72,768]{1,0:T(8,128)(2,1)S(1)} %collective-permute-done.3.refs_4_), channel_id=1, source_target_pairs={{8,0},{9,1},{10,2},{11,3},{16,8},{17,9},{18,10},{19,11},{24,16},{2... | collective-permute-start | bytes 331784 | tf_op jit(solution)/shard_map/ppermute | solution.py:340
  11.8 5.8 %collective-permute-start.2 = (bf16[72,768]{1,0:T(8,128)(2,1)S(1)}, bf16[72,768]{1,0:T(8,128)(2,1)S(1)}, u32[]{:S(2)}, u32[]{:S(2)}) collective-permute-start(bf16[72,768]{1,0:T(8,128)(2,1)S(1)} %collective-permute-done.1.refs_1_), channel_id=1, source_target_pairs={{0,8},{1,9},{2,10},{3,11},{8,16},{9,17},{10,18},{11,19},{16,24},{1... | collective-permute-start | bytes 331784 | tf_op jit(solution)/shard_map/ppermute | solution.py:340
  13.6 5.6 %collective-permute-start.12 = (bf16[72,768]{1,0:T(8,128)(2,1)S(1)}, bf16[72,768]{1,0:T(8,128)(2,1)S(1)}, u32[]{:S(2)}, u32[]{:S(2)}) collective-permute-start(bf16[72,768]{1,0:T(8,128)(2,1)S(1)} %pack.1.refs_3_), channel_id=1, source_target_pairs={{0,1},{1,0},{2,3},{3,2},{8,9},{9,8},{10,11},{11,10},{16,17},{17,16... | collective-permute-start | bytes 331784 | tf_op jit(solution)/shard_map/ppermute | solution.py:340
  15.1 6.4 %collective-permute-start.13 = (bf16[72,768]{1,0:T(8,128)(2,1)S(1)}, bf16[72,768]{1,0:T(8,128)(2,1)S(1)}, u32[]{:S(2)}, u32[]{:S(2)}) collective-permute-start(bf16[72,768]{1,0:T(8,128)(2,1)S(1)} %collective-permute-done.3.refs_4_), channel_id=1, source_target_pairs={{0,1},{1,0},{2,3},{3,2},{8,9},{9,8},{10,11},{11,10},{16,17},{17,16... | collective-permute-start | bytes 331784 | tf_op jit(solution)/shard_map/ppermute | solution.py:340
  15.6 6.5 %collective-permute-start.5 = (bf16[72,768]{1,0:T(8,128)(2,1)S(1)}, bf16[72,768]{1,0:T(8,128)(2,1)S(1)}, u32[]{:S(2)}, u32[]{:S(2)}) collective-permute-start(bf16[72,768]{1,0:T(8,128)(2,1)S(1)} %collective-permute-done.4.refs_5_), channel_id=1, source_target_pairs={{8,0},{9,1},{10,2},{11,3},{16,8},{17,9},{18,10},{19,11},{24,16},{2... | collective-permute-start | bytes 331784 | tf_op jit(solution)/shard_map/ppermute | solution.py:340
  15.8 8.1 %collective-permute-start.9 = (bf16[72,768]{1,0:T(8,128)(2,1)S(1)}, bf16[72,768]{1,0:T(8,128)(2,1)S(1)}, u32[]{:S(2)}, u32[]{:S(2)}) collective-permute-start(bf16[72,768]{1,0:T(8,128)(2,1)S(1)} %collective-permute-done.1.refs_1_), channel_id=1, source_target_pairs={{0,1},{1,0},{2,3},{3,2},{8,9},{9,8},{10,11},{11,10},{16,17},{17,16... | collective-permute-start | bytes 331784 | tf_op jit(solution)/shard_map/ppermute | solution.py:340
  17.6 7.9 %collective-permute-start.6 = (bf16[72,768]{1,0:T(8,128)(2,1)S(1)}, bf16[72,768]{1,0:T(8,128)(2,1)S(1)}, u32[]{:S(2)}, u32[]{:S(2)}) collective-permute-start(bf16[72,768]{1,0:T(8,128)(2,1)S(1)} %collective-permute-done.2.refs_0_), channel_id=1, source_target_pairs={{0,8},{1,9},{2,10},{3,11},{8,16},{9,17},{10,18},{11,19},{16,24},{1... | collective-permute-start | bytes 331784 | tf_op jit(solution)/shard_map/ppermute | solution.py:340
  19.2 9.0 %collective-permute-start.11 = (bf16[72,768]{1,0:T(8,128)(2,1)S(1)}, bf16[72,768]{1,0:T(8,128)(2,1)S(1)}, u32[]{:S(2)}, u32[]{:S(2)}) collective-permute-start(bf16[72,768]{1,0:T(8,128)(2,1)S(1)} %collective-permute-done.refs_2_), channel_id=1, source_target_pairs={{0,1},{1,0},{2,3},{3,2},{8,9},{9,8},{10,11},{11,10},{16,17},{17,16... | collective-permute-start | bytes 331784 | tf_op jit(solution)/shard_map/ppermute | solution.py:340
  21.5 6.7 %collective-permute-start.14 = (bf16[72,768]{1,0:T(8,128)(2,1)S(1)}, bf16[72,768]{1,0:T(8,128)(2,1)S(1)}, u32[]{:S(2)}, u32[]{:S(2)}) collective-permute-start(bf16[72,768]{1,0:T(8,128)(2,1)S(1)} %collective-permute-done.13.refs_4_), channel_id=1, source_target_pairs={{8,0},{9,1},{10,2},{11,3},{16,8},{17,9},{18,10},{19,11},{24,16},{2... | collective-permute-start | bytes 331784 | tf_op jit(solution)/shard_map/ppermute | solution.py:340
  22.1 6.1 %collective-permute-start.15 = (bf16[72,768]{1,0:T(8,128)(2,1)S(1)}, bf16[72,768]{1,0:T(8,128)(2,1)S(1)}, u32[]{:S(2)}, u32[]{:S(2)}) collective-permute-start(bf16[72,768]{1,0:T(8,128)(2,1)S(1)} %collective-permute-done.5.refs_6_), channel_id=1, source_target_pairs={{0,1},{1,0},{2,3},{3,2},{8,9},{9,8},{10,11},{11,10},{16,17},{17,16... | collective-permute-start | bytes 331784 | tf_op jit(solution)/shard_map/ppermute | solution.py:340
  25.4 4.7 %collective-permute-start.16 = (bf16[72,768]{1,0:T(8,128)(2,1)S(1)}, bf16[72,768]{1,0:T(8,128)(2,1)S(1)}, u32[]{:S(2)}, u32[]{:S(2)}) collective-permute-start(bf16[72,768]{1,0:T(8,128)(2,1)S(1)} %collective-permute-done.6.refs_7_), channel_id=1, source_target_pairs={{0,1},{1,0},{2,3},{3,2},{8,9},{9,8},{10,11},{11,10},{16,17},{17,16... | collective-permute-start | bytes 331784 | tf_op jit(solution)/shard_map/ppermute | solution.py:340
  28.1 6.4 %collective-permute-start.7 = (bf16[256,768]{1,0:T(8,128)(2,1)S(1)}, bf16[256,768]{1,0:T(8,128)(2,1)S(1)}, u32[]{:S(2)}, u32[]{:S(2)}) collective-permute-start(bf16[256,768]{1,0:T(8,128)(2,1)S(1)} %get-tuple-element.30), channel_id=1, source_target_pairs={{0,2},{1,3},{2,0},{3,1},{8,10},{9,11},{10,8},{11,9},{16,18},{17,19... | collective-permute-start | bytes 1179656 | tf_op jit(solution)/shard_map/ppermute | solution.py:354
  31.2 5.5 %collective-permute-start.17 = (bf16[256,768]{1,0:T(8,128)(2,1)S(1)}, bf16[256,768]{1,0:T(8,128)(2,1)S(1)}, u32[]{:S(2)}, u32[]{:S(2)}) collective-permute-start(bf16[256,768]{1,0:T(8,128)(2,1)S(1)} %get-tuple-element.35), channel_id=1, source_target_pairs={{0,2},{1,3},{2,0},{3,1},{8,10},{9,11},{10,8},{11,9},{16,18},{17,19... | collective-permute-start | bytes 1179656 | tf_op jit(solution)/shard_map/ppermute | solution.py:354
  38.9 5.2 %collective-permute-start.28 = (bf16[64,768]{1,0:T(8,128)(2,1)S(1)}, bf16[64,768]{1,0:T(8,128)(2,1)S(1)}, u32[]{:S(2)}, u32[]{:S(2)}) collective-permute-start(bf16[64,768]{1,0:T(8,128)(2,1)S(1)} %get-tuple-element.49), channel_id=1, source_target_pairs={{0,8},{1,9},{2,10},{3,11},{8,16},{9,17},{10,18},{11,19},{16,24},{1... | collective-permute-start | bytes 294920 | tf_op jit(solution)/shard_map/ppermute | solution.py:368
  41.1 8.5 %collective-permute-start.21 = (bf16[64,768]{1,0:T(8,128)(2,1)S(1)}, bf16[64,768]{1,0:T(8,128)(2,1)S(1)}, u32[]{:S(2)}, u32[]{:S(2)}) collective-permute-start(bf16[64,768]{1,0:T(8,128)(2,1)S(1)} %get-tuple-element.43), channel_id=1, source_target_pairs={{8,0},{9,1},{10,2},{11,3},{16,8},{17,9},{18,10},{19,11},{24,16},{2... | collective-permute-start | bytes 294920 | tf_op jit(solution)/shard_map/ppermute | solution.py:368
  44.1 26.1 %collective-permute-start.29 = (bf16[64,768]{1,0:T(8,128)(2,1)S(1)}, bf16[64,768]{1,0:T(8,128)(2,1)S(1)}, u32[]{:S(2)}, u32[]{:S(2)}) collective-permute-start(bf16[64,768]{1,0:T(8,128)(2,1)S(1)} %add_convert_fusion.4), channel_id=1, source_target_pairs={{0,8},{1,9},{2,10},{3,11},{8,16},{9,17},{10,18},{11,19},{16,24},{1... | collective-permute-start | bytes 294920 | tf_op jit(solution)/shard_map/ppermute | solution.py:368
  45.8 29.2 %collective-permute-start.19 = (bf16[64,768]{1,0:T(8,128)(2,1)S(1)}, bf16[64,768]{1,0:T(8,128)(2,1)S(1)}, u32[]{:S(2)}, u32[]{:S(2)}) collective-permute-start(bf16[64,768]{1,0:T(8,128)(2,1)S(1)} %get-tuple-element.38), channel_id=1, source_target_pairs={{0,1},{1,0},{2,3},{3,2},{8,9},{9,8},{10,11},{11,10},{16,17},{17,16... | collective-permute-start | bytes 294920 | tf_op jit(solution)/shard_map/ppermute | solution.py:368
  47.6 24.4 %collective-permute-start.20 = (bf16[64,768]{1,0:T(8,128)(2,1)S(1)}, bf16[64,768]{1,0:T(8,128)(2,1)S(1)}, u32[]{:S(2)}, u32[]{:S(2)}) collective-permute-start(bf16[64,768]{1,0:T(8,128)(2,1)S(1)} %get-tuple-element.40), channel_id=1, source_target_pairs={{0,1},{1,0},{2,3},{3,2},{8,9},{9,8},{10,11},{11,10},{16,17},{17,16... | collective-permute-start | bytes 294920 | tf_op jit(solution)/shard_map/ppermute | solution.py:368
  47.8 6.7 %collective-permute-start.23 = (bf16[64,768]{1,0:T(8,128)(2,1)S(1)}, bf16[64,768]{1,0:T(8,128)(2,1)S(1)}, u32[]{:S(2)}, u32[]{:S(2)}) collective-permute-start(bf16[64,768]{1,0:T(8,128)(2,1)S(1)} %get-tuple-element.46), channel_id=1, source_target_pairs={{0,1},{1,0},{2,3},{3,2},{8,9},{9,8},{10,11},{11,10},{16,17},{17,16... | collective-permute-start | bytes 294920 | tf_op jit(solution)/shard_map/ppermute | solution.py:368
  49.6 6.3 %collective-permute-start.30 = (bf16[64,768]{1,0:T(8,128)(2,1)S(1)}, bf16[64,768]{1,0:T(8,128)(2,1)S(1)}, u32[]{:S(2)}, u32[]{:S(2)}) collective-permute-start(bf16[64,768]{1,0:T(8,128)(2,1)S(1)} %get-tuple-element.52), channel_id=1, source_target_pairs={{0,8},{1,9},{2,10},{3,11},{8,16},{9,17},{10,18},{11,19},{16,24},{1... | collective-permute-start | bytes 294920 | tf_op jit(solution)/shard_map/ppermute | solution.py:368
  54.5 11.0 %collective-permute-start.22 = (bf16[64,768]{1,0:T(8,128)(2,1)S(1)}, bf16[64,768]{1,0:T(8,128)(2,1)S(1)}, u32[]{:S(2)}, u32[]{:S(2)}) collective-permute-start(bf16[64,768]{1,0:T(8,128)(2,1)S(1)} %add_convert_fusion.9), channel_id=1, source_target_pairs={{0,1},{1,0},{2,3},{3,2},{8,9},{9,8},{10,11},{11,10},{16,17},{17,16... | collective-permute-start | bytes 294920 | tf_op jit(solution)/shard_map/ppermute | solution.py:368
  (10 other events, 41.8 us)

commit v6 on v5

--- a/solution.py
+++ b/solution.py
@@ -14,64 +14,11 @@
 
 
 class Rings:
-    def __init__(self, length, clockwise, counter, mirror, partner):
-        self.length = length
-        self.perms = (clockwise, counter, mirror)
+    def __init__(self, ring, mirror, partner):
+        self.ring = ring
+        self.back = [(b, a) for a, b in ring]
+        self.mirror = mirror
         self.partner = partner
-
-
-def wrap(step, length):
-    step %= length
-    return step - length if step > length // 2 else step
-
-
-def seen_from_source(channel, block, length):
-    step, plane = block
-    if channel == 0:
-        return (wrap(step + 1, length), plane)
-    if channel == 1:
-        return (wrap(step - 1, length), plane)
-    return (step, 1 - plane)
-
-
-def gather_sequence():
-    return (
-        (0, (-1, 0)),
-        (1, (1, 0)),
-        (2, (0, 1)),
-        (0, (-2, 0)),
-        (1, (2, 0)),
-        (2, (1, 1)),
-        (0, (-3, 0)),
-        (1, (3, 0)),
-        (2, (-2, 1)),
-        (0, (4, 0)),
-        (1, (2, 1)),
-        (0, (-3, 1)),
-        (2, (-1, 1)),
-        (2, (4, 1)),
-        (2, (3, 1)),
-    )
-
-
-def return_sequence():
-    return (
-        (2, (4, 1)),
-        (0, (-3, 1)),
-        (1, (3, 1)),
-        (2, (0, 1)),
-        (0, (4, 0)),
-        (2, (-2, 1)),
-        (1, (2, 1)),
-        (0, (-3, 0)),
-        (1, (3, 0)),
-        (2, (-1, 1)),
-        (0, (-2, 0)),
-        (1, (2, 0)),
-        (2, (1, 1)),
-        (0, (-1, 0)),
-        (1, (1, 0)),
-    )
 
 
 def find_rings(mesh):
@@ -115,20 +62,19 @@
         return None
     if any(place[(c, k)][0] != place[(mirrored(c), k)][0] for c in order for k in range(2)):
         return None
-    clockwise, counter, mirror, partner = [], [], [], []
+    ring, mirror, partner = [], [], []
     for here in range(length):
         after = (here + 1) % length
         for core in range(2):
             for turn in (lambda c: c, mirrored):
                 a, b = index(turn(order[here]), core), index(turn(order[after]), core)
-                clockwise.append((a, b))
-                counter.append((b, a))
+                ring.append((b, a) if core else (a, b))
                 partner.append((a, index(turn(order[here]), 1 - core)))
             a, b = index(order[here], core), index(mirrored(order[here]), core)
             mirror += [(a, b), (b, a)]
     if any(mate != one ^ n_dev for one, mate in partner):
         return None
-    return Rings(length, clockwise, counter, mirror, partner)
+    return Rings(ring, mirror, partner)
 
 
 def pack_kernel(ids_hbm, gates_hbm, tokens_hbm, out_ref, ids_ref, gates_ref, sem, *, experts):
@@ -178,14 +124,16 @@
     return jnp.where(seats == seat, 1.0, 0.0)
 
 
-def select_kernel(*refs, blocks, count, cap, stride):
+def select_kernel(*refs, count, cap, stride):
     here = lax.axis_index("grp") * stride + lax.axis_index("dev")
     mate = here ^ stride
-    block_refs = refs[:blocks]
     own_ref, other_ref, seat_ref, gate_ref = refs[-4:]
+    each = count + SUB
+    pieces = [(r, at) for r in refs[:-4] for at in range(0, r.shape[0], each)]
+    blocks = len(pieces)
     pairs = blocks // 2
     dot = functools.partial(jnp.dot, preferred_element_type=jnp.float32)
-    tails = jnp.concatenate([r[count:, :] for r in block_refs], axis=0)
+    tails = jnp.concatenate([r[at + count : at + each, :] for r, at in pieces], axis=0)
     upper = (
         lax.broadcasted_iota(jnp.int32, (LANES, LANES), 0)
         < lax.broadcasted_iota(jnp.int32, (LANES, LANES), 1)
@@ -197,7 +145,7 @@
     row_of = lax.broadcasted_iota(jnp.int32, (pairs, blocks * SUB), 0)
     col_of = lax.broadcasted_iota(jnp.int32, (pairs, blocks * SUB), 1)
     groups = tails.shape[1] // LANES
-    rows = jnp.concatenate([r[:count, :] for r in block_refs], axis=0)
+    rows = jnp.concatenate([r[at : at + count, :] for r, at in pieces], axis=0)
     picks = []
     for expert in (here, mate):
         sub = expert % SUB
@@ -226,12 +174,11 @@
 
 def select(blocks, count, cap, stride):
     width = blocks[0].shape[1]
-    pairs = len(blocks) // 2
+    pairs = sum(b.shape[0] for b in blocks) // (2 * (count + SUB))
     taken = jax.ShapeDtypeStruct((cap, width), jnp.bfloat16)
-    vmem = pl.BlockSpec(memory_space=pltpu.VMEM)
     return pl.pallas_call(
-        functools.partial(select_kernel, blocks=len(blocks), count=count, cap=cap, stride=stride),
-        in_specs=[vmem] * len(blocks),
+        functools.partial(select_kernel, count=count, cap=cap, stride=stride),
+        in_specs=[pl.BlockSpec(memory_space=pltpu.VMEM)] * len(blocks),
         out_shape=[
             taken,
             taken,
@@ -271,29 +218,26 @@
     )(pltpu.with_memory_space_constraint(weights, pltpu.HBM))
 
 
-def expert_kernel(own_ref, came_ref, in_a, out_a, out_ref):
-    dot = functools.partial(jnp.dot, preferred_element_type=jnp.float32)
+def expert_kernel(own_ref, came_ref, first_ref, second_ref, out_ref):
     rows = own_ref[...] + came_ref[...]
-    result = None
-    for first, second in ((in_a, out_a),):
-        hidden = jnp.maximum(dot(rows, first[...]), 0.0).astype(jnp.bfloat16)
-        part = dot(hidden, second[...])
-        result = part if result is None else result + part
+    hidden = jnp.dot(rows, first_ref[...], preferred_element_type=jnp.float32)
+    hidden = jnp.maximum(hidden, 0.0).astype(jnp.bfloat16)
+    result = jnp.dot(hidden, second_ref[...], preferred_element_type=jnp.float32)
     out_ref[...] = result.astype(jnp.bfloat16)
 
 
-def expert(own, came, weights):
+def expert(own, came, first, second):
     vmem = pl.BlockSpec(memory_space=pltpu.VMEM)
     return pl.pallas_call(
         expert_kernel,
-        in_specs=[vmem] * (2 + len(weights)),
+        in_specs=[vmem] * 4,
         out_shape=jax.ShapeDtypeStruct(own.shape, jnp.bfloat16),
         name="expert",
         compiler_params=pltpu.CompilerParams(vmem_limit_bytes=16 * MIB),
-    )(own, came, *weights)
-
-
-def spread_kernel(own_ref, came_ref, seat_ref, gate_ref, *out_refs, count, cap):
+    )(own, came, first, second)
+
+
+def spread_kernel(own_ref, came_ref, seat_ref, gate_ref, *out_refs, cap):
     pairs = seat_ref.shape[1]
     value = None
     for k, ref in enumerate((own_ref, came_ref)):
@@ -309,20 +253,27 @@
         )
         value = part if value is None else value + part
     value = value.astype(jnp.bfloat16)
-    for o, out_ref in enumerate(out_refs):
-        out_ref[...] = value[o * count : (o + 1) * count, :]
-
-
-def spread(own, came, seat, gate, count):
-    blocks = 2 * seat.shape[1]
+    at = 0
+    for out_ref in out_refs:
+        out_ref[...] = value[at : at + out_ref.shape[0], :]
+        at += out_ref.shape[0]
+
+
+def spread(own, came, seat, gate, sizes):
     cap, width = own.shape
-    out = jax.ShapeDtypeStruct((count, width), jnp.bfloat16)
     return pl.pallas_call(
-        functools.partial(spread_kernel, count=count, cap=cap),
-        out_shape=[out] * blocks,
+        functools.partial(spread_kernel, cap=cap),
+        out_shape=[jax.ShapeDtypeStruct((size, width), jnp.bfloat16) for size in sizes],
         name="spread",
         compiler_params=pltpu.CompilerParams(vmem_limit_bytes=12 * MIB),
     )(own, came, seat, gate)
+
+
+def total(*values):
+    result = values[0].astype(jnp.float32)
+    for more in values[1:]:
+        result = result + more.astype(jnp.float32)
+    return result.astype(jnp.bfloat16)
 
 
 def on_rings(rings, tokens, expert_ids, gates, w_in, w_out):
@@ -330,44 +281,51 @@
     n_dev = lax.axis_size("dev")
     experts = lax.axis_size("grp") * n_dev
     count, width = tokens.shape
-    length = rings.length
-    if 2 * count != LANES or length % 4 or experts % SUB or experts * LANES > SUB * width:
+    if 2 * count != LANES or experts % SUB or experts * LANES > SUB * width:
         return per_device(tokens, expert_ids, gates, w_in, w_out)
-    inverse = (rings.perms[1], rings.perms[0], rings.perms[2])
-    held = {(0, 0): pack(expert_ids, gates, tokens, experts)}
-    for channel, block in gather_sequence():
-        source = held[seen_from_source(channel, block, length)]
-        held[block] = lax.ppermute(source, axes, rings.perms[channel])
-    order = sorted(held, key=lambda b: (b[1], b[0]))
+
+    def send(value, pairs):
+        return lax.ppermute(value, axes, pairs)
+
+    own = pack(expert_ids, gates, tokens, experts)
+    half = own.shape[0]
+    swapped = send(own, rings.partner)
+    y0 = send(own, rings.mirror)
+    r1 = send(jnp.concatenate([own, swapped], axis=0), rings.ring)
+    y1 = send(r1, rings.mirror)
+    r2 = send(r1, rings.ring)
+    y2 = send(r2, rings.mirror)
+    r3 = send(r2, rings.ring)
+    r4 = send(r3[:half], rings.ring)
+    y4 = send(r4, rings.mirror)
+    y3 = send(y2, rings.ring)
+
+    units = w_in.shape[2]
+    first = load(w_in, (0, 0), (width, units))
+    second = load(w_out, (0, 0), (units, width))
     cap = 4 * count
-    units = w_in.shape[2]
-    weights = []
-    for array, at, shape in (
-        (w_in, (0, 0), (width, units)),
-        (w_out, (0, 0), (units, width)),
-    ):
-        weights.append(load(array, at, shape))
-    parts = {}
-    for plane in range(2):
-        blocks = order[plane * length : (plane + 1) * length]
-        own, other, seat, gate = select([held[b] for b in blocks], count, cap, n_dev)
-        came = lax.ppermute(other, axes, rings.partner)
-        result = expert(own, came, weights)
-        theirs = lax.ppermute(result, axes, rings.partner)
-        sums = spread(result, theirs, seat, gate, count)
-        for block, value in zip(blocks, sums, strict=True):
-            parts[block] = [value]
-
-    def total(block):
-        value = parts[block][0].astype(jnp.float32)
-        for more in parts[block][1:]:
-            value = value + more.astype(jnp.float32)
-        return value.astype(jnp.bfloat16)
-
-    for channel, block in return_sequence():
-        value = lax.ppermute(total(block), axes, inverse[channel])
-        parts[seen_from_source(channel, block, length)].append(value)
-    return total((0, 0))
+    sizes = (count, count, 2 * count, 2 * count, 2 * count)
+    sums = []
+    for blocks in ((own, r4, r1, r2, r3), (y0, y4, y1, y2, y3)):
+        mine, other, seat, gate = select(blocks, count, cap, n_dev)
+        came = send(other, rings.partner)
+        result = expert(mine, came, first, second)
+        theirs = send(result, rings.partner)
+        sums.append(spread(result, theirs, seat, gate, sizes))
+    (s0, s4, s1, s2, s3), (t0, t4, t1, t2, t3) = sums
+
+    from_y3 = send(t3, rings.back)
+    from_y4 = send(t4, rings.mirror)
+    from_y2 = send(total(t2, from_y3), rings.mirror)
+    from_r4 = send(total(s4, from_y4), rings.back)
+    s3 = jnp.concatenate([total(s3[:count], from_r4), s3[count:]], axis=0)
+    from_r3 = send(s3, rings.back)
+    from_y1 = send(t1, rings.mirror)
+    from_r2 = send(total(s2, from_r3, from_y2), rings.back)
+    from_y0 = send(t0, rings.mirror)
+    from_r1 = send(total(s1, from_r2, from_y1), rings.back)
+    swapped = send(from_r1[count:], rings.partner)
+    return total(s0, from_y0, from_r1[:count], swapped)
 
 
 def earlier_count(onehot):

time: 80.1 us -> 76.4 us (0.954)
  starting transfers between devices: 36.8 us -> 25.4 us
  waiting for transfers between devices: 31.6 us -> 39.2 us
    ppermute x34 -> x24, starting transfers between devices: 36.8 us -> 25.4 us  [send(): return lax.ppermute(value, axes, pairs)]
    ppermute x34 -> x24, waiting for transfers between devices: 31.6 us -> 39.2 us  [send(): return lax.ppermute(value, axes, pairs)]
  transfers between devices with their start and end apart: 34 -> 24, of which waited for: 12 -> 16; matrix products, arithmetic and copies ran while one was open for 0% -> 0% of each run, Pallas kernels for 12% -> 11%
where the time goes in v6:
time: 76.4 us; the launch traced here: 76.2 us
  waiting for transfers between devices  39.2 us (51%)
  starting transfers between devices  25.4 us (33%)
  Pallas kernels  10.4 us (14%)
  other arithmetic  1 us (1%)
    ppermute x24, waiting for transfers between devices, send(): return lax.ppermute(value, axes, pairs)  39.2 us
    ppermute x24, starting transfers between devices, send(): return lax.ppermute(value, axes, pairs)  25.4 us
    pallas_call x2, Pallas kernels, load(): pl.pallas_call(functools.partial(load_kernel, at=at), in_specs=[pl.BlockS...  3.31 us
    pallas_call x2, Pallas kernels, expert(): pl.pallas_call(expert_kernel, in_specs=[vmem] * 4, out_shape=jax.ShapeDty...  3.04 us
    pallas_call x2, Pallas kernels, select(): pl.pallas_call(functools.partial(select_kernel, count=count, cap=cap, str...  1.9 us
  transfers between devices with their start and end apart: 24, of which 16 were waited for; matrix products, arithmetic and copies ran while one was open for 0% of the time, Pallas kernels for 11%

profile of v6, /device:TPU:0, one launch (start us, length us, event | category | flops | bytes accessed | tf_op | source)
XLA Modules:
  0.0 76.2 jit_solution(13716632886514170746)
XLA Ops:
  2.5 3.0 %collective-permute-start.1 = (bf16[144,768]{1,0:T(8,128)(2,1)S(1)}, bf16[144,768]{1,0:T(8,128)(2,1)S(1)}, u32[]{:S(2)}, u32[]{:S(2)}) collective-permute-start(bf16[144,768]{1,0:T(8,128)(2,1)S(1)} %pad_maximum_fusion), channel_id=1, source_target_pairs={{0,8},{1,9},{10,2},{11,3},{8,16},{9,17},{18,10},{19,11},{16,24},{1... | collective-permute-start | bytes 663560 | tf_op jit(solution)/shard_map/ppermute | solution.py:288
  5.4 3.8 %collective-permute-done.1.refs_2_ = bf16[144,768]{1,0:T(8,128)(2,1)S(1)} collective-permute-done((bf16[144,768]{1,0:T(8,128)(2,1)S(1)}, bf16[144,768]{1,0:T(8,128)(2,1)S(1)}, u32[]{:S(2)}, u32[]{:S(2)}) %collective-permute-start.1) | collective-permute-done | bytes 221216 | tf_op jit(solution)/shard_map/ppermute | solution.py:288
  9.3 2.1 %collective-permute-start.2 = (bf16[144,768]{1,0:T(8,128)(2,1)S(1)}, bf16[144,768]{1,0:T(8,128)(2,1)S(1)}, u32[]{:S(2)}, u32[]{:S(2)}) collective-permute-start(bf16[144,768]{1,0:T(8,128)(2,1)S(1)} %collective-permute-done.1.refs_2_), channel_id=1, source_target_pairs={{0,8},{1,9},{10,2},{11,3},{8,16},{9,17},{18,10},{19,11},{16,24},{1... | collective-permute-start | bytes 663560 | tf_op jit(solution)/shard_map/ppermute | solution.py:288
  11.4 3.8 %collective-permute-done.2.refs_3_ = bf16[144,768]{1,0:T(8,128)(2,1)S(1)} collective-permute-done((bf16[144,768]{1,0:T(8,128)(2,1)S(1)}, bf16[144,768]{1,0:T(8,128)(2,1)S(1)}, u32[]{:S(2)}, u32[]{:S(2)}) %collective-permute-start.2) | collective-permute-done | bytes 221216 | tf_op jit(solution)/shard_map/ppermute | solution.py:288
  15.2 2.1 %collective-permute-start.3 = (bf16[144,768]{1,0:T(8,128)(2,1)S(1)}, bf16[144,768]{1,0:T(8,128)(2,1)S(1)}, u32[]{:S(2)}, u32[]{:S(2)}) collective-permute-start(bf16[144,768]{1,0:T(8,128)(2,1)S(1)} %collective-permute-done.2.refs_3_), channel_id=1, source_target_pairs={{0,8},{1,9},{10,2},{11,3},{8,16},{9,17},{18,10},{19,11},{16,24},{1... | collective-permute-start | bytes 663560 | tf_op jit(solution)/shard_map/ppermute | solution.py:288
  17.3 1.5 %collective-permute-start.10 = (bf16[144,768]{1,0:T(8,128)(2,1)S(1)}, bf16[144,768]{1,0:T(8,128)(2,1)S(1)}, u32[]{:S(2)}, u32[]{:S(2)}) collective-permute-start(bf16[144,768]{1,0:T(8,128)(2,1)S(1)} %collective-permute-done.2.refs_3_), channel_id=1, source_target_pairs={{0,1},{1,0},{2,3},{3,2},{8,9},{9,8},{10,11},{11,10},{16,17},{17,16... | collective-permute-start | bytes 663560 | tf_op jit(solution)/shard_map/ppermute | solution.py:288
  19.3 1.8 %collective-permute-done.3.refs_4_ = bf16[144,768]{1,0:T(8,128)(2,1)S(1)} collective-permute-done((bf16[144,768]{1,0:T(8,128)(2,1)S(1)}, bf16[144,768]{1,0:T(8,128)(2,1)S(1)}, u32[]{:S(2)}, u32[]{:S(2)}) %collective-permute-start.3) | collective-permute-done | bytes 221216 | tf_op jit(solution)/shard_map/ppermute | solution.py:288
  21.1 2.2 %collective-permute-start.4 = (bf16[72,768]{1,0:T(8,128)(2,1)S(1)}, bf16[72,768]{1,0:T(8,128)(2,1)S(1)}, u32[]{:S(2)}, u32[]{:S(2)}) collective-permute-start(bf16[72,768]{1,0:T(8,128)(2,1)S(1)} %slice.20), channel_id=1, source_target_pairs={{0,8},{1,9},{10,2},{11,3},{8,16},{9,17},{18,10},{19,11},{16,24},{1... | collective-permute-start | bytes 331784 | tf_op jit(solution)/shard_map/ppermute | solution.py:288
  23.3 1.8 %collective-permute-done.10.refs_3_ = bf16[144,768]{1,0:T(8,128)(2,1)S(1)} collective-permute-done((bf16[144,768]{1,0:T(8,128)(2,1)S(1)}, bf16[144,768]{1,0:T(8,128)(2,1)S(1)}, u32[]{:S(2)}, u32[]{:S(2)}) %collective-permute-start.10) | collective-permute-done | bytes 221216 | tf_op jit(solution)/shard_map/ppermute | solution.py:288
  26.1 1.8 %collective-permute-start.7 = (bf16[72,768]{1,0:T(8,128)(2,1)S(1)}, bf16[72,768]{1,0:T(8,128)(2,1)S(1)}, u32[]{:S(2)}, u32[]{:S(2)}) collective-permute-start(bf16[72,768]{1,0:T(8,128)(2,1)S(1)} %pack.1.refs_0_), channel_id=1, source_target_pairs={{0,1},{1,0},{2,3},{3,2},{8,9},{9,8},{10,11},{11,10},{16,17},{17,16... | collective-permute-start | bytes 331784 | tf_op jit(solution)/shard_map/ppermute | solution.py:288
  28.1 2.9 %collective-permute-done.7.refs_0_ = bf16[72,768]{1,0:T(8,128)(2,1)S(1)} collective-permute-done((bf16[72,768]{1,0:T(8,128)(2,1)S(1)}, bf16[72,768]{1,0:T(8,128)(2,1)S(1)}, u32[]{:S(2)}, u32[]{:S(2)}) %collective-permute-start.7) | collective-permute-done | bytes 110624 | tf_op jit(solution)/shard_map/ppermute | solution.py:288
  31.0 1.7 %collective-permute-done.8.refs_1_ = bf16[72,768]{1,0:T(8,128)(2,1)S(1)} collective-permute-done((bf16[72,768]{1,0:T(8,128)(2,1)S(1)}, bf16[72,768]{1,0:T(8,128)(2,1)S(1)}, u32[]{:S(2)}, u32[]{:S(2)}) %collective-permute-start.8) | collective-permute-done | bytes 110624 | tf_op jit(solution)/shard_map/ppermute | solution.py:288
  35.3 1.7 %load.2.first_ref = bf16[768,1536]{1,0:T(8,128)(2,1)S(1)} custom-call(bf16[1,768,1536]{2,1,0:T(8,128)(2,1)} %source.2), custom_call_target="tpu_custom_call" | custom-call | tf_op jit(solution)/shard_map/load/pallas_call | solution.py:211
  36.9 1.7 %load.3.second_ref = bf16[1536,768]{1,0:T(8,128)(2,1)S(1)} custom-call(bf16[1,1536,768]{2,1,0:T(8,128)(2,1)} %source.3), custom_call_target="tpu_custom_call" | custom-call | tf_op jit(solution)/shard_map/load/pallas_call | solution.py:211
  38.6 1.5 %expert.3.own_ref = bf16[256,768]{1,0:T(8,128)(2,1)S(1)} custom-call(bf16[256,768]{1,0:T(8,128)(2,1)S(1)} %get-tuple-element.28.own_ref, bf16[256,768]{1,0:T(8,128)(2,1)S(1)} %collective-permute-done.12.came_ref, bf16[768,1536]{1,0:T(8,128)(2,1)S(1)} %load.2.first_ref, bf16[1536,768]{1,0:T(8,128)(2,1)S(1)} %load.3.second_ref), custom_call_target="tpu_custom_call" | custom-call | tf_op jit(solution)/shard_map/expert/pallas_call | solution.py:231
  44.8 2.9 %collective-permute-done.15 = bf16[64,768]{1,0:T(8,128)(2,1)S(1)} collective-permute-done((bf16[64,768]{1,0:T(8,128)(2,1)S(1)}, bf16[64,768]{1,0:T(8,128)(2,1)S(1)}, u32[]{:S(2)}, u32[]{:S(2)}) %collective-permute-start.15) | collective-permute-done | bytes 98336 | tf_op jit(solution)/shard_map/ppermute | solution.py:288
  48.9 1.6 %collective-permute-start.18 = (bf16[128,768]{1,0:T(8,128)(2,1)S(1)}, bf16[128,768]{1,0:T(8,128)(2,1)S(1)}, u32[]{:S(2)}, u32[]{:S(2)}) collective-permute-start(bf16[128,768]{1,0:T(8,128)(2,1)S(1)} %get-tuple-element.39), channel_id=1, source_target_pairs={{8,0},{9,1},{2,10},{3,11},{16,8},{17,9},{10,18},{11,19},{24,16},{2... | collective-permute-start | bytes 589832 | tf_op jit(solution)/shard_map/ppermute | solution.py:288
  50.5 1.9 %collective-permute-done.16 = bf16[64,768]{1,0:T(8,128)(2,1)S(1)} collective-permute-done((bf16[64,768]{1,0:T(8,128)(2,1)S(1)}, bf16[64,768]{1,0:T(8,128)(2,1)S(1)}, u32[]{:S(2)}, u32[]{:S(2)}) %collective-permute-start.16) | collective-permute-done | bytes 98336 | tf_op jit(solution)/shard_map/ppermute | solution.py:288
  54.6 1.6 %collective-permute-start.19 = (bf16[128,768]{1,0:T(8,128)(2,1)S(1)}, bf16[128,768]{1,0:T(8,128)(2,1)S(1)}, u32[]{:S(2)}, u32[]{:S(2)}) collective-permute-start(bf16[128,768]{1,0:T(8,128)(2,1)S(1)} %add_convert_fusion.2), channel_id=1, source_target_pairs={{0,1},{1,0},{2,3},{3,2},{8,9},{9,8},{10,11},{11,10},{16,17},{17,16... | collective-permute-start | bytes 589832 | tf_op jit(solution)/shard_map/ppermute | solution.py:288
  58.2 4.3 %collective-permute-done.19 = bf16[128,768]{1,0:T(8,128)(2,1)S(1)} collective-permute-done((bf16[128,768]{1,0:T(8,128)(2,1)S(1)}, bf16[128,768]{1,0:T(8,128)(2,1)S(1)}, u32[]{:S(2)}, u32[]{:S(2)}) %collective-permute-start.19) | collective-permute-done | bytes 196640 | tf_op jit(solution)/shard_map/ppermute | solution.py:288
  62.8 1.9 %collective-permute-done.21 = bf16[128,768]{1,0:T(8,128)(2,1)S(1)} collective-permute-done((bf16[128,768]{1,0:T(8,128)(2,1)S(1)}, bf16[128,768]{1,0:T(8,128)(2,1)S(1)}, u32[]{:S(2)}, u32[]{:S(2)}) %collective-permute-start.21) | collective-permute-done | bytes 196640 | tf_op jit(solution)/shard_map/ppermute | solution.py:288
  64.6 3.6 %collective-permute-done.20 = bf16[128,768]{1,0:T(8,128)(2,1)S(1)} collective-permute-done((bf16[128,768]{1,0:T(8,128)(2,1)S(1)}, bf16[128,768]{1,0:T(8,128)(2,1)S(1)}, u32[]{:S(2)}, u32[]{:S(2)}) %collective-permute-start.20) | collective-permute-done | bytes 196640 | tf_op jit(solution)/shard_map/ppermute | solution.py:288
  68.6 1.5 %collective-permute-start.14 = (bf16[64,768]{1,0:T(8,128)(2,1)S(1)}, bf16[64,768]{1,0:T(8,128)(2,1)S(1)}, u32[]{:S(2)}, u32[]{:S(2)}) collective-permute-start(bf16[64,768]{1,0:T(8,128)(2,1)S(1)} %get-tuple-element.32), channel_id=1, source_target_pairs={{0,1},{1,0},{2,3},{3,2},{8,9},{9,8},{10,11},{11,10},{16,17},{17,16... | collective-permute-start | bytes 294920 | tf_op jit(solution)/shard_map/ppermute | solution.py:288
  70.1 4.0 %collective-permute-done.22 = bf16[128,768]{1,0:T(8,128)(2,1)S(1)} collective-permute-done((bf16[128,768]{1,0:T(8,128)(2,1)S(1)}, bf16[128,768]{1,0:T(8,128)(2,1)S(1)}, u32[]{:S(2)}, u32[]{:S(2)}) %collective-permute-start.22) | collective-permute-done | bytes 196640 | tf_op jit(solution)/shard_map/ppermute | solution.py:288
  (44 shorter events, 19.3 us)
Async XLA Ops:
  0.9 1.5 %collective-permute-start = (bf16[72,768]{1,0:T(8,128)(2,1)S(1)}, bf16[72,768]{1,0:T(8,128)(2,1)S(1)}, u32[]{:S(2)}, u32[]{:S(2)}) collective-permute-start(bf16[72,768]{1,0:T(8,128)(2,1)S(1)} %pack.1.refs_0_), channel_id=1, source_target_pairs={{0,2},{1,3},{2,0},{3,1},{8,10},{9,11},{10,8},{11,9},{16,18},{17,19... | collective-permute-start | bytes 331784 | tf_op jit(solution)/shard_map/ppermute | solution.py:288
  2.5 6.8 %collective-permute-start.1 = (bf16[144,768]{1,0:T(8,128)(2,1)S(1)}, bf16[144,768]{1,0:T(8,128)(2,1)S(1)}, u32[]{:S(2)}, u32[]{:S(2)}) collective-permute-start(bf16[144,768]{1,0:T(8,128)(2,1)S(1)} %pad_maximum_fusion), channel_id=1, source_target_pairs={{0,8},{1,9},{10,2},{11,3},{8,16},{9,17},{18,10},{19,11},{16,24},{1... | collective-permute-start | bytes 663560 | tf_op jit(solution)/shard_map/ppermute | solution.py:288
  9.3 5.9 %collective-permute-start.2 = (bf16[144,768]{1,0:T(8,128)(2,1)S(1)}, bf16[144,768]{1,0:T(8,128)(2,1)S(1)}, u32[]{:S(2)}, u32[]{:S(2)}) collective-permute-start(bf16[144,768]{1,0:T(8,128)(2,1)S(1)} %collective-permute-done.1.refs_2_), channel_id=1, source_target_pairs={{0,8},{1,9},{10,2},{11,3},{8,16},{9,17},{18,10},{19,11},{16,24},{1... | collective-permute-start | bytes 663560 | tf_op jit(solution)/shard_map/ppermute | solution.py:288
  15.2 5.9 %collective-permute-start.3 = (bf16[144,768]{1,0:T(8,128)(2,1)S(1)}, bf16[144,768]{1,0:T(8,128)(2,1)S(1)}, u32[]{:S(2)}, u32[]{:S(2)}) collective-permute-start(bf16[144,768]{1,0:T(8,128)(2,1)S(1)} %collective-permute-done.2.refs_3_), channel_id=1, source_target_pairs={{0,8},{1,9},{10,2},{11,3},{8,16},{9,17},{18,10},{19,11},{16,24},{1... | collective-permute-start | bytes 663560 | tf_op jit(solution)/shard_map/ppermute | solution.py:288
  17.3 7.8 %collective-permute-start.10 = (bf16[144,768]{1,0:T(8,128)(2,1)S(1)}, bf16[144,768]{1,0:T(8,128)(2,1)S(1)}, u32[]{:S(2)}, u32[]{:S(2)}) collective-permute-start(bf16[144,768]{1,0:T(8,128)(2,1)S(1)} %collective-permute-done.2.refs_3_), channel_id=1, source_target_pairs={{0,1},{1,0},{2,3},{3,2},{8,9},{9,8},{10,11},{11,10},{16,17},{17,16... | collective-permute-start | bytes 663560 | tf_op jit(solution)/shard_map/ppermute | solution.py:288
  18.8 12.2 %collective-permute-start.9 = (bf16[144,768]{1,0:T(8,128)(2,1)S(1)}, bf16[144,768]{1,0:T(8,128)(2,1)S(1)}, u32[]{:S(2)}, u32[]{:S(2)}) collective-permute-start(bf16[144,768]{1,0:T(8,128)(2,1)S(1)} %collective-permute-done.1.refs_2_), channel_id=1, source_target_pairs={{0,1},{1,0},{2,3},{3,2},{8,9},{9,8},{10,11},{11,10},{16,17},{17,16... | collective-permute-start | bytes 663560 | tf_op jit(solution)/shard_map/ppermute | solution.py:288
  21.1 6.8 %collective-permute-start.4 = (bf16[72,768]{1,0:T(8,128)(2,1)S(1)}, bf16[72,768]{1,0:T(8,128)(2,1)S(1)}, u32[]{:S(2)}, u32[]{:S(2)}) collective-permute-start(bf16[72,768]{1,0:T(8,128)(2,1)S(1)} %slice.20), channel_id=1, source_target_pairs={{0,8},{1,9},{10,2},{11,3},{8,16},{9,17},{18,10},{19,11},{16,24},{1... | collective-permute-start | bytes 331784 | tf_op jit(solution)/shard_map/ppermute | solution.py:288
  25.1 5.9 %collective-permute-start.11 = (bf16[144,768]{1,0:T(8,128)(2,1)S(1)}, bf16[144,768]{1,0:T(8,128)(2,1)S(1)}, u32[]{:S(2)}, u32[]{:S(2)}) collective-permute-start(bf16[144,768]{1,0:T(8,128)(2,1)S(1)} %collective-permute-done.10.refs_3_), channel_id=1, source_target_pairs={{0,8},{1,9},{10,2},{11,3},{8,16},{9,17},{18,10},{19,11},{16,24},{1... | collective-permute-start | bytes 663560 | tf_op jit(solution)/shard_map/ppermute | solution.py:288
  26.1 4.9 %collective-permute-start.7 = (bf16[72,768]{1,0:T(8,128)(2,1)S(1)}, bf16[72,768]{1,0:T(8,128)(2,1)S(1)}, u32[]{:S(2)}, u32[]{:S(2)}) collective-permute-start(bf16[72,768]{1,0:T(8,128)(2,1)S(1)} %pack.1.refs_0_), channel_id=1, source_target_pairs={{0,1},{1,0},{2,3},{3,2},{8,9},{9,8},{10,11},{11,10},{16,17},{17,16... | collective-permute-start | bytes 331784 | tf_op jit(solution)/shard_map/ppermute | solution.py:288
  28.0 4.7 %collective-permute-start.8 = (bf16[72,768]{1,0:T(8,128)(2,1)S(1)}, bf16[72,768]{1,0:T(8,128)(2,1)S(1)}, u32[]{:S(2)}, u32[]{:S(2)}) collective-permute-start(bf16[72,768]{1,0:T(8,128)(2,1)S(1)} %collective-permute-done.4.refs_1_), channel_id=1, source_target_pairs={{0,1},{1,0},{2,3},{3,2},{8,9},{9,8},{10,11},{11,10},{16,17},{17,16... | collective-permute-start | bytes 331784 | tf_op jit(solution)/shard_map/ppermute | solution.py:288
  33.7 4.9 %collective-permute-start.12 = (bf16[256,768]{1,0:T(8,128)(2,1)S(1)}, bf16[256,768]{1,0:T(8,128)(2,1)S(1)}, u32[]{:S(2)}, u32[]{:S(2)}) collective-permute-start(bf16[256,768]{1,0:T(8,128)(2,1)S(1)} %get-tuple-element.29), channel_id=1, source_target_pairs={{0,2},{1,3},{2,0},{3,1},{8,10},{9,11},{10,8},{11,9},{16,18},{17,19... | collective-permute-start | bytes 1179656 | tf_op jit(solution)/shard_map/ppermute | solution.py:288
  34.7 5.5 %collective-permute-start.5 = (bf16[256,768]{1,0:T(8,128)(2,1)S(1)}, bf16[256,768]{1,0:T(8,128)(2,1)S(1)}, u32[]{:S(2)}, u32[]{:S(2)}) collective-permute-start(bf16[256,768]{1,0:T(8,128)(2,1)S(1)} %get-tuple-element.24), channel_id=1, source_target_pairs={{0,2},{1,3},{2,0},{3,1},{8,10},{9,11},{10,8},{11,9},{16,18},{17,19... | collective-permute-start | bytes 1179656 | tf_op jit(solution)/shard_map/ppermute | solution.py:288
  40.1 2.2 %collective-permute-start.13 = (bf16[256,768]{1,0:T(8,128)(2,1)S(1)}, bf16[256,768]{1,0:T(8,128)(2,1)S(1)}, u32[]{:S(2)}, u32[]{:S(2)}) collective-permute-start(bf16[256,768]{1,0:T(8,128)(2,1)S(1)} %expert.3.own_ref), channel_id=1, source_target_pairs={{0,2},{1,3},{2,0},{3,1},{8,10},{9,11},{10,8},{11,9},{16,18},{17,19... | collective-permute-start | bytes 1179656 | tf_op jit(solution)/shard_map/ppermute | solution.py:288
  41.7 2.4 %collective-permute-start.6 = (bf16[256,768]{1,0:T(8,128)(2,1)S(1)}, bf16[256,768]{1,0:T(8,128)(2,1)S(1)}, u32[]{:S(2)}, u32[]{:S(2)}) collective-permute-start(bf16[256,768]{1,0:T(8,128)(2,1)S(1)} %expert.2.own_ref), channel_id=1, source_target_pairs={{0,2},{1,3},{2,0},{3,1},{8,10},{9,11},{10,8},{11,9},{16,18},{17,19... | collective-permute-start | bytes 1179656 | tf_op jit(solution)/shard_map/ppermute | solution.py:288
  42.9 4.8 %collective-permute-start.15 = (bf16[64,768]{1,0:T(8,128)(2,1)S(1)}, bf16[64,768]{1,0:T(8,128)(2,1)S(1)}, u32[]{:S(2)}, u32[]{:S(2)}) collective-permute-start(bf16[64,768]{1,0:T(8,128)(2,1)S(1)} %get-tuple-element.37), channel_id=1, source_target_pairs={{0,1},{1,0},{2,3},{3,2},{8,9},{9,8},{10,11},{11,10},{16,17},{17,16... | collective-permute-start | bytes 294920 | tf_op jit(solution)/shard_map/ppermute | solution.py:288
  47.7 4.7 %collective-permute-start.16 = (bf16[64,768]{1,0:T(8,128)(2,1)S(1)}, bf16[64,768]{1,0:T(8,128)(2,1)S(1)}, u32[]{:S(2)}, u32[]{:S(2)}) collective-permute-start(bf16[64,768]{1,0:T(8,128)(2,1)S(1)} %add_convert_fusion.5), channel_id=1, source_target_pairs={{8,0},{9,1},{2,10},{3,11},{16,8},{17,9},{10,18},{11,19},{24,16},{2... | collective-permute-start | bytes 294920 | tf_op jit(solution)/shard_map/ppermute | solution.py:288
  48.9 5.7 %collective-permute-start.18 = (bf16[128,768]{1,0:T(8,128)(2,1)S(1)}, bf16[128,768]{1,0:T(8,128)(2,1)S(1)}, u32[]{:S(2)}, u32[]{:S(2)}) collective-permute-start(bf16[128,768]{1,0:T(8,128)(2,1)S(1)} %get-tuple-element.39), channel_id=1, source_target_pairs={{8,0},{9,1},{2,10},{3,11},{16,8},{17,9},{10,18},{11,19},{24,16},{2... | collective-permute-start | bytes 589832 | tf_op jit(solution)/shard_map/ppermute | solution.py:288
  52.5 5.7 %collective-permute-start.17 = (bf16[128,768]{1,0:T(8,128)(2,1)S(1)}, bf16[128,768]{1,0:T(8,128)(2,1)S(1)}, u32[]{:S(2)}, u32[]{:S(2)}) collective-permute-start(bf16[128,768]{1,0:T(8,128)(2,1)S(1)} %pad_maximum_fusion.1), channel_id=1, source_target_pairs={{8,0},{9,1},{2,10},{3,11},{16,8},{17,9},{10,18},{11,19},{24,16},{2... | collective-permute-start | bytes 589832 | tf_op jit(solution)/shard_map/ppermute | solution.py:288
  54.6 7.8 %collective-permute-start.19 = (bf16[128,768]{1,0:T(8,128)(2,1)S(1)}, bf16[128,768]{1,0:T(8,128)(2,1)S(1)}, u32[]{:S(2)}, u32[]{:S(2)}) collective-permute-start(bf16[128,768]{1,0:T(8,128)(2,1)S(1)} %add_convert_fusion.2), channel_id=1, source_target_pairs={{0,1},{1,0},{2,3},{3,2},{8,9},{9,8},{10,11},{11,10},{16,17},{17,16... | collective-permute-start | bytes 589832 | tf_op jit(solution)/shard_map/ppermute | solution.py:288
  56.2 8.4 %collective-permute-start.21 = (bf16[128,768]{1,0:T(8,128)(2,1)S(1)}, bf16[128,768]{1,0:T(8,128)(2,1)S(1)}, u32[]{:S(2)}, u32[]{:S(2)}) collective-permute-start(bf16[128,768]{1,0:T(8,128)(2,1)S(1)} %get-tuple-element.40), channel_id=1, source_target_pairs={{0,1},{1,0},{2,3},{3,2},{8,9},{9,8},{10,11},{11,10},{16,17},{17,16... | collective-permute-start | bytes 589832 | tf_op jit(solution)/shard_map/ppermute | solution.py:288
  62.6 5.7 %collective-permute-start.20 = (bf16[128,768]{1,0:T(8,128)(2,1)S(1)}, bf16[128,768]{1,0:T(8,128)(2,1)S(1)}, u32[]{:S(2)}, u32[]{:S(2)}) collective-permute-start(bf16[128,768]{1,0:T(8,128)(2,1)S(1)} %add_convert_fusion.1), channel_id=1, source_target_pairs={{8,0},{9,1},{2,10},{3,11},{16,8},{17,9},{10,18},{11,19},{24,16},{2... | collective-permute-start | bytes 589832 | tf_op jit(solution)/shard_map/ppermute | solution.py:288
  68.4 5.7 %collective-permute-start.22 = (bf16[128,768]{1,0:T(8,128)(2,1)S(1)}, bf16[128,768]{1,0:T(8,128)(2,1)S(1)}, u32[]{:S(2)}, u32[]{:S(2)}) collective-permute-start(bf16[128,768]{1,0:T(8,128)(2,1)S(1)} %add_convert_fusion), channel_id=1, source_target_pairs={{8,0},{9,1},{2,10},{3,11},{16,8},{17,9},{10,18},{11,19},{24,16},{2... | collective-permute-start | bytes 589832 | tf_op jit(solution)/shard_map/ppermute | solution.py:288
  68.6 5.6 %collective-permute-start.14 = (bf16[64,768]{1,0:T(8,128)(2,1)S(1)}, bf16[64,768]{1,0:T(8,128)(2,1)S(1)}, u32[]{:S(2)}, u32[]{:S(2)}) collective-permute-start(bf16[64,768]{1,0:T(8,128)(2,1)S(1)} %get-tuple-element.32), channel_id=1, source_target_pairs={{0,1},{1,0},{2,3},{3,2},{8,9},{9,8},{10,11},{11,10},{16,17},{17,16... | collective-permute-start | bytes 294920 | tf_op jit(solution)/shard_map/ppermute | solution.py:288
  74.1 1.4 %collective-permute-start.23 = (bf16[64,768]{1,0:T(8,128)(2,1)S(1)}, bf16[64,768]{1,0:T(8,128)(2,1)S(1)}, u32[]{:S(2)}, u32[]{:S(2)}) collective-permute-start(bf16[64,768]{1,0:T(8,128)(2,1)S(1)} %slice.22), channel_id=1, source_target_pairs={{0,2},{1,3},{2,0},{3,1},{8,10},{9,11},{10,8},{11,9},{16,18},{17,19... | collective-permute-start | bytes 294920 | tf_op jit(solution)/shard_map/ppermute | solution.py:288

commit v7 on v5

--- a/solution.py
+++ b/solution.py
@@ -11,6 +11,38 @@
 LANES = 128
 SUB = 8
 MIB = 1 << 20
+RETURN = (
+    (2, ((4, 1),)),
+    (0, ((-3, 1),)),
+    (1, ((3, 1),)),
+    (2, ((0, 1),)),
+    (0, ((4, 0),)),
+    (2, ((-2, 1),)),
+    (1, ((2, 1),)),
+    (0, ((-3, 0),)),
+    (1, ((3, 0),)),
+    (2, ((-1, 1),)),
+    (0, ((-2, 0),)),
+    (1, ((2, 0),)),
+    (2, ((1, 1),)),
+    (0, ((-1, 0),)),
+    (1, ((1, 0),)),
+)
+GATHER = (
+    (0, ((-1, 0),)),
+    (1, ((1, 0),)),
+    (2, ((0, 1),)),
+    (0, ((-2, 0),)),
+    (1, ((2, 0),)),
+    (2, ((1, 1), (-1, 1))),
+    (0, ((-3, 0),)),
+    (1, ((3, 0),)),
+    (2, ((2, 1),)),
+    (0, ((4, 0),)),
+    (2, ((3, 1), (-3, 1))),
+    (0, ((-2, 1),)),
+    (2, ((4, 1),)),
+)
 
 
 class Rings:
@@ -35,43 +67,11 @@
 
 
 def gather_sequence():
-    return (
-        (0, (-1, 0)),
-        (1, (1, 0)),
-        (2, (0, 1)),
-        (0, (-2, 0)),
-        (1, (2, 0)),
-        (2, (1, 1)),
-        (0, (-3, 0)),
-        (1, (3, 0)),
-        (2, (-2, 1)),
-        (0, (4, 0)),
-        (1, (2, 1)),
-        (0, (-3, 1)),
-        (2, (-1, 1)),
-        (2, (4, 1)),
-        (2, (3, 1)),
-    )
+    return GATHER
 
 
 def return_sequence():
-    return (
-        (2, (4, 1)),
-        (0, (-3, 1)),
-        (1, (3, 1)),
-        (2, (0, 1)),
-        (0, (4, 0)),
-        (2, (-2, 1)),
-        (1, (2, 1)),
-        (0, (-3, 0)),
-        (1, (3, 0)),
-        (2, (-1, 1)),
-        (0, (-2, 0)),
-        (1, (2, 0)),
-        (2, (1, 1)),
-        (0, (-1, 0)),
-        (1, (1, 0)),
-    )
+    return RETURN
 
 
 def find_rings(mesh):
@@ -178,65 +178,61 @@
     return jnp.where(seats == seat, 1.0, 0.0)
 
 
-def select_kernel(*refs, blocks, count, cap, stride):
+def select_kernel(*refs, count, cap, stride, lent):
     here = lax.axis_index("grp") * stride + lax.axis_index("dev")
     mate = here ^ stride
-    block_refs = refs[:blocks]
-    own_ref, other_ref, seat_ref, gate_ref = refs[-4:]
+    out_ref, seat_ref, gate_ref = refs[-3:]
+    each = count + SUB
+    pieces = [(r, at) for r in refs[:-3] for at in range(0, r.shape[0], each)]
+    blocks = len(pieces)
     pairs = blocks // 2
     dot = functools.partial(jnp.dot, preferred_element_type=jnp.float32)
-    tails = jnp.concatenate([r[count:, :] for r in block_refs], axis=0)
+    tails = jnp.concatenate([r[at + count : at + each, :] for r, at in pieces], axis=0)
     upper = (
         lax.broadcasted_iota(jnp.int32, (LANES, LANES), 0)
         < lax.broadcasted_iota(jnp.int32, (LANES, LANES), 1)
     ).astype(jnp.bfloat16)
-    left = lax.broadcasted_iota(jnp.int32, (2 * pairs, 2 * pairs), 0)
-    right = lax.broadcasted_iota(jnp.int32, (2 * pairs, 2 * pairs), 1)
-    before = ((right < left) & (right // pairs == left // pairs)).astype(jnp.bfloat16)
+    before = (
+        lax.broadcasted_iota(jnp.int32, (pairs, pairs), 1)
+        < lax.broadcasted_iota(jnp.int32, (pairs, pairs), 0)
+    ).astype(jnp.bfloat16)
     lane = lax.broadcasted_iota(jnp.int32, (pairs, LANES), 1)
     row_of = lax.broadcasted_iota(jnp.int32, (pairs, blocks * SUB), 0)
     col_of = lax.broadcasted_iota(jnp.int32, (pairs, blocks * SUB), 1)
     groups = tails.shape[1] // LANES
-    rows = jnp.concatenate([r[:count, :] for r in block_refs], axis=0)
-    picks = []
-    for expert in (here, mate):
-        sub = expert % SUB
-        group = expert // SUB
-        table = tails[:, :LANES]
-        for q in range(1, groups):
-            table = jnp.where(group == q, tails[:, q * LANES : (q + 1) * LANES], table)
-        pick_a = (col_of == (2 * row_of) * SUB + sub).astype(jnp.bfloat16)
-        pick_b = (col_of == (2 * row_of + 1) * SUB + sub).astype(jnp.bfloat16)
-        picks.append(jnp.where(lane < count, dot(pick_a, table), dot(pick_b, table)))
-    gate = jnp.concatenate(picks, axis=0)
+    rows = jnp.concatenate([r[at : at + count, :] for r, at in pieces], axis=0)
+    expert = mate if lent else here
+    sub = expert % SUB
+    group = expert // SUB
+    table = tails[:, :LANES]
+    for q in range(1, groups):
+        table = jnp.where(group == q, tails[:, q * LANES : (q + 1) * LANES], table)
+    pick_a = (col_of == (2 * row_of) * SUB + sub).astype(jnp.bfloat16)
+    pick_b = (col_of == (2 * row_of + 1) * SUB + sub).astype(jnp.bfloat16)
+    gate = jnp.where(lane < count, dot(pick_a, table), dot(pick_b, table))
     chosen = gate > 0.0
     ones = jnp.where(chosen, 1.0, 0.0)
-    total = jnp.broadcast_to(jnp.sum(ones, axis=1, keepdims=True), (2 * pairs, LANES))
+    total = jnp.broadcast_to(jnp.sum(ones, axis=1, keepdims=True), (pairs, LANES))
     spot = dot(ones.astype(jnp.bfloat16), upper) + dot(before, total.astype(jnp.bfloat16))
     spot = spot.astype(jnp.int32)
     seat = jnp.where(here < mate, spot, cap - 1 - spot)
     seat = jnp.where(chosen, seat, -1)
-    for k, out_ref in enumerate((own_ref, other_ref)):
-        mine = seat[k * pairs : (k + 1) * pairs, :]
-        seat_ref[k] = mine
-        gate_ref[k] = gate[k * pairs : (k + 1) * pairs, :]
-        hot = jnp.concatenate([one_hot(mine[o : o + 1, :], cap) for o in range(pairs)], axis=1)
-        out_ref[...] = dot(hot.astype(jnp.bfloat16), rows).astype(jnp.bfloat16)
-
-
-def select(blocks, count, cap, stride):
+    seat_ref[...] = seat
+    gate_ref[...] = gate
+    hot = jnp.concatenate([one_hot(seat[o : o + 1, :], cap) for o in range(pairs)], axis=1)
+    out_ref[...] = dot(hot.astype(jnp.bfloat16), rows).astype(jnp.bfloat16)
+
+
+def select(blocks, count, cap, stride, lent):
     width = blocks[0].shape[1]
-    pairs = len(blocks) // 2
-    taken = jax.ShapeDtypeStruct((cap, width), jnp.bfloat16)
-    vmem = pl.BlockSpec(memory_space=pltpu.VMEM)
+    pairs = sum(b.shape[0] for b in blocks) // (2 * (count + SUB))
     return pl.pallas_call(
-        functools.partial(select_kernel, blocks=len(blocks), count=count, cap=cap, stride=stride),
-        in_specs=[vmem] * len(blocks),
+        functools.partial(select_kernel, count=count, cap=cap, stride=stride, lent=lent),
+        in_specs=[pl.BlockSpec(memory_space=pltpu.VMEM)] * len(blocks),
         out_shape=[
-            taken,
-            taken,
-            jax.ShapeDtypeStruct((2, pairs, LANES), jnp.int32),
-            jax.ShapeDtypeStruct((2, pairs, LANES), jnp.float32),
+            jax.ShapeDtypeStruct((cap, width), jnp.bfloat16),
+            jax.ShapeDtypeStruct((pairs, LANES), jnp.int32),
+            jax.ShapeDtypeStruct((pairs, LANES), jnp.float32),
         ],
         name="select",
         compiler_params=pltpu.CompilerParams(vmem_limit_bytes=16 * MIB),
@@ -293,14 +289,14 @@
     )(own, came, *weights)
 
 
-def spread_kernel(own_ref, came_ref, seat_ref, gate_ref, *out_refs, count, cap):
-    pairs = seat_ref.shape[1]
+def spread_kernel(*refs, cap):
+    out_refs = refs[6:]
     value = None
-    for k, ref in enumerate((own_ref, came_ref)):
+    for ref, seat_ref, gate_ref in (refs[:3], refs[3:6]):
         weights = jnp.concatenate(
             [
-                one_hot(seat_ref[k, o : o + 1, :], cap) * gate_ref[k, o : o + 1, :]
-                for o in range(pairs)
+                one_hot(seat_ref[o : o + 1, :], cap) * gate_ref[o : o + 1, :]
+                for o in range(seat_ref.shape[0])
             ],
             axis=1,
         ).astype(jnp.bfloat16)
@@ -309,20 +305,20 @@
         )
         value = part if value is None else value + part
     value = value.astype(jnp.bfloat16)
-    for o, out_ref in enumerate(out_refs):
-        out_ref[...] = value[o * count : (o + 1) * count, :]
-
-
-def spread(own, came, seat, gate, count):
-    blocks = 2 * seat.shape[1]
-    cap, width = own.shape
-    out = jax.ShapeDtypeStruct((count, width), jnp.bfloat16)
+    at = 0
+    for out_ref in out_refs:
+        out_ref[...] = value[at : at + out_ref.shape[0], :]
+        at += out_ref.shape[0]
+
+
+def spread(own, came, sizes):
+    cap, width = own[0].shape
     return pl.pallas_call(
-        functools.partial(spread_kernel, count=count, cap=cap),
-        out_shape=[out] * blocks,
+        functools.partial(spread_kernel, cap=cap),
+        out_shape=[jax.ShapeDtypeStruct((size, width), jnp.bfloat16) for size in sizes],
         name="spread",
         compiler_params=pltpu.CompilerParams(vmem_limit_bytes=12 * MIB),
-    )(own, came, seat, gate)
+    )(*own, *came)
 
 
 def on_rings(rings, tokens, expert_ids, gates, w_in, w_out):
@@ -334,11 +330,21 @@
     if 2 * count != LANES or length % 4 or experts % SUB or experts * LANES > SUB * width:
         return per_device(tokens, expert_ids, gates, w_in, w_out)
     inverse = (rings.perms[1], rings.perms[0], rings.perms[2])
-    held = {(0, 0): pack(expert_ids, gates, tokens, experts)}
-    for channel, block in gather_sequence():
-        source = held[seen_from_source(channel, block, length)]
-        held[block] = lax.ppermute(source, axes, rings.perms[channel])
-    order = sorted(held, key=lambda b: (b[1], b[0]))
+    own = pack(expert_ids, gates, tokens, experts)
+    each = own.shape[0]
+    held = {(0, 0): (own, 0)}
+    arrays = [[(own, ((0, 0),))], []]
+
+    def one(block):
+        array, at = held[block]
+        return array if array.shape[0] == each else array[at : at + each]
+
+    for channel, blocks in gather_sequence():
+        source = [one(seen_from_source(channel, b, length)) for b in blocks]
+        source = source[0] if len(source) == 1 else jnp.concatenate(source, axis=0)
+        came = lax.ppermute(source, axes, rings.perms[channel])
+        arrays[blocks[0][1]].append((came, blocks))
+        held.update({b: (came, i * each) for i, b in enumerate(blocks)})
     cap = 4 * count
     units = w_in.shape[2]
     weights = []
@@ -349,12 +355,14 @@
         weights.append(load(array, at, shape))
     parts = {}
     for plane in range(2):
-        blocks = order[plane * length : (plane + 1) * length]
-        own, other, seat, gate = select([held[b] for b in blocks], count, cap, n_dev)
+        blocks = [b for _, some in arrays[plane] for b in some]
+        pieces = [array for array, _ in arrays[plane]]
+        other, *their_seats = select(pieces, count, cap, n_dev, True)
         came = lax.ppermute(other, axes, rings.partner)
-        result = expert(own, came, weights)
+        mine, *my_seats = select(pieces, count, cap, n_dev, False)
+        result = expert(mine, came, weights)
         theirs = lax.ppermute(result, axes, rings.partner)
-        sums = spread(result, theirs, seat, gate, count)
+        sums = spread((result, *my_seats), (theirs, *their_seats), [count] * len(blocks))
         for block, value in zip(blocks, sums, strict=True):
             parts[block] = [value]
 
@@ -364,9 +372,13 @@
             value = value + more.astype(jnp.float32)
         return value.astype(jnp.bfloat16)
 
-    for channel, block in return_sequence():
-        value = lax.ppermute(total(block), axes, inverse[channel])
-        parts[seen_from_source(channel, block, length)].append(value)
+    for channel, blocks in return_sequence():
+        source = [total(b) for b in blocks]
+        source = source[0] if len(source) == 1 else jnp.concatenate(source, axis=0)
+        came = lax.ppermute(source, axes, inverse[channel])
+        for i, block in enumerate(blocks):
+            piece = came if len(blocks) == 1 else came[i * count : (i + 1) * count]
+            parts[seen_from_source(channel, block, length)].append(piece)
     return total((0, 0))
 
 

time: 80.1 us -> 82.6 us (1.031)
  waiting for transfers between devices: 31.6 us -> 36.7 us
  starting transfers between devices: 36.8 us -> 33.2 us
  Pallas kernels: 10.4 us -> 11.3 us
    ppermute x30 -> x28, waiting for transfers between devices: 31.6 us -> 36.7 us  [the longest x15 22.2 us: on_rings(): came = lax.ppermute(source, axes, inverse[channel])]
    ppermute x30 -> x28, starting transfers between devices: 36 us -> 32.5 us  [the longest x15 17 us: on_rings(): came = lax.ppermute(source, axes, inverse[channel])]
    pallas_call x4 -> x6, Pallas kernels: 3.11 us -> 4.05 us  [the longest x4 2.82 us: select(): pl.pallas_call(functools.partial(select_kernel, count=count, cap=cap, str...]
  transfers between devices with their start and end apart: 34 -> 32, of which waited for: 12 -> 13; matrix products, arithmetic and copies ran while one was open for 0% -> 0% of each run, Pallas kernels for 12% -> 13%
where the time goes in v7:
time: 82.6 us; the launch traced here: 82.4 us
  waiting for transfers between devices  36.7 us (44%)
  starting transfers between devices  33.2 us (40%)
  Pallas kernels  11.3 us (14%)
  other arithmetic  1 us (1%)
    ppermute x15, waiting for transfers between devices, on_rings(): came = lax.ppermute(source, axes, inverse[channel])  22.2 us
    ppermute x15, starting transfers between devices, on_rings(): came = lax.ppermute(source, axes, inverse[channel])  17 us
    ppermute x13, starting transfers between devices, on_rings(): came = lax.ppermute(source, axes, rings.perms[channel])  15.6 us
    ppermute x13, waiting for transfers between devices, on_rings(): came = lax.ppermute(source, axes, rings.perms[channel])  14.5 us
    pallas_call x2, Pallas kernels, load(): pl.pallas_call(functools.partial(load_kernel, at=at), in_specs=[pl.BlockS...  3.31 us
    pallas_call x2, Pallas kernels, expert(): pl.pallas_call(expert_kernel, in_specs=[vmem] * (2 + len(weights)), out_s...  3.04 us
    pallas_call x4, Pallas kernels, select(): pl.pallas_call(functools.partial(select_kernel, count=count, cap=cap, str...  2.82 us
  transfers between devices with their start and end apart: 32, of which 13 were waited for; matrix products, arithmetic and copies ran while one was open for 0% of the time, Pallas kernels for 13%

profile of v7, /device:TPU:0, one launch (start us, length us, event | category | flops | bytes accessed | tf_op | source)
XLA Modules:
  0.0 82.4 jit_solution(4589057926646048032)
XLA Ops:
  0.9 3.0 %collective-permute-start.1 = (bf16[72,768]{1,0:T(8,128)(2,1)S(1)}, bf16[72,768]{1,0:T(8,128)(2,1)S(1)}, u32[]{:S(2)}, u32[]{:S(2)}) collective-permute-start(bf16[72,768]{1,0:T(8,128)(2,1)S(1)} %pack.1.refs_0_), channel_id=1, source_target_pairs={{8,0},{9,1},{10,2},{11,3},{16,8},{17,9},{18,10},{19,11},{24,16},{2... | collective-permute-start | bytes 331784 | tf_op jit(solution)/shard_map/ppermute | solution.py:345
  4.1 3.0 %collective-permute-done.1.refs_2_ = bf16[72,768]{1,0:T(8,128)(2,1)S(1)} collective-permute-done((bf16[72,768]{1,0:T(8,128)(2,1)S(1)}, bf16[72,768]{1,0:T(8,128)(2,1)S(1)}, u32[]{:S(2)}, u32[]{:S(2)}) %collective-permute-start.1) | collective-permute-done | bytes 110624 | tf_op jit(solution)/shard_map/ppermute | solution.py:345
  7.1 1.7 %collective-permute-start.3 = (bf16[72,768]{1,0:T(8,128)(2,1)S(1)}, bf16[72,768]{1,0:T(8,128)(2,1)S(1)}, u32[]{:S(2)}, u32[]{:S(2)}) collective-permute-start(bf16[72,768]{1,0:T(8,128)(2,1)S(1)} %collective-permute-done.1.refs_2_), channel_id=1, source_target_pairs={{8,0},{9,1},{10,2},{11,3},{16,8},{17,9},{18,10},{19,11},{24,16},{2... | collective-permute-start | bytes 331784 | tf_op jit(solution)/shard_map/ppermute | solution.py:345
  9.1 2.7 %collective-permute-done.3.refs_4_ = bf16[72,768]{1,0:T(8,128)(2,1)S(1)} collective-permute-done((bf16[72,768]{1,0:T(8,128)(2,1)S(1)}, bf16[72,768]{1,0:T(8,128)(2,1)S(1)}, u32[]{:S(2)}, u32[]{:S(2)}) %collective-permute-start.3) | collective-permute-done | bytes 110624 | tf_op jit(solution)/shard_map/ppermute | solution.py:345
  11.8 1.7 %collective-permute-start.5 = (bf16[72,768]{1,0:T(8,128)(2,1)S(1)}, bf16[72,768]{1,0:T(8,128)(2,1)S(1)}, u32[]{:S(2)}, u32[]{:S(2)}) collective-permute-start(bf16[72,768]{1,0:T(8,128)(2,1)S(1)} %collective-permute-done.3.refs_4_), channel_id=1, source_target_pairs={{8,0},{9,1},{10,2},{11,3},{16,8},{17,9},{18,10},{19,11},{24,16},{2... | collective-permute-start | bytes 331784 | tf_op jit(solution)/shard_map/ppermute | solution.py:345
  13.9 1.7 %collective-permute-start.10 = (bf16[144,768]{1,0:T(8,128)(2,1)S(1)}, bf16[144,768]{1,0:T(8,128)(2,1)S(1)}, u32[]{:S(2)}, u32[]{:S(2)}) collective-permute-start(bf16[144,768]{1,0:T(8,128)(2,1)S(1)} %pad_maximum_fusion), channel_id=1, source_target_pairs={{0,1},{1,0},{2,3},{3,2},{8,9},{9,8},{10,11},{11,10},{16,17},{17,16... | collective-permute-start | bytes 663560 | tf_op jit(solution)/shard_map/ppermute | solution.py:345
  15.6 3.3 %collective-permute-done.4.refs_5_ = bf16[72,768]{1,0:T(8,128)(2,1)S(1)} collective-permute-done((bf16[72,768]{1,0:T(8,128)(2,1)S(1)}, bf16[72,768]{1,0:T(8,128)(2,1)S(1)}, u32[]{:S(2)}, u32[]{:S(2)}) %collective-permute-start.4) | collective-permute-done | bytes 110624 | tf_op jit(solution)/shard_map/ppermute | solution.py:345
  19.4 2.0 %collective-permute-start.12 = (bf16[144,768]{1,0:T(8,128)(2,1)S(1)}, bf16[144,768]{1,0:T(8,128)(2,1)S(1)}, u32[]{:S(2)}, u32[]{:S(2)}) collective-permute-start(bf16[144,768]{1,0:T(8,128)(2,1)S(1)} %pad_maximum_fusion.1), channel_id=1, source_target_pairs={{0,1},{1,0},{2,3},{3,2},{8,9},{9,8},{10,11},{11,10},{16,17},{17,16... | collective-permute-start | bytes 663560 | tf_op jit(solution)/shard_map/ppermute | solution.py:345
  21.5 1.9 %collective-permute-start.11 = (bf16[72,768]{1,0:T(8,128)(2,1)S(1)}, bf16[72,768]{1,0:T(8,128)(2,1)S(1)}, u32[]{:S(2)}, u32[]{:S(2)}) collective-permute-start(bf16[72,768]{1,0:T(8,128)(2,1)S(1)} %collective-permute-done.3.refs_4_), channel_id=1, source_target_pairs={{0,1},{1,0},{2,3},{3,2},{8,9},{9,8},{10,11},{11,10},{16,17},{17,16... | collective-permute-start | bytes 331784 | tf_op jit(solution)/shard_map/ppermute | solution.py:345
  23.4 1.7 %collective-permute-start.13 = (bf16[72,768]{1,0:T(8,128)(2,1)S(1)}, bf16[72,768]{1,0:T(8,128)(2,1)S(1)}, u32[]{:S(2)}, u32[]{:S(2)}) collective-permute-start(bf16[72,768]{1,0:T(8,128)(2,1)S(1)} %slice.4), channel_id=1, source_target_pairs={{0,8},{1,9},{2,10},{3,11},{8,16},{9,17},{10,18},{11,19},{16,24},{1... | collective-permute-start | bytes 331784 | tf_op jit(solution)/shard_map/ppermute | solution.py:345
  26.3 3.1 %collective-permute-done.9.refs_0_ = bf16[72,768]{1,0:T(8,128)(2,1)S(1)} collective-permute-done((bf16[72,768]{1,0:T(8,128)(2,1)S(1)}, bf16[72,768]{1,0:T(8,128)(2,1)S(1)}, u32[]{:S(2)}, u32[]{:S(2)}) %collective-permute-start.9) | collective-permute-done | bytes 110624 | tf_op jit(solution)/shard_map/ppermute | solution.py:345
  32.5 1.7 %load.2.in_a = bf16[768,1536]{1,0:T(8,128)(2,1)S(1)} custom-call(bf16[1,768,1536]{2,1,0:T(8,128)(2,1)} %source.2), custom_call_target="tpu_custom_call" | custom-call | tf_op jit(solution)/shard_map/load/pallas_call | solution.py:260
  34.2 1.7 %load.3.out_a = bf16[1536,768]{1,0:T(8,128)(2,1)S(1)} custom-call(bf16[1,1536,768]{2,1,0:T(8,128)(2,1)} %source.3), custom_call_target="tpu_custom_call" | custom-call | tf_op jit(solution)/shard_map/load/pallas_call | solution.py:260
  41.6 1.7 %collective-permute-start.26 = (bf16[64,768]{1,0:T(8,128)(2,1)S(1)}, bf16[64,768]{1,0:T(8,128)(2,1)S(1)}, u32[]{:S(2)}, u32[]{:S(2)}) collective-permute-start(bf16[64,768]{1,0:T(8,128)(2,1)S(1)} %get-tuple-element.57), channel_id=1, source_target_pairs={{0,8},{1,9},{2,10},{3,11},{8,16},{9,17},{10,18},{11,19},{16,24},{1... | collective-permute-start | bytes 294920 | tf_op jit(solution)/shard_map/ppermute | solution.py:378
  45.0 1.8 %collective-permute-done.26 = bf16[64,768]{1,0:T(8,128)(2,1)S(1)} collective-permute-done((bf16[64,768]{1,0:T(8,128)(2,1)S(1)}, bf16[64,768]{1,0:T(8,128)(2,1)S(1)}, u32[]{:S(2)}, u32[]{:S(2)}) %collective-permute-start.26) | collective-permute-done | bytes 98336 | tf_op jit(solution)/shard_map/ppermute | solution.py:378
  46.9 1.7 %collective-permute-start.27 = (bf16[64,768]{1,0:T(8,128)(2,1)S(1)}, bf16[64,768]{1,0:T(8,128)(2,1)S(1)}, u32[]{:S(2)}, u32[]{:S(2)}) collective-permute-start(bf16[64,768]{1,0:T(8,128)(2,1)S(1)} %add_convert_fusion.4), channel_id=1, source_target_pairs={{0,8},{1,9},{2,10},{3,11},{8,16},{9,17},{10,18},{11,19},{16,24},{1... | collective-permute-start | bytes 294920 | tf_op jit(solution)/shard_map/ppermute | solution.py:378
  52.1 1.6 %collective-permute-start.28 = (bf16[64,768]{1,0:T(8,128)(2,1)S(1)}, bf16[64,768]{1,0:T(8,128)(2,1)S(1)}, u32[]{:S(2)}, u32[]{:S(2)}) collective-permute-start(bf16[64,768]{1,0:T(8,128)(2,1)S(1)} %get-tuple-element.60), channel_id=1, source_target_pairs={{0,8},{1,9},{2,10},{3,11},{8,16},{9,17},{10,18},{11,19},{16,24},{1... | collective-permute-start | bytes 294920 | tf_op jit(solution)/shard_map/ppermute | solution.py:378
  53.7 3.3 %collective-permute-done.21 = bf16[64,768]{1,0:T(8,128)(2,1)S(1)} collective-permute-done((bf16[64,768]{1,0:T(8,128)(2,1)S(1)}, bf16[64,768]{1,0:T(8,128)(2,1)S(1)}, u32[]{:S(2)}, u32[]{:S(2)}) %collective-permute-start.21) | collective-permute-done | bytes 98336 | tf_op jit(solution)/shard_map/ppermute | solution.py:378
  59.0 4.1 %collective-permute-done.22 = bf16[64,768]{1,0:T(8,128)(2,1)S(1)} collective-permute-done((bf16[64,768]{1,0:T(8,128)(2,1)S(1)}, bf16[64,768]{1,0:T(8,128)(2,1)S(1)}, u32[]{:S(2)}, u32[]{:S(2)}) %collective-permute-start.22) | collective-permute-done | bytes 98336 | tf_op jit(solution)/shard_map/ppermute | solution.py:378
  64.7 3.0 %collective-permute-done.29 = bf16[64,768]{1,0:T(8,128)(2,1)S(1)} collective-permute-done((bf16[64,768]{1,0:T(8,128)(2,1)S(1)}, bf16[64,768]{1,0:T(8,128)(2,1)S(1)}, u32[]{:S(2)}, u32[]{:S(2)}) %collective-permute-start.29) | collective-permute-done | bytes 98336 | tf_op jit(solution)/shard_map/ppermute | solution.py:378
  69.0 3.3 %collective-permute-done.23 = bf16[64,768]{1,0:T(8,128)(2,1)S(1)} collective-permute-done((bf16[64,768]{1,0:T(8,128)(2,1)S(1)}, bf16[64,768]{1,0:T(8,128)(2,1)S(1)}, u32[]{:S(2)}, u32[]{:S(2)}) %collective-permute-start.23) | collective-permute-done | bytes 98336 | tf_op jit(solution)/shard_map/ppermute | solution.py:378
  72.9 1.6 %collective-permute-start.31 = (bf16[64,768]{1,0:T(8,128)(2,1)S(1)}, bf16[64,768]{1,0:T(8,128)(2,1)S(1)}, u32[]{:S(2)}, u32[]{:S(2)}) collective-permute-start(bf16[64,768]{1,0:T(8,128)(2,1)S(1)} %add_convert_fusion.1), channel_id=1, source_target_pairs={{0,8},{1,9},{2,10},{3,11},{8,16},{9,17},{10,18},{11,19},{16,24},{1... | collective-permute-start | bytes 294920 | tf_op jit(solution)/shard_map/ppermute | solution.py:378
  74.5 2.5 %collective-permute-done.24 = bf16[64,768]{1,0:T(8,128)(2,1)S(1)} collective-permute-done((bf16[64,768]{1,0:T(8,128)(2,1)S(1)}, bf16[64,768]{1,0:T(8,128)(2,1)S(1)}, u32[]{:S(2)}, u32[]{:S(2)}) %collective-permute-start.24) | collective-permute-done | bytes 98336 | tf_op jit(solution)/shard_map/ppermute | solution.py:378
  77.6 4.1 %collective-permute-done.25 = bf16[64,768]{1,0:T(8,128)(2,1)S(1)} collective-permute-done((bf16[64,768]{1,0:T(8,128)(2,1)S(1)}, bf16[64,768]{1,0:T(8,128)(2,1)S(1)}, u32[]{:S(2)}, u32[]{:S(2)}) %collective-permute-start.25) | collective-permute-done | bytes 98336 | tf_op jit(solution)/shard_map/ppermute | solution.py:378
  (64 shorter events, 24.5 us)
Async XLA Ops:
  0.9 6.2 %collective-permute-start.1 = (bf16[72,768]{1,0:T(8,128)(2,1)S(1)}, bf16[72,768]{1,0:T(8,128)(2,1)S(1)}, u32[]{:S(2)}, u32[]{:S(2)}) collective-permute-start(bf16[72,768]{1,0:T(8,128)(2,1)S(1)} %pack.1.refs_0_), channel_id=1, source_target_pairs={{8,0},{9,1},{10,2},{11,3},{16,8},{17,9},{18,10},{19,11},{24,16},{2... | collective-permute-start | bytes 331784 | tf_op jit(solution)/shard_map/ppermute | solution.py:345
  3.9 4.8 %collective-permute-start = (bf16[72,768]{1,0:T(8,128)(2,1)S(1)}, bf16[72,768]{1,0:T(8,128)(2,1)S(1)}, u32[]{:S(2)}, u32[]{:S(2)}) collective-permute-start(bf16[72,768]{1,0:T(8,128)(2,1)S(1)} %pack.1.refs_0_), channel_id=1, source_target_pairs={{0,8},{1,9},{2,10},{3,11},{8,16},{9,17},{10,18},{11,19},{16,24},{1... | collective-permute-start | bytes 331784 | tf_op jit(solution)/shard_map/ppermute | solution.py:345
  7.1 4.7 %collective-permute-start.3 = (bf16[72,768]{1,0:T(8,128)(2,1)S(1)}, bf16[72,768]{1,0:T(8,128)(2,1)S(1)}, u32[]{:S(2)}, u32[]{:S(2)}) collective-permute-start(bf16[72,768]{1,0:T(8,128)(2,1)S(1)} %collective-permute-done.1.refs_2_), channel_id=1, source_target_pairs={{8,0},{9,1},{10,2},{11,3},{16,8},{17,9},{18,10},{19,11},{24,16},{2... | collective-permute-start | bytes 331784 | tf_op jit(solution)/shard_map/ppermute | solution.py:345
  8.7 4.7 %collective-permute-start.2 = (bf16[72,768]{1,0:T(8,128)(2,1)S(1)}, bf16[72,768]{1,0:T(8,128)(2,1)S(1)}, u32[]{:S(2)}, u32[]{:S(2)}) collective-permute-start(bf16[72,768]{1,0:T(8,128)(2,1)S(1)} %collective-permute-done.refs_1_), channel_id=1, source_target_pairs={{0,8},{1,9},{2,10},{3,11},{8,16},{9,17},{10,18},{11,19},{16,24},{1... | collective-permute-start | bytes 331784 | tf_op jit(solution)/shard_map/ppermute | solution.py:345
  11.8 7.5 %collective-permute-start.5 = (bf16[72,768]{1,0:T(8,128)(2,1)S(1)}, bf16[72,768]{1,0:T(8,128)(2,1)S(1)}, u32[]{:S(2)}, u32[]{:S(2)}) collective-permute-start(bf16[72,768]{1,0:T(8,128)(2,1)S(1)} %collective-permute-done.3.refs_4_), channel_id=1, source_target_pairs={{8,0},{9,1},{10,2},{11,3},{16,8},{17,9},{18,10},{19,11},{24,16},{2... | collective-permute-start | bytes 331784 | tf_op jit(solution)/shard_map/ppermute | solution.py:345
  13.5 5.5 %collective-permute-start.4 = (bf16[72,768]{1,0:T(8,128)(2,1)S(1)}, bf16[72,768]{1,0:T(8,128)(2,1)S(1)}, u32[]{:S(2)}, u32[]{:S(2)}) collective-permute-start(bf16[72,768]{1,0:T(8,128)(2,1)S(1)} %collective-permute-done.2.refs_3_), channel_id=1, source_target_pairs={{0,8},{1,9},{2,10},{3,11},{8,16},{9,17},{10,18},{11,19},{16,24},{1... | collective-permute-start | bytes 331784 | tf_op jit(solution)/shard_map/ppermute | solution.py:345
  13.9 9.5 %collective-permute-start.10 = (bf16[144,768]{1,0:T(8,128)(2,1)S(1)}, bf16[144,768]{1,0:T(8,128)(2,1)S(1)}, u32[]{:S(2)}, u32[]{:S(2)}) collective-permute-start(bf16[144,768]{1,0:T(8,128)(2,1)S(1)} %pad_maximum_fusion), channel_id=1, source_target_pairs={{0,1},{1,0},{2,3},{3,2},{8,9},{9,8},{10,11},{11,10},{16,17},{17,16... | collective-permute-start | bytes 663560 | tf_op jit(solution)/shard_map/ppermute | solution.py:345
  19.0 6.1 %collective-permute-start.6 = (bf16[72,768]{1,0:T(8,128)(2,1)S(1)}, bf16[72,768]{1,0:T(8,128)(2,1)S(1)}, u32[]{:S(2)}, u32[]{:S(2)}) collective-permute-start(bf16[72,768]{1,0:T(8,128)(2,1)S(1)} %collective-permute-done.4.refs_5_), channel_id=1, source_target_pairs={{0,8},{1,9},{2,10},{3,11},{8,16},{9,17},{10,18},{11,19},{16,24},{1... | collective-permute-start | bytes 331784 | tf_op jit(solution)/shard_map/ppermute | solution.py:345
  19.4 12.4 %collective-permute-start.12 = (bf16[144,768]{1,0:T(8,128)(2,1)S(1)}, bf16[144,768]{1,0:T(8,128)(2,1)S(1)}, u32[]{:S(2)}, u32[]{:S(2)}) collective-permute-start(bf16[144,768]{1,0:T(8,128)(2,1)S(1)} %pad_maximum_fusion.1), channel_id=1, source_target_pairs={{0,1},{1,0},{2,3},{3,2},{8,9},{9,8},{10,11},{11,10},{16,17},{17,16... | collective-permute-start | bytes 663560 | tf_op jit(solution)/shard_map/ppermute | solution.py:345
  21.4 8.0 %collective-permute-start.9 = (bf16[72,768]{1,0:T(8,128)(2,1)S(1)}, bf16[72,768]{1,0:T(8,128)(2,1)S(1)}, u32[]{:S(2)}, u32[]{:S(2)}) collective-permute-start(bf16[72,768]{1,0:T(8,128)(2,1)S(1)} %pack.1.refs_0_), channel_id=1, source_target_pairs={{0,1},{1,0},{2,3},{3,2},{8,9},{9,8},{10,11},{11,10},{16,17},{17,16... | collective-permute-start | bytes 331784 | tf_op jit(solution)/shard_map/ppermute | solution.py:345
  21.5 9.1 %collective-permute-start.11 = (bf16[72,768]{1,0:T(8,128)(2,1)S(1)}, bf16[72,768]{1,0:T(8,128)(2,1)S(1)}, u32[]{:S(2)}, u32[]{:S(2)}) collective-permute-start(bf16[72,768]{1,0:T(8,128)(2,1)S(1)} %collective-permute-done.3.refs_4_), channel_id=1, source_target_pairs={{0,1},{1,0},{2,3},{3,2},{8,9},{9,8},{10,11},{11,10},{16,17},{17,16... | collective-permute-start | bytes 331784 | tf_op jit(solution)/shard_map/ppermute | solution.py:345
  23.4 7.2 %collective-permute-start.13 = (bf16[72,768]{1,0:T(8,128)(2,1)S(1)}, bf16[72,768]{1,0:T(8,128)(2,1)S(1)}, u32[]{:S(2)}, u32[]{:S(2)}) collective-permute-start(bf16[72,768]{1,0:T(8,128)(2,1)S(1)} %slice.4), channel_id=1, source_target_pairs={{0,8},{1,9},{2,10},{3,11},{8,16},{9,17},{10,18},{11,19},{16,24},{1... | collective-permute-start | bytes 331784 | tf_op jit(solution)/shard_map/ppermute | solution.py:345
  25.1 6.7 %collective-permute-start.14 = (bf16[72,768]{1,0:T(8,128)(2,1)S(1)}, bf16[72,768]{1,0:T(8,128)(2,1)S(1)}, u32[]{:S(2)}, u32[]{:S(2)}) collective-permute-start(bf16[72,768]{1,0:T(8,128)(2,1)S(1)} %collective-permute-done.6.refs_7_), channel_id=1, source_target_pairs={{0,1},{1,0},{2,3},{3,2},{8,9},{9,8},{10,11},{11,10},{16,17},{17,16... | collective-permute-start | bytes 331784 | tf_op jit(solution)/shard_map/ppermute | solution.py:345
  29.4 7.2 %collective-permute-start.7 = (bf16[256,768]{1,0:T(8,128)(2,1)S(1)}, bf16[256,768]{1,0:T(8,128)(2,1)S(1)}, u32[]{:S(2)}, u32[]{:S(2)}) collective-permute-start(bf16[256,768]{1,0:T(8,128)(2,1)S(1)} %get-tuple-element.34), channel_id=1, source_target_pairs={{0,2},{1,3},{2,0},{3,1},{8,10},{9,11},{10,8},{11,9},{16,18},{17,19... | collective-permute-start | bytes 1179656 | tf_op jit(solution)/shard_map/ppermute | solution.py:361
  32.4 6.9 %collective-permute-start.15 = (bf16[256,768]{1,0:T(8,128)(2,1)S(1)}, bf16[256,768]{1,0:T(8,128)(2,1)S(1)}, u32[]{:S(2)}, u32[]{:S(2)}) collective-permute-start(bf16[256,768]{1,0:T(8,128)(2,1)S(1)} %get-tuple-element.41), channel_id=1, source_target_pairs={{0,2},{1,3},{2,0},{3,1},{8,10},{9,11},{10,8},{11,9},{16,18},{17,19... | collective-permute-start | bytes 1179656 | tf_op jit(solution)/shard_map/ppermute | solution.py:361
  41.6 5.2 %collective-permute-start.26 = (bf16[64,768]{1,0:T(8,128)(2,1)S(1)}, bf16[64,768]{1,0:T(8,128)(2,1)S(1)}, u32[]{:S(2)}, u32[]{:S(2)}) collective-permute-start(bf16[64,768]{1,0:T(8,128)(2,1)S(1)} %get-tuple-element.57), channel_id=1, source_target_pairs={{0,8},{1,9},{2,10},{3,11},{8,16},{9,17},{10,18},{11,19},{16,24},{1... | collective-permute-start | bytes 294920 | tf_op jit(solution)/shard_map/ppermute | solution.py:378
  43.9 8.2 %collective-permute-start.19 = (bf16[64,768]{1,0:T(8,128)(2,1)S(1)}, bf16[64,768]{1,0:T(8,128)(2,1)S(1)}, u32[]{:S(2)}, u32[]{:S(2)}) collective-permute-start(bf16[64,768]{1,0:T(8,128)(2,1)S(1)} %get-tuple-element.51), channel_id=1, source_target_pairs={{8,0},{9,1},{10,2},{11,3},{16,8},{17,9},{18,10},{19,11},{24,16},{2... | collective-permute-start | bytes 294920 | tf_op jit(solution)/shard_map/ppermute | solution.py:378
  46.9 26.0 %collective-permute-start.27 = (bf16[64,768]{1,0:T(8,128)(2,1)S(1)}, bf16[64,768]{1,0:T(8,128)(2,1)S(1)}, u32[]{:S(2)}, u32[]{:S(2)}) collective-permute-start(bf16[64,768]{1,0:T(8,128)(2,1)S(1)} %add_convert_fusion.4), channel_id=1, source_target_pairs={{0,8},{1,9},{2,10},{3,11},{8,16},{9,17},{10,18},{11,19},{16,24},{1... | collective-permute-start | bytes 294920 | tf_op jit(solution)/shard_map/ppermute | solution.py:378
  48.6 29.0 %collective-permute-start.17 = (bf16[64,768]{1,0:T(8,128)(2,1)S(1)}, bf16[64,768]{1,0:T(8,128)(2,1)S(1)}, u32[]{:S(2)}, u32[]{:S(2)}) collective-permute-start(bf16[64,768]{1,0:T(8,128)(2,1)S(1)} %get-tuple-element.46), channel_id=1, source_target_pairs={{0,1},{1,0},{2,3},{3,2},{8,9},{9,8},{10,11},{11,10},{16,17},{17,16... | collective-permute-start | bytes 294920 | tf_op jit(solution)/shard_map/ppermute | solution.py:378
  50.1 24.4 %collective-permute-start.18 = (bf16[64,768]{1,0:T(8,128)(2,1)S(1)}, bf16[64,768]{1,0:T(8,128)(2,1)S(1)}, u32[]{:S(2)}, u32[]{:S(2)}) collective-permute-start(bf16[64,768]{1,0:T(8,128)(2,1)S(1)} %get-tuple-element.48), channel_id=1, source_target_pairs={{0,1},{1,0},{2,3},{3,2},{8,9},{9,8},{10,11},{11,10},{16,17},{17,16... | collective-permute-start | bytes 294920 | tf_op jit(solution)/shard_map/ppermute | solution.py:378
  50.6 6.4 %collective-permute-start.21 = (bf16[64,768]{1,0:T(8,128)(2,1)S(1)}, bf16[64,768]{1,0:T(8,128)(2,1)S(1)}, u32[]{:S(2)}, u32[]{:S(2)}) collective-permute-start(bf16[64,768]{1,0:T(8,128)(2,1)S(1)} %get-tuple-element.54), channel_id=1, source_target_pairs={{0,1},{1,0},{2,3},{3,2},{8,9},{9,8},{10,11},{11,10},{16,17},{17,16... | collective-permute-start | bytes 294920 | tf_op jit(solution)/shard_map/ppermute | solution.py:378
  52.1 6.3 %collective-permute-start.28 = (bf16[64,768]{1,0:T(8,128)(2,1)S(1)}, bf16[64,768]{1,0:T(8,128)(2,1)S(1)}, u32[]{:S(2)}, u32[]{:S(2)}) collective-permute-start(bf16[64,768]{1,0:T(8,128)(2,1)S(1)} %get-tuple-element.60), channel_id=1, source_target_pairs={{0,8},{1,9},{2,10},{3,11},{8,16},{9,17},{10,18},{11,19},{16,24},{1... | collective-permute-start | bytes 294920 | tf_op jit(solution)/shard_map/ppermute | solution.py:378
  57.0 11.2 %collective-permute-start.20 = (bf16[64,768]{1,0:T(8,128)(2,1)S(1)}, bf16[64,768]{1,0:T(8,128)(2,1)S(1)}, u32[]{:S(2)}, u32[]{:S(2)}) collective-permute-start(bf16[64,768]{1,0:T(8,128)(2,1)S(1)} %add_convert_fusion.9), channel_id=1, source_target_pairs={{0,1},{1,0},{2,3},{3,2},{8,9},{9,8},{10,11},{11,10},{16,17},{17,16... | collective-permute-start | bytes 294920 | tf_op jit(solution)/shard_map/ppermute | solution.py:378
  68.2 4.7 %collective-permute-start.30 = (bf16[64,768]{1,0:T(8,128)(2,1)S(1)}, bf16[64,768]{1,0:T(8,128)(2,1)S(1)}, u32[]{:S(2)}, u32[]{:S(2)}) collective-permute-start(bf16[64,768]{1,0:T(8,128)(2,1)S(1)} %add_convert_fusion.2), channel_id=1, source_target_pairs={{0,1},{1,0},{2,3},{3,2},{8,9},{9,8},{10,11},{11,10},{16,17},{17,16... | collective-permute-start | bytes 294920 | tf_op jit(solution)/shard_map/ppermute | solution.py:378
  (8 other events, 33.2 us)

commit v8 on v7

--- a/solution.py
+++ b/solution.py
@@ -34,12 +34,12 @@
     (2, ((0, 1),)),
     (0, ((-2, 0),)),
     (1, ((2, 0),)),
-    (2, ((1, 1), (-1, 1))),
+    (2, ((1, 1), (-1, 1),)),
     (0, ((-3, 0),)),
     (1, ((3, 0),)),
     (2, ((2, 1),)),
     (0, ((4, 0),)),
-    (2, ((3, 1), (-3, 1))),
+    (2, ((3, 1), (-3, 1),)),
     (0, ((-2, 1),)),
     (2, ((4, 1),)),
 )
@@ -289,14 +289,14 @@
     )(own, came, *weights)
 
 
-def spread_kernel(*refs, cap):
+def spread_kernel(*refs, cap, some):
     out_refs = refs[6:]
     value = None
     for ref, seat_ref, gate_ref in (refs[:3], refs[3:6]):
         weights = jnp.concatenate(
             [
                 one_hot(seat_ref[o : o + 1, :], cap) * gate_ref[o : o + 1, :]
-                for o in range(seat_ref.shape[0])
+                for o in some
             ],
             axis=1,
         ).astype(jnp.bfloat16)
@@ -311,10 +311,10 @@
         at += out_ref.shape[0]
 
 
-def spread(own, came, sizes):
+def spread(own, came, sizes, some):
     cap, width = own[0].shape
     return pl.pallas_call(
-        functools.partial(spread_kernel, cap=cap),
+        functools.partial(spread_kernel, cap=cap, some=some),
         out_shape=[jax.ShapeDtypeStruct((size, width), jnp.bfloat16) for size in sizes],
         name="spread",
         compiler_params=pltpu.CompilerParams(vmem_limit_bytes=12 * MIB),
@@ -362,7 +362,12 @@
         mine, *my_seats = select(pieces, count, cap, n_dev, False)
         result = expert(mine, came, weights)
         theirs = lax.ppermute(result, axes, rings.partner)
-        sums = spread((result, *my_seats), (theirs, *their_seats), [count] * len(blocks))
+        pairs = len(blocks) // 2
+        cut = pairs // 2 if plane else 0
+        both = ((result, *my_seats), (theirs, *their_seats))
+        sums = spread(*both, [count] * (2 * (pairs - cut)), range(cut, pairs))
+        if cut:
+            sums = spread(*both, [count] * (2 * cut), range(cut)) + sums
         for block, value in zip(blocks, sums, strict=True):
             parts[block] = [value]
 

time: 82.6 us -> 79.7 us (0.965)
  waiting for transfers between devices: 36.7 us -> 33 us
    ppermute x15, waiting for transfers between devices: 22.2 us -> 18.5 us  [on_rings(): came = lax.ppermute(source, axes, inverse[channel])]
  transfers between devices with their start and end apart: 32 -> 32, of which waited for: 13 -> 12; matrix products, arithmetic and copies ran while one was open for 0% -> 0% of each run, Pallas kernels for 13% -> 13%
where the time goes in v8:
time: 79.7 us; the launch traced here: 79.5 us
  starting transfers between devices  33.7 us (42%)
  waiting for transfers between devices  33 us (41%)
  Pallas kernels  11.5 us (14%)
  other arithmetic  1 us (1%)
    ppermute x15, waiting for transfers between devices, on_rings(): came = lax.ppermute(source, axes, inverse[channel])  18.5 us
    ppermute x15, starting transfers between devices, on_rings(): came = lax.ppermute(source, axes, inverse[channel])  17.5 us
    ppermute x13, starting transfers between devices, on_rings(): came = lax.ppermute(source, axes, rings.perms[channel])  15.6 us
    ppermute x13, waiting for transfers between devices, on_rings(): came = lax.ppermute(source, axes, rings.perms[channel])  14.5 us
    pallas_call x2, Pallas kernels, load(): pl.pallas_call(functools.partial(load_kernel, at=at), in_specs=[pl.BlockS...  3.31 us
    pallas_call x2, Pallas kernels, expert(): pl.pallas_call(expert_kernel, in_specs=[vmem] * (2 + len(weights)), out_s...  3.04 us
    pallas_call x4, Pallas kernels, select(): pl.pallas_call(functools.partial(select_kernel, count=count, cap=cap, str...  2.82 us
  transfers between devices with their start and end apart: 32, of which 12 were waited for; matrix products, arithmetic and copies ran while one was open for 0% of the time, Pallas kernels for 13%

profile of v8, /device:TPU:0, one launch (start us, length us, event | category | flops | bytes accessed | tf_op | source)
XLA Modules:
  0.0 79.5 jit_solution(7698141853180364611)
XLA Ops:
  0.9 3.0 %collective-permute-start.1 = (bf16[72,768]{1,0:T(8,128)(2,1)S(1)}, bf16[72,768]{1,0:T(8,128)(2,1)S(1)}, u32[]{:S(2)}, u32[]{:S(2)}) collective-permute-start(bf16[72,768]{1,0:T(8,128)(2,1)S(1)} %pack.1.refs_0_), channel_id=1, source_target_pairs={{8,0},{9,1},{10,2},{11,3},{16,8},{17,9},{18,10},{19,11},{24,16},{2... | collective-permute-start | bytes 331784 | tf_op jit(solution)/shard_map/ppermute | solution.py:345
  4.1 3.0 %collective-permute-done.1.refs_2_ = bf16[72,768]{1,0:T(8,128)(2,1)S(1)} collective-permute-done((bf16[72,768]{1,0:T(8,128)(2,1)S(1)}, bf16[72,768]{1,0:T(8,128)(2,1)S(1)}, u32[]{:S(2)}, u32[]{:S(2)}) %collective-permute-start.1) | collective-permute-done | bytes 110624 | tf_op jit(solution)/shard_map/ppermute | solution.py:345
  7.1 1.7 %collective-permute-start.3 = (bf16[72,768]{1,0:T(8,128)(2,1)S(1)}, bf16[72,768]{1,0:T(8,128)(2,1)S(1)}, u32[]{:S(2)}, u32[]{:S(2)}) collective-permute-start(bf16[72,768]{1,0:T(8,128)(2,1)S(1)} %collective-permute-done.1.refs_2_), channel_id=1, source_target_pairs={{8,0},{9,1},{10,2},{11,3},{16,8},{17,9},{18,10},{19,11},{24,16},{2... | collective-permute-start | bytes 331784 | tf_op jit(solution)/shard_map/ppermute | solution.py:345
  9.1 2.7 %collective-permute-done.3.refs_4_ = bf16[72,768]{1,0:T(8,128)(2,1)S(1)} collective-permute-done((bf16[72,768]{1,0:T(8,128)(2,1)S(1)}, bf16[72,768]{1,0:T(8,128)(2,1)S(1)}, u32[]{:S(2)}, u32[]{:S(2)}) %collective-permute-start.3) | collective-permute-done | bytes 110624 | tf_op jit(solution)/shard_map/ppermute | solution.py:345
  11.8 1.7 %collective-permute-start.5 = (bf16[72,768]{1,0:T(8,128)(2,1)S(1)}, bf16[72,768]{1,0:T(8,128)(2,1)S(1)}, u32[]{:S(2)}, u32[]{:S(2)}) collective-permute-start(bf16[72,768]{1,0:T(8,128)(2,1)S(1)} %collective-permute-done.3.refs_4_), channel_id=1, source_target_pairs={{8,0},{9,1},{10,2},{11,3},{16,8},{17,9},{18,10},{19,11},{24,16},{2... | collective-permute-start | bytes 331784 | tf_op jit(solution)/shard_map/ppermute | solution.py:345
  13.9 1.7 %collective-permute-start.10 = (bf16[144,768]{1,0:T(8,128)(2,1)S(1)}, bf16[144,768]{1,0:T(8,128)(2,1)S(1)}, u32[]{:S(2)}, u32[]{:S(2)}) collective-permute-start(bf16[144,768]{1,0:T(8,128)(2,1)S(1)} %pad_maximum_fusion), channel_id=1, source_target_pairs={{0,1},{1,0},{2,3},{3,2},{8,9},{9,8},{10,11},{11,10},{16,17},{17,16... | collective-permute-start | bytes 663560 | tf_op jit(solution)/shard_map/ppermute | solution.py:345
  15.6 3.3 %collective-permute-done.4.refs_5_ = bf16[72,768]{1,0:T(8,128)(2,1)S(1)} collective-permute-done((bf16[72,768]{1,0:T(8,128)(2,1)S(1)}, bf16[72,768]{1,0:T(8,128)(2,1)S(1)}, u32[]{:S(2)}, u32[]{:S(2)}) %collective-permute-start.4) | collective-permute-done | bytes 110624 | tf_op jit(solution)/shard_map/ppermute | solution.py:345
  19.4 2.0 %collective-permute-start.12 = (bf16[144,768]{1,0:T(8,128)(2,1)S(1)}, bf16[144,768]{1,0:T(8,128)(2,1)S(1)}, u32[]{:S(2)}, u32[]{:S(2)}) collective-permute-start(bf16[144,768]{1,0:T(8,128)(2,1)S(1)} %pad_maximum_fusion.1), channel_id=1, source_target_pairs={{0,1},{1,0},{2,3},{3,2},{8,9},{9,8},{10,11},{11,10},{16,17},{17,16... | collective-permute-start | bytes 663560 | tf_op jit(solution)/shard_map/ppermute | solution.py:345
  21.5 1.9 %collective-permute-start.11 = (bf16[72,768]{1,0:T(8,128)(2,1)S(1)}, bf16[72,768]{1,0:T(8,128)(2,1)S(1)}, u32[]{:S(2)}, u32[]{:S(2)}) collective-permute-start(bf16[72,768]{1,0:T(8,128)(2,1)S(1)} %collective-permute-done.3.refs_4_), channel_id=1, source_target_pairs={{0,1},{1,0},{2,3},{3,2},{8,9},{9,8},{10,11},{11,10},{16,17},{17,16... | collective-permute-start | bytes 331784 | tf_op jit(solution)/shard_map/ppermute | solution.py:345
  23.4 1.7 %collective-permute-start.13 = (bf16[72,768]{1,0:T(8,128)(2,1)S(1)}, bf16[72,768]{1,0:T(8,128)(2,1)S(1)}, u32[]{:S(2)}, u32[]{:S(2)}) collective-permute-start(bf16[72,768]{1,0:T(8,128)(2,1)S(1)} %slice.4), channel_id=1, source_target_pairs={{0,8},{1,9},{2,10},{3,11},{8,16},{9,17},{10,18},{11,19},{16,24},{1... | collective-permute-start | bytes 331784 | tf_op jit(solution)/shard_map/ppermute | solution.py:345
  26.3 3.1 %collective-permute-done.9.refs_0_ = bf16[72,768]{1,0:T(8,128)(2,1)S(1)} collective-permute-done((bf16[72,768]{1,0:T(8,128)(2,1)S(1)}, bf16[72,768]{1,0:T(8,128)(2,1)S(1)}, u32[]{:S(2)}, u32[]{:S(2)}) %collective-permute-start.9) | collective-permute-done | bytes 110624 | tf_op jit(solution)/shard_map/ppermute | solution.py:345
  32.5 1.7 %load.2.in_a = bf16[768,1536]{1,0:T(8,128)(2,1)S(1)} custom-call(bf16[1,768,1536]{2,1,0:T(8,128)(2,1)} %source.2), custom_call_target="tpu_custom_call" | custom-call | tf_op jit(solution)/shard_map/load/pallas_call | solution.py:260
  34.2 1.7 %load.3.out_a = bf16[1536,768]{1,0:T(8,128)(2,1)S(1)} custom-call(bf16[1,1536,768]{2,1,0:T(8,128)(2,1)} %source.3), custom_call_target="tpu_custom_call" | custom-call | tf_op jit(solution)/shard_map/load/pallas_call | solution.py:260
  36.6 1.5 %expert.2.refs_0_ = bf16[256,768]{1,0:T(8,128)(2,1)S(1)} custom-call(bf16[256,768]{1,0:T(8,128)(2,1)S(1)} %get-tuple-element.33.own_ref, bf16[256,768]{1,0:T(8,128)(2,1)S(1)} %collective-permute-done.7.came_ref, bf16[768,1536]{1,0:T(8,128)(2,1)S(1)} %load.2.in_a, bf16[1536,768]{1,0:T(8,128)(2,1)S(1)} %load.3.out_a), custom_call_target="tpu_custom_call" | custom-call | tf_op jit(solution)/shard_map/expert/pallas_call | solution.py:283
  41.6 1.7 %collective-permute-start.26 = (bf16[64,768]{1,0:T(8,128)(2,1)S(1)}, bf16[64,768]{1,0:T(8,128)(2,1)S(1)}, u32[]{:S(2)}, u32[]{:S(2)}) collective-permute-start(bf16[64,768]{1,0:T(8,128)(2,1)S(1)} %get-tuple-element.57), channel_id=1, source_target_pairs={{0,8},{1,9},{2,10},{3,11},{8,16},{9,17},{10,18},{11,19},{16,24},{1... | collective-permute-start | bytes 294920 | tf_op jit(solution)/shard_map/ppermute | solution.py:383
  44.8 2.1 %collective-permute-done.26 = bf16[64,768]{1,0:T(8,128)(2,1)S(1)} collective-permute-done((bf16[64,768]{1,0:T(8,128)(2,1)S(1)}, bf16[64,768]{1,0:T(8,128)(2,1)S(1)}, u32[]{:S(2)}, u32[]{:S(2)}) %collective-permute-start.26) | collective-permute-done | bytes 98336 | tf_op jit(solution)/shard_map/ppermute | solution.py:383
  46.9 1.7 %collective-permute-start.27 = (bf16[64,768]{1,0:T(8,128)(2,1)S(1)}, bf16[64,768]{1,0:T(8,128)(2,1)S(1)}, u32[]{:S(2)}, u32[]{:S(2)}) collective-permute-start(bf16[64,768]{1,0:T(8,128)(2,1)S(1)} %add_convert_fusion.4), channel_id=1, source_target_pairs={{0,8},{1,9},{2,10},{3,11},{8,16},{9,17},{10,18},{11,19},{16,24},{1... | collective-permute-start | bytes 294920 | tf_op jit(solution)/shard_map/ppermute | solution.py:383
  50.1 1.6 %collective-permute-start.28 = (bf16[64,768]{1,0:T(8,128)(2,1)S(1)}, bf16[64,768]{1,0:T(8,128)(2,1)S(1)}, u32[]{:S(2)}, u32[]{:S(2)}) collective-permute-start(bf16[64,768]{1,0:T(8,128)(2,1)S(1)} %get-tuple-element.60), channel_id=1, source_target_pairs={{0,8},{1,9},{2,10},{3,11},{8,16},{9,17},{10,18},{11,19},{16,24},{1... | collective-permute-start | bytes 294920 | tf_op jit(solution)/shard_map/ppermute | solution.py:383
  56.0 4.1 %collective-permute-done.22 = bf16[64,768]{1,0:T(8,128)(2,1)S(1)} collective-permute-done((bf16[64,768]{1,0:T(8,128)(2,1)S(1)}, bf16[64,768]{1,0:T(8,128)(2,1)S(1)}, u32[]{:S(2)}, u32[]{:S(2)}) %collective-permute-start.22) | collective-permute-done | bytes 98336 | tf_op jit(solution)/shard_map/ppermute | solution.py:383
  60.1 1.6 %collective-permute-start.29 = (bf16[64,768]{1,0:T(8,128)(2,1)S(1)}, bf16[64,768]{1,0:T(8,128)(2,1)S(1)}, u32[]{:S(2)}, u32[]{:S(2)}) collective-permute-start(bf16[64,768]{1,0:T(8,128)(2,1)S(1)} %add_convert_fusion.3), channel_id=1, source_target_pairs={{0,8},{1,9},{2,10},{3,11},{8,16},{9,17},{10,18},{11,19},{16,24},{1... | collective-permute-start | bytes 294920 | tf_op jit(solution)/shard_map/ppermute | solution.py:383
  61.7 3.0 %collective-permute-done.29 = bf16[64,768]{1,0:T(8,128)(2,1)S(1)} collective-permute-done((bf16[64,768]{1,0:T(8,128)(2,1)S(1)}, bf16[64,768]{1,0:T(8,128)(2,1)S(1)}, u32[]{:S(2)}, u32[]{:S(2)}) %collective-permute-start.29) | collective-permute-done | bytes 98336 | tf_op jit(solution)/shard_map/ppermute | solution.py:383
  66.2 3.1 %collective-permute-done.23 = bf16[64,768]{1,0:T(8,128)(2,1)S(1)} collective-permute-done((bf16[64,768]{1,0:T(8,128)(2,1)S(1)}, bf16[64,768]{1,0:T(8,128)(2,1)S(1)}, u32[]{:S(2)}, u32[]{:S(2)}) %collective-permute-start.23) | collective-permute-done | bytes 98336 | tf_op jit(solution)/shard_map/ppermute | solution.py:383
  71.6 2.5 %collective-permute-done.24 = bf16[64,768]{1,0:T(8,128)(2,1)S(1)} collective-permute-done((bf16[64,768]{1,0:T(8,128)(2,1)S(1)}, bf16[64,768]{1,0:T(8,128)(2,1)S(1)}, u32[]{:S(2)}, u32[]{:S(2)}) %collective-permute-start.24) | collective-permute-done | bytes 98336 | tf_op jit(solution)/shard_map/ppermute | solution.py:383
  75.0 3.8 %collective-permute-done.25 = bf16[64,768]{1,0:T(8,128)(2,1)S(1)} collective-permute-done((bf16[64,768]{1,0:T(8,128)(2,1)S(1)}, bf16[64,768]{1,0:T(8,128)(2,1)S(1)}, u32[]{:S(2)}, u32[]{:S(2)}) %collective-permute-start.25) | collective-permute-done | bytes 98336 | tf_op jit(solution)/shard_map/ppermute | solution.py:383
  (65 shorter events, 23.6 us)
Async XLA Ops:
  0.9 6.2 %collective-permute-start.1 = (bf16[72,768]{1,0:T(8,128)(2,1)S(1)}, bf16[72,768]{1,0:T(8,128)(2,1)S(1)}, u32[]{:S(2)}, u32[]{:S(2)}) collective-permute-start(bf16[72,768]{1,0:T(8,128)(2,1)S(1)} %pack.1.refs_0_), channel_id=1, source_target_pairs={{8,0},{9,1},{10,2},{11,3},{16,8},{17,9},{18,10},{19,11},{24,16},{2... | collective-permute-start | bytes 331784 | tf_op jit(solution)/shard_map/ppermute | solution.py:345
  3.9 4.8 %collective-permute-start = (bf16[72,768]{1,0:T(8,128)(2,1)S(1)}, bf16[72,768]{1,0:T(8,128)(2,1)S(1)}, u32[]{:S(2)}, u32[]{:S(2)}) collective-permute-start(bf16[72,768]{1,0:T(8,128)(2,1)S(1)} %pack.1.refs_0_), channel_id=1, source_target_pairs={{0,8},{1,9},{2,10},{3,11},{8,16},{9,17},{10,18},{11,19},{16,24},{1... | collective-permute-start | bytes 331784 | tf_op jit(solution)/shard_map/ppermute | solution.py:345
  7.1 4.7 %collective-permute-start.3 = (bf16[72,768]{1,0:T(8,128)(2,1)S(1)}, bf16[72,768]{1,0:T(8,128)(2,1)S(1)}, u32[]{:S(2)}, u32[]{:S(2)}) collective-permute-start(bf16[72,768]{1,0:T(8,128)(2,1)S(1)} %collective-permute-done.1.refs_2_), channel_id=1, source_target_pairs={{8,0},{9,1},{10,2},{11,3},{16,8},{17,9},{18,10},{19,11},{24,16},{2... | collective-permute-start | bytes 331784 | tf_op jit(solution)/shard_map/ppermute | solution.py:345
  8.7 4.7 %collective-permute-start.2 = (bf16[72,768]{1,0:T(8,128)(2,1)S(1)}, bf16[72,768]{1,0:T(8,128)(2,1)S(1)}, u32[]{:S(2)}, u32[]{:S(2)}) collective-permute-start(bf16[72,768]{1,0:T(8,128)(2,1)S(1)} %collective-permute-done.refs_1_), channel_id=1, source_target_pairs={{0,8},{1,9},{2,10},{3,11},{8,16},{9,17},{10,18},{11,19},{16,24},{1... | collective-permute-start | bytes 331784 | tf_op jit(solution)/shard_map/ppermute | solution.py:345
  11.8 7.5 %collective-permute-start.5 = (bf16[72,768]{1,0:T(8,128)(2,1)S(1)}, bf16[72,768]{1,0:T(8,128)(2,1)S(1)}, u32[]{:S(2)}, u32[]{:S(2)}) collective-permute-start(bf16[72,768]{1,0:T(8,128)(2,1)S(1)} %collective-permute-done.3.refs_4_), channel_id=1, source_target_pairs={{8,0},{9,1},{10,2},{11,3},{16,8},{17,9},{18,10},{19,11},{24,16},{2... | collective-permute-start | bytes 331784 | tf_op jit(solution)/shard_map/ppermute | solution.py:345
  13.5 5.5 %collective-permute-start.4 = (bf16[72,768]{1,0:T(8,128)(2,1)S(1)}, bf16[72,768]{1,0:T(8,128)(2,1)S(1)}, u32[]{:S(2)}, u32[]{:S(2)}) collective-permute-start(bf16[72,768]{1,0:T(8,128)(2,1)S(1)} %collective-permute-done.2.refs_3_), channel_id=1, source_target_pairs={{0,8},{1,9},{2,10},{3,11},{8,16},{9,17},{10,18},{11,19},{16,24},{1... | collective-permute-start | bytes 331784 | tf_op jit(solution)/shard_map/ppermute | solution.py:345
  13.9 9.5 %collective-permute-start.10 = (bf16[144,768]{1,0:T(8,128)(2,1)S(1)}, bf16[144,768]{1,0:T(8,128)(2,1)S(1)}, u32[]{:S(2)}, u32[]{:S(2)}) collective-permute-start(bf16[144,768]{1,0:T(8,128)(2,1)S(1)} %pad_maximum_fusion), channel_id=1, source_target_pairs={{0,1},{1,0},{2,3},{3,2},{8,9},{9,8},{10,11},{11,10},{16,17},{17,16... | collective-permute-start | bytes 663560 | tf_op jit(solution)/shard_map/ppermute | solution.py:345
  19.0 6.1 %collective-permute-start.6 = (bf16[72,768]{1,0:T(8,128)(2,1)S(1)}, bf16[72,768]{1,0:T(8,128)(2,1)S(1)}, u32[]{:S(2)}, u32[]{:S(2)}) collective-permute-start(bf16[72,768]{1,0:T(8,128)(2,1)S(1)} %collective-permute-done.4.refs_5_), channel_id=1, source_target_pairs={{0,8},{1,9},{2,10},{3,11},{8,16},{9,17},{10,18},{11,19},{16,24},{1... | collective-permute-start | bytes 331784 | tf_op jit(solution)/shard_map/ppermute | solution.py:345
  19.4 12.4 %collective-permute-start.12 = (bf16[144,768]{1,0:T(8,128)(2,1)S(1)}, bf16[144,768]{1,0:T(8,128)(2,1)S(1)}, u32[]{:S(2)}, u32[]{:S(2)}) collective-permute-start(bf16[144,768]{1,0:T(8,128)(2,1)S(1)} %pad_maximum_fusion.1), channel_id=1, source_target_pairs={{0,1},{1,0},{2,3},{3,2},{8,9},{9,8},{10,11},{11,10},{16,17},{17,16... | collective-permute-start | bytes 663560 | tf_op jit(solution)/shard_map/ppermute | solution.py:345
  21.4 8.0 %collective-permute-start.9 = (bf16[72,768]{1,0:T(8,128)(2,1)S(1)}, bf16[72,768]{1,0:T(8,128)(2,1)S(1)}, u32[]{:S(2)}, u32[]{:S(2)}) collective-permute-start(bf16[72,768]{1,0:T(8,128)(2,1)S(1)} %pack.1.refs_0_), channel_id=1, source_target_pairs={{0,1},{1,0},{2,3},{3,2},{8,9},{9,8},{10,11},{11,10},{16,17},{17,16... | collective-permute-start | bytes 331784 | tf_op jit(solution)/shard_map/ppermute | solution.py:345
  21.5 9.1 %collective-permute-start.11 = (bf16[72,768]{1,0:T(8,128)(2,1)S(1)}, bf16[72,768]{1,0:T(8,128)(2,1)S(1)}, u32[]{:S(2)}, u32[]{:S(2)}) collective-permute-start(bf16[72,768]{1,0:T(8,128)(2,1)S(1)} %collective-permute-done.3.refs_4_), channel_id=1, source_target_pairs={{0,1},{1,0},{2,3},{3,2},{8,9},{9,8},{10,11},{11,10},{16,17},{17,16... | collective-permute-start | bytes 331784 | tf_op jit(solution)/shard_map/ppermute | solution.py:345
  23.4 7.2 %collective-permute-start.13 = (bf16[72,768]{1,0:T(8,128)(2,1)S(1)}, bf16[72,768]{1,0:T(8,128)(2,1)S(1)}, u32[]{:S(2)}, u32[]{:S(2)}) collective-permute-start(bf16[72,768]{1,0:T(8,128)(2,1)S(1)} %slice.4), channel_id=1, source_target_pairs={{0,8},{1,9},{2,10},{3,11},{8,16},{9,17},{10,18},{11,19},{16,24},{1... | collective-permute-start | bytes 331784 | tf_op jit(solution)/shard_map/ppermute | solution.py:345
  25.1 6.7 %collective-permute-start.14 = (bf16[72,768]{1,0:T(8,128)(2,1)S(1)}, bf16[72,768]{1,0:T(8,128)(2,1)S(1)}, u32[]{:S(2)}, u32[]{:S(2)}) collective-permute-start(bf16[72,768]{1,0:T(8,128)(2,1)S(1)} %collective-permute-done.6.refs_7_), channel_id=1, source_target_pairs={{0,1},{1,0},{2,3},{3,2},{8,9},{9,8},{10,11},{11,10},{16,17},{17,16... | collective-permute-start | bytes 331784 | tf_op jit(solution)/shard_map/ppermute | solution.py:345
  29.4 7.2 %collective-permute-start.7 = (bf16[256,768]{1,0:T(8,128)(2,1)S(1)}, bf16[256,768]{1,0:T(8,128)(2,1)S(1)}, u32[]{:S(2)}, u32[]{:S(2)}) collective-permute-start(bf16[256,768]{1,0:T(8,128)(2,1)S(1)} %get-tuple-element.34), channel_id=1, source_target_pairs={{0,2},{1,3},{2,0},{3,1},{8,10},{9,11},{10,8},{11,9},{16,18},{17,19... | collective-permute-start | bytes 1179656 | tf_op jit(solution)/shard_map/ppermute | solution.py:361
  32.4 6.9 %collective-permute-start.15 = (bf16[256,768]{1,0:T(8,128)(2,1)S(1)}, bf16[256,768]{1,0:T(8,128)(2,1)S(1)}, u32[]{:S(2)}, u32[]{:S(2)}) collective-permute-start(bf16[256,768]{1,0:T(8,128)(2,1)S(1)} %get-tuple-element.41), channel_id=1, source_target_pairs={{0,2},{1,3},{2,0},{3,1},{8,10},{9,11},{10,8},{11,9},{16,18},{17,19... | collective-permute-start | bytes 1179656 | tf_op jit(solution)/shard_map/ppermute | solution.py:361
  41.6 5.2 %collective-permute-start.26 = (bf16[64,768]{1,0:T(8,128)(2,1)S(1)}, bf16[64,768]{1,0:T(8,128)(2,1)S(1)}, u32[]{:S(2)}, u32[]{:S(2)}) collective-permute-start(bf16[64,768]{1,0:T(8,128)(2,1)S(1)} %get-tuple-element.57), channel_id=1, source_target_pairs={{0,8},{1,9},{2,10},{3,11},{8,16},{9,17},{10,18},{11,19},{16,24},{1... | collective-permute-start | bytes 294920 | tf_op jit(solution)/shard_map/ppermute | solution.py:383
  43.7 8.9 %collective-permute-start.19 = (bf16[64,768]{1,0:T(8,128)(2,1)S(1)}, bf16[64,768]{1,0:T(8,128)(2,1)S(1)}, u32[]{:S(2)}, u32[]{:S(2)}) collective-permute-start(bf16[64,768]{1,0:T(8,128)(2,1)S(1)} %get-tuple-element.51), channel_id=1, source_target_pairs={{8,0},{9,1},{10,2},{11,3},{16,8},{17,9},{18,10},{19,11},{24,16},{2... | collective-permute-start | bytes 294920 | tf_op jit(solution)/shard_map/ppermute | solution.py:383
  46.9 23.4 %collective-permute-start.27 = (bf16[64,768]{1,0:T(8,128)(2,1)S(1)}, bf16[64,768]{1,0:T(8,128)(2,1)S(1)}, u32[]{:S(2)}, u32[]{:S(2)}) collective-permute-start(bf16[64,768]{1,0:T(8,128)(2,1)S(1)} %add_convert_fusion.4), channel_id=1, source_target_pairs={{0,8},{1,9},{2,10},{3,11},{8,16},{9,17},{10,18},{11,19},{16,24},{1... | collective-permute-start | bytes 294920 | tf_op jit(solution)/shard_map/ppermute | solution.py:383
  48.6 5.6 %collective-permute-start.21 = (bf16[64,768]{1,0:T(8,128)(2,1)S(1)}, bf16[64,768]{1,0:T(8,128)(2,1)S(1)}, u32[]{:S(2)}, u32[]{:S(2)}) collective-permute-start(bf16[64,768]{1,0:T(8,128)(2,1)S(1)} %get-tuple-element.54), channel_id=1, source_target_pairs={{0,1},{1,0},{2,3},{3,2},{8,9},{9,8},{10,11},{11,10},{16,17},{17,16... | collective-permute-start | bytes 294920 | tf_op jit(solution)/shard_map/ppermute | solution.py:383
  50.1 5.3 %collective-permute-start.28 = (bf16[64,768]{1,0:T(8,128)(2,1)S(1)}, bf16[64,768]{1,0:T(8,128)(2,1)S(1)}, u32[]{:S(2)}, u32[]{:S(2)}) collective-permute-start(bf16[64,768]{1,0:T(8,128)(2,1)S(1)} %get-tuple-element.60), channel_id=1, source_target_pairs={{0,8},{1,9},{2,10},{3,11},{8,16},{9,17},{10,18},{11,19},{16,24},{1... | collective-permute-start | bytes 294920 | tf_op jit(solution)/shard_map/ppermute | solution.py:383
  52.1 22.9 %collective-permute-start.17 = (bf16[64,768]{1,0:T(8,128)(2,1)S(1)}, bf16[64,768]{1,0:T(8,128)(2,1)S(1)}, u32[]{:S(2)}, u32[]{:S(2)}) collective-permute-start(bf16[64,768]{1,0:T(8,128)(2,1)S(1)} %get-tuple-element.46), channel_id=1, source_target_pairs={{0,1},{1,0},{2,3},{3,2},{8,9},{9,8},{10,11},{11,10},{16,17},{17,16... | collective-permute-start | bytes 294920 | tf_op jit(solution)/shard_map/ppermute | solution.py:383
  52.7 18.9 %collective-permute-start.18 = (bf16[64,768]{1,0:T(8,128)(2,1)S(1)}, bf16[64,768]{1,0:T(8,128)(2,1)S(1)}, u32[]{:S(2)}, u32[]{:S(2)}) collective-permute-start(bf16[64,768]{1,0:T(8,128)(2,1)S(1)} %get-tuple-element.48), channel_id=1, source_target_pairs={{0,1},{1,0},{2,3},{3,2},{8,9},{9,8},{10,11},{11,10},{16,17},{17,16... | collective-permute-start | bytes 294920 | tf_op jit(solution)/shard_map/ppermute | solution.py:383
  54.2 11.1 %collective-permute-start.20 = (bf16[64,768]{1,0:T(8,128)(2,1)S(1)}, bf16[64,768]{1,0:T(8,128)(2,1)S(1)}, u32[]{:S(2)}, u32[]{:S(2)}) collective-permute-start(bf16[64,768]{1,0:T(8,128)(2,1)S(1)} %add_convert_fusion.9), channel_id=1, source_target_pairs={{0,1},{1,0},{2,3},{3,2},{8,9},{9,8},{10,11},{11,10},{16,17},{17,16... | collective-permute-start | bytes 294920 | tf_op jit(solution)/shard_map/ppermute | solution.py:383
  65.3 5.0 %collective-permute-start.30 = (bf16[64,768]{1,0:T(8,128)(2,1)S(1)}, bf16[64,768]{1,0:T(8,128)(2,1)S(1)}, u32[]{:S(2)}, u32[]{:S(2)}) collective-permute-start(bf16[64,768]{1,0:T(8,128)(2,1)S(1)} %add_convert_fusion.2), channel_id=1, source_target_pairs={{0,1},{1,0},{2,3},{3,2},{8,9},{9,8},{10,11},{11,10},{16,17},{17,16... | collective-permute-start | bytes 294920 | tf_op jit(solution)/shard_map/ppermute | solution.py:383
  (8 other events, 33.2 us)
